TPU v7x, 32 devices: a whole 2x2x4 slice. The times are simulated.
32 devices in a mesh: gx: 4 (over z), gy: 4 (over y, x), gz: 2 (over core).
Axes of the slice: x: 2, y: 2, z: 4, core: 2. Of those that a mesh axis runs over, the one named last changes fastest.
Arguments:
- adjoint_residual: float32 [32, 64, 256], P('gx', 'gy', 'gz'), may hold values from -6 to 6
- face_x: float32 [32, 64, 256], P('gx', 'gy', 'gz'), may hold values from 0.03 to 30
- face_y: float32 [32, 64, 256], P('gx', 'gy', 'gz'), may hold values from 0.03 to 30
- face_z: float32 [32, 64, 256], P('gx', 'gy', 'gz'), may hold values from 0.03 to 30
Outputs:
- correction: float32 [32, 64, 256], P('gx', 'gy', 'gz')
All inputs are finite; a program needn't handle non-finite values.
Results may differ from a plain program's by a relative error of at most 0.0001.
Values sent between devices are 32-bit elements; how exact they have to be, the bound alone decides.
No kernel may reach another device: no remote copies, remote signals or barrier semaphores. Data moves between devices by JAX's collectives and lax.ppermute only.
A program may use at most 64 MiB of HBM per device.

v0:
```python
import jax
import jax.numpy as jnp
from jax import lax
from jax.sharding import PartitionSpec as P

LEVELS = 4
COARSE_ITERS = 6


damping = 2.0 / 3.0


def extended(block, sides, width):
    for axis, dim in sides:
        count = lax.axis_size(axis)
        forward = [(i, i + 1) for i in range(count - 1)]
        backward = [(target, source) for source, target in forward]
        low = lax.ppermute(
            lax.slice_in_dim(block, block.shape[dim] - width, None, axis=dim), axis, forward
        )
        high = lax.ppermute(lax.slice_in_dim(block, 0, width, axis=dim), axis, backward)
        block = jnp.concatenate([low, block, high], axis=dim)
    return block


def from_behind(block, axis, distance):
    devices = range(lax.axis_size(axis))
    route = [(i - distance, i) for i in devices if i - distance in devices]
    return lax.ppermute(block, axis, route)


def stencil(padded, field, coefs):
    low_x, high_x, low_y, high_y, low_z, high_z = coefs
    diagonal = low_x + high_x + low_y + high_y + low_z + high_z
    result = diagonal * field - low_x * padded[:-2, 1:-1, 1:-1] - high_x * padded[2:, 1:-1, 1:-1]
    result = result - low_y * padded[1:-1, :-2, 1:-1] - high_y * padded[1:-1, 2:, 1:-1]
    return result - low_z * padded[1:-1, 1:-1, :-2] - high_z * padded[1:-1, 1:-1, 2:]


def operate(field, coefs):
    padded = extended(field, (("gx", 0), ("gy", 1), ("gz", 2)), 1)
    return stencil(padded, field, coefs)


def operate_whole(field, coefs):
    return stencil(jnp.pad(field, 1), field, coefs)


def blocked(values):
    return values.reshape(values.shape[0] // 2, 2, values.shape[1] // 2, 2, values.shape[2] // 2, 2)


def coarse_face(values, dim, parity):
    others = tuple((2 * k + 1 for k in range(3) if k != dim))
    summed = jnp.sum(blocked(values), axis=others)
    return 0.5 * lax.index_in_dim(summed, parity, dim + 1, keepdims=False)


def coarsen(coefs):
    result = []
    for dim in range(3):
        result.append(coarse_face(coefs[2 * dim], dim, 0))
        result.append(coarse_face(coefs[2 * dim + 1], dim, 1))
    return tuple(result)


def restrict(values):
    return jnp.sum(blocked(values), axis=(1, 3, 5))


def prolong(values):
    shape_out = (values.shape[0] * 2, values.shape[1] * 2, values.shape[2] * 2)
    wide = jnp.broadcast_to(
        values[:, None, :, None, :, None],
        (values.shape[0], 2, values.shape[1], 2, values.shape[2], 2),
    )
    return wide.reshape(shape_out)


def total_local(value):
    return value


def conj_grad(rhs, coefs, apply_op, total):
    solution = jnp.zeros_like(rhs)
    remain = rhs
    search = rhs
    norm_now = total(jnp.sum(remain * remain))
    for step in range(COARSE_ITERS):
        image = apply_op(search, coefs)
        alpha = norm_now / total(jnp.sum(search * image))
        solution = solution + alpha * search
        remain = remain - alpha * image
        norm_next = total(jnp.sum(remain * remain))
        search = remain + norm_next / norm_now * search
        norm_now = norm_next
    return solution


def coarse_solve(rhs, coefs):
    part_x, part_y, part_z = rhs.shape
    count_x = lax.axis_size("gx")
    count_y = lax.axis_size("gy")
    count_z = lax.axis_size("gz")
    stacked = jnp.stack((rhs,) + coefs)[None]
    whole = lax.all_gather(stacked, ("gx", "gy", "gz"), axis=0, tiled=True)
    whole = whole.reshape(count_x, count_y, count_z, 7, part_x, part_y, part_z)
    whole = whole.transpose(3, 0, 4, 1, 5, 2, 6).reshape(
        7, count_x * part_x, count_y * part_y, count_z * part_z
    )
    whole_coefs = tuple((whole[k] for k in range(1, 7)))
    solution = conj_grad(whole[0], whole_coefs, operate_whole, total_local)
    starts = (
        lax.axis_index("gx") * part_x,
        lax.axis_index("gy") * part_y,
        lax.axis_index("gz") * part_z,
    )
    return lax.dynamic_slice(solution, starts, (part_x, part_y, part_z))


def cycle(rhs, levels_left, coefs):
    if levels_left == 1:
        return coarse_solve(rhs, coefs)
    diagonal = coefs[0] + coefs[1] + coefs[2] + coefs[3] + coefs[4] + coefs[5]
    field = damping * rhs / diagonal
    field = field + damping * (rhs - operate(field, coefs)) / diagonal
    remain = rhs - operate(field, coefs)
    field = field + prolong(cycle(restrict(remain), levels_left - 1, coarsen(coefs)))
    field = field + damping * (rhs - operate(field, coefs)) / diagonal
    return field


def per_device(adjoint_residual, face_x, face_y, face_z):
    rim_x = from_behind(face_x[:1], "gx", -1)
    rim_y = from_behind(face_y[:, :1], "gy", -1)
    rim_z = from_behind(face_z[:, :, :1], "gz", -1)
    high_x = jnp.concatenate([face_x[1:], rim_x], 0)
    high_y = jnp.concatenate([face_y[:, 1:], rim_y], 1)
    high_z = jnp.concatenate([face_z[:, :, 1:], rim_z], 2)
    coefs = (face_x, high_x, face_y, high_y, face_z, high_z)
    return cycle(adjoint_residual, LEVELS, coefs)


def solution(mesh):
    return jax.shard_map(
        per_device,
        mesh=mesh,
        in_specs=(
            P("gx", "gy", "gz"),
            P("gx", "gy", "gz"),
            P("gx", "gy", "gz"),
            P("gx", "gy", "gz"),
        ),
        out_specs=P("gx", "gy", "gz"),
        check_vma=False,
    )
```

profile of v0, /device:TPU:0, one launch (start us, length us, event | category | flops | bytes accessed | tf_op | source)
XLA Modules:
  0.0 335.5 jit_solution(15201036902934139529)
XLA Ops:
  5.4 6.3 %reshape.224 = f32[4,2,8,2,64,2]{5,4,3,2,1,0:T(8,128)} reshape(f32[8,16,128]{2,1,0:T(8,128)} %param.7) | data formatting | bytes 131072 | tf_op jit(solution)/shard_map/reshape | solution.py:50
  11.7 5.5 %reshape.222 = f32[4,2,8,2,64,2]{5,4,3,2,1,0:T(8,128)} reshape(f32[8,16,128]{2,1,0:T(8,128)S(1)} %copy-done) | data formatting | bytes 131072 | tf_op jit(solution)/shard_map/reshape | solution.py:50
  23.3 5.5 %reshape.220 = f32[4,2,8,2,64,2]{5,4,3,2,1,0:T(8,128)} reshape(f32[8,16,128]{2,1,0:T(8,128)S(1)} %copy-done.2) | data formatting | bytes 131072 | tf_op jit(solution)/shard_map/reshape | solution.py:50
  31.8 5.6 %collective-permute-start.3 = (f32[1,16,128]{2,1,0:T(8,128)S(1)}, f32[1,16,128]{2,1,0:T(8,128)S(1)}, u32[]{:S(2)}, u32[]{:S(2)}) collective-permute-start(f32[1,16,128]{2,1,0:T(8,128)S(1)} %get-tuple-element.49), channel_id=1, source_target_pairs={{0,8},{8,16},{16,24},{1,9},{9,17},{17,25},{2,10},{10,18},{18,26},{... | collective-permute-start | bytes 24584 | tf_op jit(solution)/shard_map/ppermute | solution.py:18
  39.4 3.5 %collective-permute-done.4 = f32[1,16,128]{2,1,0:T(8,128)S(1)} collective-permute-done((f32[1,16,128]{2,1,0:T(8,128)S(1)}, f32[1,16,128]{2,1,0:T(8,128)S(1)}, u32[]{:S(2)}, u32[]{:S(2)}) %collective-permute-start.4) | collective-permute-done | bytes 8224 | tf_op jit(solution)/shard_map/ppermute | solution.py:21
  43.0 4.5 %collective-permute-start.5 = (f32[10,1,128]{2,1,0:T(1,128)S(1)}, f32[10,1,128]{2,1,0:T(1,128)S(1)}, u32[]{:S(2)}, u32[]{:S(2)}) collective-permute-start(f32[10,1,128]{2,1,0:T(1,128)S(1)} %get-tuple-element.42), channel_id=1, source_target_pairs={{0,2},{2,4},{4,6},{1,3},{3,5},{5,7},{8,10},{10,12},{12,14},{9,11},... | collective-permute-start | bytes 15368 | tf_op jit(solution)/shard_map/ppermute | solution.py:18
  49.5 4.3 %collective-permute-done.6 = f32[10,1,128]{2,1,0:T(1,128)S(1)} collective-permute-done((f32[10,1,128]{2,1,0:T(1,128)S(1)}, f32[10,1,128]{2,1,0:T(1,128)S(1)}, u32[]{:S(2)}, u32[]{:S(2)}) %collective-permute-start.6) | collective-permute-done | bytes 5152 | tf_op jit(solution)/shard_map/ppermute | solution.py:21
  60.0 4.5 %collective-permute-start.9 = (f32[1,16,128]{2,1,0:T(8,128)S(1)}, f32[1,16,128]{2,1,0:T(8,128)S(1)}, u32[]{:S(2)}, u32[]{:S(2)}) collective-permute-start(f32[1,16,128]{2,1,0:T(8,128)S(1)} %get-tuple-element.47), channel_id=1, source_target_pairs={{0,8},{8,16},{16,24},{1,9},{9,17},{17,25},{2,10},{10,18},{18,26},{... | collective-permute-start | bytes 24584 | tf_op jit(solution)/shard_map/ppermute | solution.py:18
  65.9 4.8 %collective-permute-start.11 = (f32[10,1,128]{2,1,0:T(1,128)S(1)}, f32[10,1,128]{2,1,0:T(1,128)S(1)}, u32[]{:S(2)}, u32[]{:S(2)}) collective-permute-start(f32[10,1,128]{2,1,0:T(1,128)S(1)} %get-tuple-element.40), channel_id=1, source_target_pairs={{0,2},{2,4},{4,6},{1,3},{3,5},{5,7},{8,10},{10,12},{12,14},{9,11},... | collective-permute-start | bytes 15368 | tf_op jit(solution)/shard_map/ppermute | solution.py:18
  72.0 4.2 %collective-permute-done.12 = f32[10,1,128]{2,1,0:T(1,128)S(1)} collective-permute-done((f32[10,1,128]{2,1,0:T(1,128)S(1)}, f32[10,1,128]{2,1,0:T(1,128)S(1)}, u32[]{:S(2)}, u32[]{:S(2)}) %collective-permute-start.12) | collective-permute-done | bytes 5152 | tf_op jit(solution)/shard_map/ppermute | solution.py:21
  79.3 5.5 %reshape.225 = f32[4,2,8,2,64,2]{5,4,3,2,1,0:T(8,128)} reshape(f32[8,16,128]{2,1,0:T(8,128)S(1)} %get-tuple-element.23) | data formatting | bytes 131072 | tf_op jit(solution)/shard_map/reshape | solution.py:50
  84.8 5.5 %reshape.223 = f32[4,2,8,2,64,2]{5,4,3,2,1,0:T(8,128)} reshape(f32[8,16,128]{2,1,0:T(8,128)S(1)} %get-tuple-element.22) | data formatting | bytes 131072 | tf_op jit(solution)/shard_map/reshape | solution.py:50
  96.7 5.5 %reshape.221 = f32[4,2,8,2,64,2]{5,4,3,2,1,0:T(8,128)} reshape(f32[8,16,128]{2,1,0:T(8,128)S(1)} %get-tuple-element.46) | data formatting | bytes 131072 | tf_op jit(solution)/shard_map/reshape | solution.py:50
  105.2 5.5 %reshape.219 = f32[4,2,8,2,64,2]{5,4,3,2,1,0:T(8,128)} reshape(f32[8,16,128]{2,1,0:T(8,128)S(1)} %fusion.18) | data formatting | bytes 131072 | tf_op jit(solution)/shard_map/reshape | solution.py:50
  113.3 4.2 %collective-permute-start.15 = (f32[1,8,64]{2,1,0:T(8,128)S(1)}, f32[1,8,64]{2,1,0:T(8,128)S(1)}, u32[]{:S(2)}, u32[]{:S(2)}) collective-permute-start(f32[1,8,64]{2,1,0:T(8,128)S(1)} %get-tuple-element.73), channel_id=1, source_target_pairs={{0,8},{8,16},{16,24},{1,9},{9,17},{17,25},{2,10},{10,18},{18,26},{... | collective-permute-start | bytes 6152 | tf_op jit(solution)/shard_map/ppermute | solution.py:18
  119.0 4.0 %collective-permute-done.16 = f32[1,8,64]{2,1,0:T(8,128)S(1)} collective-permute-done((f32[1,8,64]{2,1,0:T(8,128)S(1)}, f32[1,8,64]{2,1,0:T(8,128)S(1)}, u32[]{:S(2)}, u32[]{:S(2)}) %collective-permute-start.16) | collective-permute-done | bytes 2080 | tf_op jit(solution)/shard_map/ppermute | solution.py:21
  127.1 4.2 %collective-permute-done.18 = f32[6,1,64]{2,1,0:T(1,128)S(1)} collective-permute-done((f32[6,1,64]{2,1,0:T(1,128)S(1)}, f32[6,1,64]{2,1,0:T(1,128)S(1)}, u32[]{:S(2)}, u32[]{:S(2)}) %collective-permute-start.18) | collective-permute-done | bytes 1568 | tf_op jit(solution)/shard_map/ppermute | solution.py:21
  135.9 3.5 %collective-permute-start.21 = (f32[1,8,64]{2,1,0:T(8,128)S(1)}, f32[1,8,64]{2,1,0:T(8,128)S(1)}, u32[]{:S(2)}, u32[]{:S(2)}) collective-permute-start(f32[1,8,64]{2,1,0:T(8,128)S(1)} %get-tuple-element.71), channel_id=1, source_target_pairs={{0,8},{8,16},{16,24},{1,9},{9,17},{17,25},{2,10},{10,18},{18,26},{... | collective-permute-start | bytes 6152 | tf_op jit(solution)/shard_map/ppermute | solution.py:18
  163.5 4.0 %collective-permute-done.28 = f32[1,4,32]{2,1,0:T(4,128)S(1)} collective-permute-done((f32[1,4,32]{2,1,0:T(4,128)S(1)}, f32[1,4,32]{2,1,0:T(4,128)S(1)}, u32[]{:S(2)}, u32[]{:S(2)}) %collective-permute-start.28) | collective-permute-done | bytes 544 | tf_op jit(solution)/shard_map/ppermute | solution.py:21
  171.7 4.2 %collective-permute-done.30 = f32[4,1,32]{2,1,0:T(1,128)S(1)} collective-permute-done((f32[4,1,32]{2,1,0:T(1,128)S(1)}, f32[4,1,32]{2,1,0:T(1,128)S(1)}, u32[]{:S(2)}, u32[]{:S(2)}) %collective-permute-start.30) | collective-permute-done | bytes 544 | tf_op jit(solution)/shard_map/ppermute | solution.py:21
  183.8 4.0 %collective-permute-done.34 = f32[1,4,32]{2,1,0:T(4,128)S(1)} collective-permute-done((f32[1,4,32]{2,1,0:T(4,128)S(1)}, f32[1,4,32]{2,1,0:T(4,128)S(1)}, u32[]{:S(2)}, u32[]{:S(2)}) %collective-permute-start.34) | collective-permute-done | bytes 544 | tf_op jit(solution)/shard_map/ppermute | solution.py:21
  192.1 4.0 %collective-permute-done.36 = f32[4,1,32]{2,1,0:T(1,128)S(1)} collective-permute-done((f32[4,1,32]{2,1,0:T(1,128)S(1)}, f32[4,1,32]{2,1,0:T(1,128)S(1)}, u32[]{:S(2)}, u32[]{:S(2)}) %collective-permute-start.36) | collective-permute-done | bytes 544 | tf_op jit(solution)/shard_map/ppermute | solution.py:21
  200.9 38.1 %all-gather = f32[224,1,2,16]{3,2,1,0:T(2,128)S(1)} all-gather(f32[7,1,2,16]{3,2,1,0:T(2,128)S(1)} %constant_dynamic-update-slice_fusion), channel_id=2, replica_groups=mesh['gx'=4,'gy'=4,'gz'=2] {'gx','gy','gz'}, dimensions={0}, use_global_device_ids=true | all-gather | bytes 29568 | tf_op jit(solution)/shard_map/all_gather | solution.py:106
  266.2 4.2 %collective-permute-done.40 = f32[1,4,32]{2,1,0:T(4,128)S(1)} collective-permute-done((f32[1,4,32]{2,1,0:T(4,128)S(1)}, f32[1,4,32]{2,1,0:T(4,128)S(1)}, u32[]{:S(2)}, u32[]{:S(2)}) %collective-permute-start.40) | collective-permute-done | bytes 544 | tf_op jit(solution)/shard_map/ppermute | solution.py:21
  274.7 4.2 %collective-permute-done.42 = f32[4,1,32]{2,1,0:T(1,128)S(1)} collective-permute-done((f32[4,1,32]{2,1,0:T(1,128)S(1)}, f32[4,1,32]{2,1,0:T(1,128)S(1)}, u32[]{:S(2)}, u32[]{:S(2)}) %collective-permute-start.42) | collective-permute-done | bytes 544 | tf_op jit(solution)/shard_map/ppermute | solution.py:21
  286.8 4.2 %collective-permute-done.46 = f32[1,8,64]{2,1,0:T(8,128)S(1)} collective-permute-done((f32[1,8,64]{2,1,0:T(8,128)S(1)}, f32[1,8,64]{2,1,0:T(8,128)S(1)}, u32[]{:S(2)}, u32[]{:S(2)}) %collective-permute-start.46) | collective-permute-done | bytes 2080 | tf_op jit(solution)/shard_map/ppermute | solution.py:21
  295.2 4.2 %collective-permute-done.48 = f32[6,1,64]{2,1,0:T(1,128)S(1)} collective-permute-done((f32[6,1,64]{2,1,0:T(1,128)S(1)}, f32[6,1,64]{2,1,0:T(1,128)S(1)}, u32[]{:S(2)}, u32[]{:S(2)}) %collective-permute-start.48) | collective-permute-done | bytes 1568 | tf_op jit(solution)/shard_map/ppermute | solution.py:21
  306.5 4.0 %reshape.229 = f32[8,16,128]{2,1,0:T(8,128)S(1)} reshape(f32[4,2,8,2,64,2]{5,4,3,2,1,0:T(8,128)} %broadcast_in_dim.33) | data formatting | bytes 131072 | tf_op jit(solution)/shard_map/reshape | solution.py:77
  310.5 3.9 %collective-permute-start.51 = (f32[1,16,128]{2,1,0:T(8,128)S(1)}, f32[1,16,128]{2,1,0:T(8,128)S(1)}, u32[]{:S(2)}, u32[]{:S(2)}) collective-permute-start(f32[1,16,128]{2,1,0:T(8,128)S(1)} %get-tuple-element.44), channel_id=1, source_target_pairs={{0,8},{8,16},{16,24},{1,9},{9,17},{17,25},{2,10},{10,18},{18,26},{... | collective-permute-start | bytes 24584 | tf_op jit(solution)/shard_map/ppermute | solution.py:18
  315.7 4.2 %collective-permute-done.52 = f32[1,16,128]{2,1,0:T(8,128)S(1)} collective-permute-done((f32[1,16,128]{2,1,0:T(8,128)S(1)}, f32[1,16,128]{2,1,0:T(8,128)S(1)}, u32[]{:S(2)}, u32[]{:S(2)}) %collective-permute-start.52) | collective-permute-done | bytes 8224 | tf_op jit(solution)/shard_map/ppermute | solution.py:21
  320.0 4.5 %collective-permute-start.53 = (f32[10,1,128]{2,1,0:T(1,128)S(1)}, f32[10,1,128]{2,1,0:T(1,128)S(1)}, u32[]{:S(2)}, u32[]{:S(2)}) collective-permute-start(f32[10,1,128]{2,1,0:T(1,128)S(1)} %get-tuple-element.38), channel_id=1, source_target_pairs={{0,2},{2,4},{4,6},{1,3},{3,5},{5,7},{8,10},{10,12},{12,14},{9,11},... | collective-permute-start | bytes 15368 | tf_op jit(solution)/shard_map/ppermute | solution.py:18
  325.8 4.2 %collective-permute-done.54 = f32[10,1,128]{2,1,0:T(1,128)S(1)} collective-permute-done((f32[10,1,128]{2,1,0:T(1,128)S(1)}, f32[10,1,128]{2,1,0:T(1,128)S(1)}, u32[]{:S(2)}, u32[]{:S(2)}) %collective-permute-start.54) | collective-permute-done | bytes 5152 | tf_op jit(solution)/shard_map/ppermute | solution.py:21
  (263 shorter events, 140.6 us)
Async XLA Ops:
  0.7 30.9 %collective-permute-start = (f32[1,16,128]{2,1,0:T(8,128)S(1)}, f32[1,16,128]{2,1,0:T(8,128)S(1)}, u32[]{:S(2)}, u32[]{:S(2)}) collective-permute-start(f32[1,16,128]{2,1,0:T(8,128)S(1)} %slice.587), channel_id=1, source_target_pairs={{8,0},{16,8},{24,16},{9,1},{17,9},{25,17},{10,2},{18,10},{26,18},{... | collective-permute-start | bytes 24584 | tf_op jit(solution)/shard_map/ppermute | solution.py:29
  2.0 29.6 %collective-permute-start.2 = (f32[8,16,1]{2,1,0:T(8,128)}, f32[8,16,1]{2,1,0:T(8,128)S(1)}, u32[]{:S(2)}, u32[]{:S(2)}) collective-permute-start(f32[8,16,1]{2,1,0:T(8,128)} %bitcast.288), channel_id=1, source_target_pairs={{1,0},{3,2},{5,4},{7,6},{9,8},{11,10},{13,12},{15,14},{17,16},{19,... | collective-permute-start | bytes 1544 | tf_op jit(solution)/shard_map/ppermute | solution.py:29
  4.1 27.6 %collective-permute-start.1 = (f32[8,1,128]{2,1,0:T(1,128)S(1)}, f32[8,1,128]{2,1,0:T(1,128)S(1)}, u32[]{:S(2)}, u32[]{:S(2)}) collective-permute-start(f32[8,1,128]{2,1,0:T(1,128)S(1)} %slice.589), channel_id=1, source_target_pairs={{2,0},{4,2},{6,4},{3,1},{5,3},{7,5},{10,8},{12,10},{14,12},{11,9},... | collective-permute-start | bytes 12296 | tf_op jit(solution)/shard_map/ppermute | solution.py:29
  31.8 7.6 %collective-permute-start.3 = (f32[1,16,128]{2,1,0:T(8,128)S(1)}, f32[1,16,128]{2,1,0:T(8,128)S(1)}, u32[]{:S(2)}, u32[]{:S(2)}) collective-permute-start(f32[1,16,128]{2,1,0:T(8,128)S(1)} %get-tuple-element.49), channel_id=1, source_target_pairs={{0,8},{8,16},{16,24},{1,9},{9,17},{17,25},{2,10},{10,18},{18,26},{... | collective-permute-start | bytes 24584 | tf_op jit(solution)/shard_map/ppermute | solution.py:18
  37.4 5.5 %collective-permute-start.4 = (f32[1,16,128]{2,1,0:T(8,128)S(1)}, f32[1,16,128]{2,1,0:T(8,128)S(1)}, u32[]{:S(2)}, u32[]{:S(2)}) collective-permute-start(f32[1,16,128]{2,1,0:T(8,128)S(1)} %get-tuple-element.50), channel_id=1, source_target_pairs={{8,0},{16,8},{24,16},{9,1},{17,9},{25,17},{10,2},{18,10},{26,18},{... | collective-permute-start | bytes 24584 | tf_op jit(solution)/shard_map/ppermute | solution.py:21
  43.0 6.6 %collective-permute-start.5 = (f32[10,1,128]{2,1,0:T(1,128)S(1)}, f32[10,1,128]{2,1,0:T(1,128)S(1)}, u32[]{:S(2)}, u32[]{:S(2)}) collective-permute-start(f32[10,1,128]{2,1,0:T(1,128)S(1)} %get-tuple-element.42), channel_id=1, source_target_pairs={{0,2},{2,4},{4,6},{1,3},{3,5},{5,7},{8,10},{10,12},{12,14},{9,11},... | collective-permute-start | bytes 15368 | tf_op jit(solution)/shard_map/ppermute | solution.py:18
  47.5 6.3 %collective-permute-start.6 = (f32[10,1,128]{2,1,0:T(1,128)S(1)}, f32[10,1,128]{2,1,0:T(1,128)S(1)}, u32[]{:S(2)}, u32[]{:S(2)}) collective-permute-start(f32[10,1,128]{2,1,0:T(1,128)S(1)} %get-tuple-element.43), channel_id=1, source_target_pairs={{2,0},{4,2},{6,4},{3,1},{5,3},{7,5},{10,8},{12,10},{14,12},{11,9},... | collective-permute-start | bytes 15368 | tf_op jit(solution)/shard_map/ppermute | solution.py:21
  58.7 6.6 %collective-permute-start.10 = (f32[1,16,128]{2,1,0:T(8,128)S(1)}, f32[1,16,128]{2,1,0:T(8,128)S(1)}, u32[]{:S(2)}, u32[]{:S(2)}) collective-permute-start(f32[1,16,128]{2,1,0:T(8,128)S(1)} %get-tuple-element.48), channel_id=1, source_target_pairs={{8,0},{16,8},{24,16},{9,1},{17,9},{25,17},{10,2},{18,10},{26,18},{... | collective-permute-start | bytes 24584 | tf_op jit(solution)/shard_map/ppermute | solution.py:21
  60.0 5.9 %collective-permute-start.9 = (f32[1,16,128]{2,1,0:T(8,128)S(1)}, f32[1,16,128]{2,1,0:T(8,128)S(1)}, u32[]{:S(2)}, u32[]{:S(2)}) collective-permute-start(f32[1,16,128]{2,1,0:T(8,128)S(1)} %get-tuple-element.47), channel_id=1, source_target_pairs={{0,8},{8,16},{16,24},{1,9},{9,17},{17,25},{2,10},{10,18},{18,26},{... | collective-permute-start | bytes 24584 | tf_op jit(solution)/shard_map/ppermute | solution.py:18
  65.9 6.1 %collective-permute-start.11 = (f32[10,1,128]{2,1,0:T(1,128)S(1)}, f32[10,1,128]{2,1,0:T(1,128)S(1)}, u32[]{:S(2)}, u32[]{:S(2)}) collective-permute-start(f32[10,1,128]{2,1,0:T(1,128)S(1)} %get-tuple-element.40), channel_id=1, source_target_pairs={{0,2},{2,4},{4,6},{1,3},{3,5},{5,7},{8,10},{10,12},{12,14},{9,11},... | collective-permute-start | bytes 15368 | tf_op jit(solution)/shard_map/ppermute | solution.py:18
  70.7 5.5 %collective-permute-start.12 = (f32[10,1,128]{2,1,0:T(1,128)S(1)}, f32[10,1,128]{2,1,0:T(1,128)S(1)}, u32[]{:S(2)}, u32[]{:S(2)}) collective-permute-start(f32[10,1,128]{2,1,0:T(1,128)S(1)} %get-tuple-element.41), channel_id=1, source_target_pairs={{2,0},{4,2},{6,4},{3,1},{5,3},{7,5},{10,8},{12,10},{14,12},{11,9},... | collective-permute-start | bytes 15368 | tf_op jit(solution)/shard_map/ppermute | solution.py:21
  76.3 28.7 %collective-permute-start.13 = (f32[10,18,1]{2,1,0:T(8,128)S(1)}, f32[10,18,1]{2,1,0:T(8,128)S(1)}, u32[]{:S(2)}, u32[]{:S(2)}) collective-permute-start(f32[10,18,1]{2,1,0:T(8,128)S(1)} %get-tuple-element.34), channel_id=1, source_target_pairs={{0,1},{2,3},{4,5},{6,7},{8,9},{10,11},{12,13},{14,15},{16,17},{18,... | collective-permute-start | bytes 2168 | tf_op jit(solution)/shard_map/ppermute | solution.py:18
  77.6 27.4 %collective-permute-start.14 = (f32[10,18,1]{2,1,0:T(8,128)S(1)}, f32[10,18,1]{2,1,0:T(8,128)S(1)}, u32[]{:S(2)}, u32[]{:S(2)}) collective-permute-start(f32[10,18,1]{2,1,0:T(8,128)S(1)} %get-tuple-element.35), channel_id=1, source_target_pairs={{1,0},{3,2},{5,4},{7,6},{9,8},{11,10},{13,12},{15,14},{17,16},{19,... | collective-permute-start | bytes 2168 | tf_op jit(solution)/shard_map/ppermute | solution.py:21
  113.3 5.7 %collective-permute-start.15 = (f32[1,8,64]{2,1,0:T(8,128)S(1)}, f32[1,8,64]{2,1,0:T(8,128)S(1)}, u32[]{:S(2)}, u32[]{:S(2)}) collective-permute-start(f32[1,8,64]{2,1,0:T(8,128)S(1)} %get-tuple-element.73), channel_id=1, source_target_pairs={{0,8},{8,16},{16,24},{1,9},{9,17},{17,25},{2,10},{10,18},{18,26},{... | collective-permute-start | bytes 6152 | tf_op jit(solution)/shard_map/ppermute | solution.py:18
  117.5 5.5 %collective-permute-start.16 = (f32[1,8,64]{2,1,0:T(8,128)S(1)}, f32[1,8,64]{2,1,0:T(8,128)S(1)}, u32[]{:S(2)}, u32[]{:S(2)}) collective-permute-start(f32[1,8,64]{2,1,0:T(8,128)S(1)} %get-tuple-element.74), channel_id=1, source_target_pairs={{8,0},{16,8},{24,16},{9,1},{17,9},{25,17},{10,2},{18,10},{26,18},{... | collective-permute-start | bytes 6152 | tf_op jit(solution)/shard_map/ppermute | solution.py:21
  125.8 5.5 %collective-permute-start.18 = (f32[6,1,64]{2,1,0:T(1,128)S(1)}, f32[6,1,64]{2,1,0:T(1,128)S(1)}, u32[]{:S(2)}, u32[]{:S(2)}) collective-permute-start(f32[6,1,64]{2,1,0:T(1,128)S(1)} %get-tuple-element.62), channel_id=1, source_target_pairs={{2,0},{4,2},{6,4},{3,1},{5,3},{7,5},{10,8},{12,10},{14,12},{11,9},... | collective-permute-start | bytes 4616 | tf_op jit(solution)/shard_map/ppermute | solution.py:21
  135.9 5.5 %collective-permute-start.21 = (f32[1,8,64]{2,1,0:T(8,128)S(1)}, f32[1,8,64]{2,1,0:T(8,128)S(1)}, u32[]{:S(2)}, u32[]{:S(2)}) collective-permute-start(f32[1,8,64]{2,1,0:T(8,128)S(1)} %get-tuple-element.71), channel_id=1, source_target_pairs={{0,8},{8,16},{16,24},{1,9},{9,17},{17,25},{2,10},{10,18},{18,26},{... | collective-permute-start | bytes 6152 | tf_op jit(solution)/shard_map/ppermute | solution.py:18
  139.4 5.5 %collective-permute-start.22 = (f32[1,8,64]{2,1,0:T(8,128)S(1)}, f32[1,8,64]{2,1,0:T(8,128)S(1)}, u32[]{:S(2)}, u32[]{:S(2)}) collective-permute-start(f32[1,8,64]{2,1,0:T(8,128)S(1)} %get-tuple-element.72), channel_id=1, source_target_pairs={{8,0},{16,8},{24,16},{9,1},{17,9},{25,17},{10,2},{18,10},{26,18},{... | collective-permute-start | bytes 6152 | tf_op jit(solution)/shard_map/ppermute | solution.py:21
  147.7 5.5 %collective-permute-start.24 = (f32[6,1,64]{2,1,0:T(1,128)S(1)}, f32[6,1,64]{2,1,0:T(1,128)S(1)}, u32[]{:S(2)}, u32[]{:S(2)}) collective-permute-start(f32[6,1,64]{2,1,0:T(1,128)S(1)} %get-tuple-element.60), channel_id=1, source_target_pairs={{2,0},{4,2},{6,4},{3,1},{5,3},{7,5},{10,8},{12,10},{14,12},{11,9},... | collective-permute-start | bytes 4616 | tf_op jit(solution)/shard_map/ppermute | solution.py:21
  158.5 5.0 %collective-permute-start.27 = (f32[1,4,32]{2,1,0:T(4,128)S(1)}, f32[1,4,32]{2,1,0:T(4,128)S(1)}, u32[]{:S(2)}, u32[]{:S(2)}) collective-permute-start(f32[1,4,32]{2,1,0:T(4,128)S(1)} %get-tuple-element.85), channel_id=1, source_target_pairs={{0,8},{8,16},{16,24},{1,9},{9,17},{17,25},{2,10},{10,18},{18,26},{... | collective-permute-start | bytes 1544 | tf_op jit(solution)/shard_map/ppermute | solution.py:18
  162.0 5.5 %collective-permute-start.28 = (f32[1,4,32]{2,1,0:T(4,128)S(1)}, f32[1,4,32]{2,1,0:T(4,128)S(1)}, u32[]{:S(2)}, u32[]{:S(2)}) collective-permute-start(f32[1,4,32]{2,1,0:T(4,128)S(1)} %get-tuple-element.86), channel_id=1, source_target_pairs={{8,0},{16,8},{24,16},{9,1},{17,9},{25,17},{10,2},{18,10},{26,18},{... | collective-permute-start | bytes 1544 | tf_op jit(solution)/shard_map/ppermute | solution.py:21
  170.3 5.5 %collective-permute-start.30 = (f32[4,1,32]{2,1,0:T(1,128)S(1)}, f32[4,1,32]{2,1,0:T(1,128)S(1)}, u32[]{:S(2)}, u32[]{:S(2)}) collective-permute-start(f32[4,1,32]{2,1,0:T(1,128)S(1)} %get-tuple-element.80), channel_id=1, source_target_pairs={{2,0},{4,2},{6,4},{3,1},{5,3},{7,5},{10,8},{12,10},{14,12},{11,9},... | collective-permute-start | bytes 1544 | tf_op jit(solution)/shard_map/ppermute | solution.py:21
  182.3 5.5 %collective-permute-start.34 = (f32[1,4,32]{2,1,0:T(4,128)S(1)}, f32[1,4,32]{2,1,0:T(4,128)S(1)}, u32[]{:S(2)}, u32[]{:S(2)}) collective-permute-start(f32[1,4,32]{2,1,0:T(4,128)S(1)} %get-tuple-element.84), channel_id=1, source_target_pairs={{8,0},{16,8},{24,16},{9,1},{17,9},{25,17},{10,2},{18,10},{26,18},{... | collective-permute-start | bytes 1544 | tf_op jit(solution)/shard_map/ppermute | solution.py:21
  190.6 5.5 %collective-permute-start.36 = (f32[4,1,32]{2,1,0:T(1,128)S(1)}, f32[4,1,32]{2,1,0:T(1,128)S(1)}, u32[]{:S(2)}, u32[]{:S(2)}) collective-permute-start(f32[4,1,32]{2,1,0:T(1,128)S(1)} %get-tuple-element.78), channel_id=1, source_target_pairs={{2,0},{4,2},{6,4},{3,1},{5,3},{7,5},{10,8},{12,10},{14,12},{11,9},... | collective-permute-start | bytes 1544 | tf_op jit(solution)/shard_map/ppermute | solution.py:21
  264.9 5.5 %collective-permute-start.40 = (f32[1,4,32]{2,1,0:T(4,128)S(1)}, f32[1,4,32]{2,1,0:T(4,128)S(1)}, u32[]{:S(2)}, u32[]{:S(2)}) collective-permute-start(f32[1,4,32]{2,1,0:T(4,128)S(1)} %get-tuple-element.82), channel_id=1, source_target_pairs={{8,0},{16,8},{24,16},{9,1},{17,9},{25,17},{10,2},{18,10},{26,18},{... | collective-permute-start | bytes 1544 | tf_op jit(solution)/shard_map/ppermute | solution.py:21
  273.4 5.5 %collective-permute-start.42 = (f32[4,1,32]{2,1,0:T(1,128)S(1)}, f32[4,1,32]{2,1,0:T(1,128)S(1)}, u32[]{:S(2)}, u32[]{:S(2)}) collective-permute-start(f32[4,1,32]{2,1,0:T(1,128)S(1)} %get-tuple-element.76), channel_id=1, source_target_pairs={{2,0},{4,2},{6,4},{3,1},{5,3},{7,5},{10,8},{12,10},{14,12},{11,9},... | collective-permute-start | bytes 1544 | tf_op jit(solution)/shard_map/ppermute | solution.py:21
  285.5 5.5 %collective-permute-start.46 = (f32[1,8,64]{2,1,0:T(8,128)S(1)}, f32[1,8,64]{2,1,0:T(8,128)S(1)}, u32[]{:S(2)}, u32[]{:S(2)}) collective-permute-start(f32[1,8,64]{2,1,0:T(8,128)S(1)} %get-tuple-element.64), channel_id=1, source_target_pairs={{8,0},{16,8},{24,16},{9,1},{17,9},{25,17},{10,2},{18,10},{26,18},{... | collective-permute-start | bytes 6152 | tf_op jit(solution)/shard_map/ppermute | solution.py:21
  293.9 5.5 %collective-permute-start.48 = (f32[6,1,64]{2,1,0:T(1,128)S(1)}, f32[6,1,64]{2,1,0:T(1,128)S(1)}, u32[]{:S(2)}, u32[]{:S(2)}) collective-permute-start(f32[6,1,64]{2,1,0:T(1,128)S(1)} %get-tuple-element.58), channel_id=1, source_target_pairs={{2,0},{4,2},{6,4},{3,1},{5,3},{7,5},{10,8},{12,10},{14,12},{11,9},... | collective-permute-start | bytes 4616 | tf_op jit(solution)/shard_map/ppermute | solution.py:21
  310.5 5.2 %collective-permute-start.51 = (f32[1,16,128]{2,1,0:T(8,128)S(1)}, f32[1,16,128]{2,1,0:T(8,128)S(1)}, u32[]{:S(2)}, u32[]{:S(2)}) collective-permute-start(f32[1,16,128]{2,1,0:T(8,128)S(1)} %get-tuple-element.44), channel_id=1, source_target_pairs={{0,8},{8,16},{16,24},{1,9},{9,17},{17,25},{2,10},{10,18},{18,26},{... | collective-permute-start | bytes 24584 | tf_op jit(solution)/shard_map/ppermute | solution.py:18
  314.4 5.5 %collective-permute-start.52 = (f32[1,16,128]{2,1,0:T(8,128)S(1)}, f32[1,16,128]{2,1,0:T(8,128)S(1)}, u32[]{:S(2)}, u32[]{:S(2)}) collective-permute-start(f32[1,16,128]{2,1,0:T(8,128)S(1)} %get-tuple-element.45), channel_id=1, source_target_pairs={{8,0},{16,8},{24,16},{9,1},{17,9},{25,17},{10,2},{18,10},{26,18},{... | collective-permute-start | bytes 24584 | tf_op jit(solution)/shard_map/ppermute | solution.py:21
  320.0 5.9 %collective-permute-start.53 = (f32[10,1,128]{2,1,0:T(1,128)S(1)}, f32[10,1,128]{2,1,0:T(1,128)S(1)}, u32[]{:S(2)}, u32[]{:S(2)}) collective-permute-start(f32[10,1,128]{2,1,0:T(1,128)S(1)} %get-tuple-element.38), channel_id=1, source_target_pairs={{0,2},{2,4},{4,6},{1,3},{3,5},{5,7},{8,10},{10,12},{12,14},{9,11},... | collective-permute-start | bytes 15368 | tf_op jit(solution)/shard_map/ppermute | solution.py:18
  324.5 5.5 %collective-permute-start.54 = (f32[10,1,128]{2,1,0:T(1,128)S(1)}, f32[10,1,128]{2,1,0:T(1,128)S(1)}, u32[]{:S(2)}, u32[]{:S(2)}) collective-permute-start(f32[10,1,128]{2,1,0:T(1,128)S(1)} %get-tuple-element.39), channel_id=1, source_target_pairs={{2,0},{4,2},{6,4},{3,1},{5,3},{7,5},{10,8},{12,10},{14,12},{11,9},... | collective-permute-start | bytes 15368 | tf_op jit(solution)/shard_map/ppermute | solution.py:21
  (29 other events, 113.9 us)
where the time goes:
time: 338 us; the launch traced here: 335 us
  starting transfers between devices  112 us (33%)
  waiting for transfers between devices  82.6 us (24%)
  local copies, waits for them, and re-layouts  55.4 us (16%)
  blocking collectives  38.1 us (11%)
  other arithmetic  31.3 us (9%)
  between operations  16.5 us (5%)
    ppermute x27, waiting for transfers between devices, extended(): lax.ppermute(lax.slice_in_dim(block, 0, width, axis=dim), axis, backward)  81.9 us
    ppermute x27, starting transfers between devices, extended(): lax.ppermute(lax.slice_in_dim(block, block.shape[dim] - width, None, axis...  72.6 us
    reshape x8, local copies, waits for them, and re-layouts, blocked(): values.reshape(values.shape[0] // 2, 2, values.shape[1] // 2, 2, values.s...  39.8 us
    all_gather x1, blocking collectives, coarse_solve(): whole = lax.all_gather(stacked, ('gx', 'gy', 'gz'), axis=0, tiled=True)  38.1 us
    ppermute x27, starting transfers between devices, extended(): lax.ppermute(lax.slice_in_dim(block, 0, width, axis=dim), axis, backward)  35.1 us
    reduce_sum x22, other arithmetic, coarse_face(): summed = jnp.sum(blocked(values), axis=others)  18 us
  transfers between devices with their start and end apart: 57, of which 26 were waited for; matrix products, arithmetic and copies ran while one was open for 17% of the time, Pallas kernels for 0%

commit v1 on v0

--- a/solution.py
+++ b/solution.py
@@ -1,6 +1,10 @@
+import functools
+
 import jax
 import jax.numpy as jnp
 from jax import lax
+from jax.experimental import pallas as pl
+from jax.experimental.pallas import tpu as pltpu
 from jax.sharding import PartitionSpec as P
 
 LEVELS = 4
@@ -8,6 +12,358 @@
 
 
 damping = 2.0 / 3.0
+
+REACH = 3
+TILE = 8
+
+
+def up(v, axis):
+    return pltpu.roll(v, v.shape[axis] - 1, axis)
+
+
+def down(v, axis):
+    return pltpu.roll(v, 1, axis)
+
+
+def iota(shape, axis):
+    return lax.broadcasted_iota(jnp.int32, shape, axis)
+
+
+def chosen(mask):
+    return jnp.where(mask, 1.0, 0.0).astype(jnp.bfloat16)
+
+
+def select_dot(values, matrix):
+    high = values.astype(jnp.bfloat16)
+    rest = values - high.astype(jnp.float32)
+    mid = rest.astype(jnp.bfloat16)
+    low = (rest - mid.astype(jnp.float32)).astype(jnp.bfloat16)
+    dot = functools.partial(jnp.dot, preferred_element_type=jnp.float32)
+    return (dot(low, matrix) + dot(mid, matrix)) + dot(high, matrix)
+
+
+def inverse(diagonal):
+    return jnp.where(diagonal > 0.0, damping / jnp.where(diagonal > 0.0, diagonal, 1.0), 0.0)
+
+
+def fine_kernel(own, side_x, side_y, t_out, k_out, m_out, ext, e1, rd, dg, e2, rows):
+    nx, ny = own.shape[2], own.shape[3]
+    nz = 2 * own.shape[4]
+    half = own.shape[4]
+    gx, gy, gz = lax.axis_index("gx"), lax.axis_index("gy"), lax.axis_index("gz")
+    for h in range(2):
+        z = slice(h * half, (h + 1) * half)
+        for a in range(4):
+            ext[a, REACH : REACH + nx, TILE : TILE + ny, z] = own[h, a]
+            ext[a, :REACH, TILE : TILE + ny, z] = side_x[0, h, a]
+            ext[a, REACH + nx :, TILE : TILE + ny, z] = side_x[1, h, a]
+            ext[a, :, :TILE, z] = side_y[0, h, a]
+            ext[a, :, TILE + ny :, z] = side_y[1, h, a]
+    shape = (ny + 2 * TILE, nz)
+    row, lane = iota(shape, 0), iota(shape, 1)
+    inner_z = lane > 0
+    in_y = jnp.logical_and(
+        jnp.logical_or(gy > 0, row >= TILE),
+        jnp.logical_or(gy < lax.axis_size("gy") - 1, row < TILE + ny),
+    )
+
+    def off(e, p):
+        fy, fz = ext[2, p], jnp.where(inner_z, ext[3, p], 0.0)
+        here = e[p]
+        total = ext[1, p] * e[p - 1] + ext[1, p + 1] * e[p + 1]
+        total = total + fy * down(here, 0) + up(fy * here, 0)
+        return total + fz * down(here, 1) + up(fz * here, 1)
+
+    for p in range(1, nx + 2 * REACH - 1):
+        fy, fz = ext[2, p], ext[3, p]
+        diagonal = ext[1, p] + ext[1, p + 1] + fy + up(fy, 0) + fz + up(jnp.where(inner_z, fz, 0.0), 1)
+        inv = inverse(diagonal)
+        dg[p], rd[p] = diagonal, inv
+        e1[p] = ext[0, p] * inv
+    for p in range(2, nx + 2 * REACH - 2):
+        value = (2.0 - damping) * e1[p] + rd[p] * off(e1, p)
+        inside = in_y
+        if p < REACH:
+            inside = jnp.logical_and(inside, gx > 0)
+        if p >= REACH + nx:
+            inside = jnp.logical_and(inside, gx < lax.axis_size("gx") - 1)
+        e2[p] = jnp.where(inside, value, 0.0)
+
+    def mine(v):
+        v = v[TILE : TILE + ny]
+        return jnp.where(gz == 0, v[:, :half], v[:, half:])
+
+    sums = []
+    for i in range(nx):
+        p = REACH + i
+        q = ext[0, p] - dg[p] * e2[p] + off(e2, p)
+        fy, fz = ext[2, p], jnp.where(inner_z, ext[3, p], 0.0)
+        inv = rd[p]
+        t_out[i] = mine(e2[p] + inv * q)
+        for n, k in enumerate((ext[1, p], ext[1, p + 1], fy, up(fy, 0), fz, up(fz, 1))):
+            k_out[n, i] = mine(inv * k)
+        sums.append(q[TILE : TILE + ny])
+    inner = slice(TILE, TILE + ny)
+    pairs = range(0, nx, 2)
+    wide = [sums[i] + sums[i + 1] for i in pairs]
+    wide += [0.5 * ext[1, REACH + i, inner] for i in pairs]
+    wide += [0.5 * (ext[2, REACH + i, inner] + ext[2, REACH + i + 1, inner]) for i in pairs]
+    thin = [0.5 * (ext[3, REACH + i, inner] + ext[3, REACH + i + 1, inner]) for i in pairs]
+    fine, coarse = iota((nz, half), 0), iota((nz, half), 1)
+    summed = select_dot(jnp.concatenate(wide, 0), chosen(fine // 2 == coarse))
+    picked = select_dot(jnp.concatenate(thin, 0), chosen(fine == 2 * coarse))
+    count = len(pairs) * ny
+    rows[: 3 * count] = summed
+    rows[3 * count :] = picked
+    part = count // 2
+    even = rows[pl.ds(0, 4 * part, stride=2)]
+    odd = rows[pl.ds(1, 4 * part, stride=2)]
+    kept = [even[:part] + odd[:part], even[part : 2 * part] + odd[part : 2 * part]]
+    kept += [even[2 * part : 3 * part], even[3 * part :] + odd[3 * part :]]
+    for a in range(2):
+        m_out[a] = jnp.where(gz == 0, kept[a], kept[2 + a]).reshape(m_out.shape[1:])
+
+
+def planes_of(ref):
+    return [ref[p] for p in range(ref.shape[0])]
+
+
+def level_parts(fx, fy, fz):
+    shape = fy[0].shape
+    row, lane = iota(shape, 0), iota(shape, 1)
+    n = len(fx)
+    zero = jnp.zeros(shape, jnp.float32)
+    fym = [jnp.where(row > 0, v, 0.0) for v in fy]
+    fzm = [jnp.where(lane > 0, v, 0.0) for v in fz]
+    high = [fx[p + 1] if p + 1 < n else zero for p in range(n)]
+    diagonal = [fx[p] + high[p] + fy[p] + up(fym[p], 0) + fz[p] + up(fzm[p], 1) for p in range(n)]
+
+    def off(e):
+        result = []
+        for p in range(n):
+            total = fym[p] * down(e[p], 0) + up(fym[p] * e[p], 0)
+            total = total + fzm[p] * down(e[p], 1) + up(fzm[p] * e[p], 1)
+            if p > 0:
+                total = total + fx[p] * e[p - 1]
+            if p + 1 < n:
+                total = total + fx[p + 1] * e[p + 1]
+            result.append(total)
+        return result
+
+    return diagonal, [inverse(d) for d in diagonal], off
+
+
+def before(b, diagonal, inv, off):
+    e1 = [v * r for v, r in zip(b, inv)]
+    e2 = [(2.0 - damping) * e + r * o for e, r, o in zip(e1, inv, off(e1))]
+    q = [v - d * e + o for v, d, e, o in zip(b, diagonal, e2, off(e2))]
+    return [e + r * v for e, r, v in zip(e2, inv, q)], q
+
+
+def after(t, c, inv, off):
+    return [v + (1.0 - damping) * k + r * o for v, k, r, o in zip(t, c, inv, off(c))]
+
+
+def coarse_solution(rhs, fx, fy, fz, depth):
+    shape = rhs.shape
+    row, lane = iota(shape, 0), iota(shape, 1)
+    fxm = jnp.where(lane >= depth, fx, 0.0)
+    fym = jnp.where(row > 0, fy, 0.0)
+    fzm = jnp.where(lane % depth > 0, fz, 0.0)
+    wide = shape[1]
+
+    def up_x(v):
+        return pltpu.roll(v, wide - depth, 1)
+
+    hx, hy, hz = up_x(fxm), up(fym, 0), up(fzm, 1)
+    diagonal = fx + hx + fy + hy + fz + hz
+
+    def operate_packed(v):
+        result = diagonal * v - fxm * pltpu.roll(v, depth, 1) - hx * up_x(v)
+        result = result - fym * down(v, 0) - hy * up(v, 0)
+        return result - fzm * down(v, 1) - hz * up(v, 1)
+
+    def total(v):
+        return jnp.sum(jnp.sum(v, axis=0, keepdims=True), axis=1, keepdims=True)
+
+    solution = jnp.zeros_like(rhs)
+    remain = rhs
+    search = rhs
+    norm_now = total(remain * remain)
+    for step in range(COARSE_ITERS):
+        image = operate_packed(search)
+        alpha = norm_now / total(search * image)
+        solution = solution + alpha * search
+        if step + 1 < COARSE_ITERS:
+            remain = remain - alpha * image
+            norm_next = total(remain * remain)
+            search = remain + norm_next / norm_now * search
+            norm_now = norm_next
+    return solution
+
+
+def whole_kernel(here, there, t_in, k_in, out, grid, fold1, fold2, spread2, window, doubled):
+    gx, gy, gz = lax.axis_index("gx"), lax.axis_index("gy"), lax.axis_index("gz")
+    cx, cy = lax.axis_size("gx"), lax.axis_size("gy")
+    bx, by = here.shape[2], here.shape[3]
+    for k in range(cx * cy):
+        x = jnp.bitwise_xor(gx, k % cx) * bx
+        y = pl.multiple_of(jnp.bitwise_xor(gy, k // cx) * by, by)
+        for a in range(2):
+            grid[2 * gz + a, pl.ds(x, bx), pl.ds(y, by), :] = here[k, a]
+            grid[2 * (1 - gz) + a, pl.ds(x, bx), pl.ds(y, by), :] = there[k, a]
+    n1, m1, w1 = grid.shape[1:]
+    b1, fx1, fy1, fz1 = (planes_of(grid.at[a]) for a in range(4))
+    diagonal1, inv1, off1 = level_parts(fx1, fy1, fz1)
+    t1, q1 = before(b1, diagonal1, inv1, off1)
+
+    n2, m2 = n1 // 2, m1 // 2
+    fine, coarse = iota((w1, w1), 0), iota((w1, w1), 1)
+    both, even = chosen(fine // 2 == coarse), chosen(fine == 2 * coarse)
+    pairs = range(0, n1, 2)
+    wide = [q1[i] + q1[i + 1] for i in pairs] + [0.5 * fx1[i] for i in pairs]
+    wide += [0.5 * (fy1[i] + fy1[i + 1]) for i in pairs]
+    thin = [0.5 * (fz1[i] + fz1[i + 1]) for i in pairs]
+    count = n2 * m1
+    fold1[: 3 * count] = select_dot(jnp.concatenate(wide, 0), both)
+    fold1[3 * count :] = select_dot(jnp.concatenate(thin, 0), even)
+    half = n2 * m2
+    low = fold1[pl.ds(0, 4 * half, stride=2)]
+    top = fold1[pl.ds(1, 4 * half, stride=2)]
+
+    def part(v):
+        return [v[p * m2 : (p + 1) * m2] for p in range(n2)]
+
+    b2 = part(low[:half] + top[:half])
+    fx2 = part(low[half : 2 * half] + top[half : 2 * half])
+    fy2 = part(low[2 * half : 3 * half])
+    fz2 = part(low[3 * half :] + top[3 * half :])
+    diagonal2, inv2, off2 = level_parts(fx2, fy2, fz2)
+    t2, q2 = before(b2, diagonal2, inv2, off2)
+
+    n3, m3 = n2 // 2, m2 // 2
+    depth = w1 // n3
+    packed = [0.0, 0.0, 0.0, 0.0]
+    for i in range(n3):
+        both = chosen((fine // 2 + i * depth == coarse) & (fine < 2 * depth))
+        even = chosen((fine + 2 * i * depth == 2 * coarse) & (fine < 2 * depth))
+        wide = [q2[2 * i] + q2[2 * i + 1], 0.5 * fx2[2 * i], 0.5 * (fy2[2 * i] + fy2[2 * i + 1])]
+        thin = 0.5 * (fz2[2 * i] + fz2[2 * i + 1])
+        summed = select_dot(jnp.concatenate(wide, 0), both)
+        packed[0] = packed[0] + summed[:m2]
+        packed[1] = packed[1] + summed[m2 : 2 * m2]
+        packed[2] = packed[2] + summed[2 * m2 :]
+        packed[3] = packed[3] + select_dot(thin, even)
+    fold2[...] = jnp.concatenate(packed, 0)
+    low = fold2[pl.ds(0, 4 * m3, stride=2)]
+    top = fold2[pl.ds(1, 4 * m3, stride=2)]
+    b3, fx3 = low[:m3] + top[:m3], low[m3 : 2 * m3] + top[m3 : 2 * m3]
+    fy3, fz3 = low[2 * m3 : 3 * m3], low[3 * m3 :] + top[3 * m3 :]
+    c3 = coarse_solution(b3, fx3, fy3, fz3, depth)
+
+    for i in range(n3):
+        row = select_dot(c3, chosen((coarse // 2 + i * depth == fine) & (coarse < 2 * depth)))
+        spread2[pl.ds(i * m2, m3, stride=2)] = row
+        spread2[pl.ds(i * m2 + 1, m3, stride=2)] = row
+    up2 = [spread2[(p // 2) * m2 : (p // 2 + 1) * m2] for p in range(n2)]
+    c2 = after(t2, up2, inv2, off2)
+
+    row = select_dot(jnp.concatenate(c2, 0), chosen(coarse // 2 == fine))
+    fold1[pl.ds(0, half, stride=2)] = row
+    fold1[pl.ds(1, half, stride=2)] = row
+    up1 = [fold1[(p // 2) * m1 : (p // 2 + 1) * m1] for p in range(n1)]
+    c1 = after(t1, up1, inv1, off1)
+
+    window[...] = jnp.zeros_like(window)
+    for p in range(n1):
+        window[1 + p, TILE : TILE + m1, :] = c1[p]
+    y = pl.multiple_of(gy * by, by)
+    near = window[pl.ds(gx * bx, bx + 2), pl.ds(y, by + 2 * TILE), :]
+    tall = by + 2 * TILE
+    near = near.reshape((bx + 2) * tall, w1)
+    spot = gz * t_in.shape[2] + iota((w1, 3 * w1), 1) % w1 + (iota((w1, 3 * w1), 1) // w1 + 1) % 3 - 1
+    wanted = iota((w1, 3 * w1), 0)
+    row = select_dot(near, chosen((2 * wanted == spot) | (2 * wanted + 1 == spot)))
+    for s in range(3):
+        doubled[s, pl.ds(0, (bx + 2) * tall, stride=2)] = row[:, s * w1 : (s + 1) * w1]
+        doubled[s, pl.ds(1, (bx + 2) * tall, stride=2)] = row[:, s * w1 : (s + 1) * w1]
+    ny = t_in.shape[1]
+
+    def at(s, i, shift):
+        first = (1 + i // 2) * 2 * tall + 2 * TILE + shift
+        return doubled[s, first : first + ny]
+
+    for i in range(t_in.shape[0]):
+        value = t_in[i] + (1.0 - damping) * at(0, i, 0)
+        value = value + k_in[0, i] * at(0, i - 1, 0) + k_in[1, i] * at(0, i + 1, 0)
+        value = value + k_in[2, i] * at(0, i, -1) + k_in[3, i] * at(0, i, 1)
+        out[i] = value + k_in[4, i] * at(2, i, 0) + k_in[5, i] * at(1, i, 0)
+
+
+def halves(block, axis, dim, width, reach):
+    count, core = lax.axis_size(axis), lax.axis_index("gz")
+    start = core * (block.shape[dim] - width)
+    slab = lax.dynamic_slice_in_dim(block, start, width, dim)
+    route = []
+    for i in range(count - 1):
+        route += [(2 * i + 1, 2 * i + 2), (2 * i + 2, 2 * i + 1)]
+    taken = lax.ppermute(slab, (axis, "gz"), route)
+    return lax.all_gather(taken, "gz", axis=0)
+
+
+def doubled_over(block, axis):
+    count = lax.axis_size(axis)
+    step = 1
+    while step < count:
+        other = lax.ppermute(block, axis, [(i, i ^ step) for i in range(count)])
+        block = jnp.concatenate([block, other], 0)
+        step *= 2
+    return block
+
+
+def f32(*shape):
+    return jax.ShapeDtypeStruct(shape, jnp.float32)
+
+
+def per_device_small(adjoint_residual, face_x, face_y, face_z):
+    nx, ny, nz = adjoint_residual.shape
+    stacked = jnp.stack((adjoint_residual, face_x, face_y, face_z))
+    own = lax.all_gather(stacked, "gz", axis=0)
+    side_x = halves(own, "gx", 2, REACH, REACH)
+    tall = jnp.concatenate([side_x[0], own, side_x[1]], 2)
+    side_y = halves(tall, "gy", 3, TILE, REACH)
+    ext_x, ext_y, wide = nx + 2 * REACH, ny + 2 * TILE, 2 * nz
+    field = pltpu.VMEM((ext_x, ext_y, wide), jnp.float32)
+    t, k, m = pl.pallas_call(
+        fine_kernel,
+        out_shape=(f32(nx, ny, nz), f32(6, nx, ny, nz), f32(2, nx // 2, ny // 2, nz)),
+        scratch_shapes=[
+            pltpu.VMEM((4, ext_x, ext_y, wide), jnp.float32),
+            field,
+            field,
+            field,
+            field,
+            pltpu.VMEM((2 * nx * ny, nz), jnp.float32),
+        ],
+        name="fine",
+    )(own, side_x, side_y)
+    here = doubled_over(doubled_over(m[None], "gx"), "gy")
+    there = lax.ppermute(here, "gz", [(0, 1), (1, 0)])
+    n1, m1 = here.shape[2] * lax.axis_size("gx"), here.shape[3] * lax.axis_size("gy")
+    tall = (nx // 2 + 2) * (ny // 2 + 2 * TILE)
+    return pl.pallas_call(
+        whole_kernel,
+        out_shape=f32(nx, ny, nz),
+        scratch_shapes=[
+            pltpu.VMEM((4, n1, m1, nz), jnp.float32),
+            pltpu.VMEM((2 * n1 * m1, nz), jnp.float32),
+            pltpu.VMEM((2 * m1, nz), jnp.float32),
+            pltpu.VMEM((n1 * m1 // 8, nz), jnp.float32),
+            pltpu.VMEM((n1 + 2, m1 + 2 * TILE, nz), jnp.float32),
+            pltpu.VMEM((3, 2 * tall, nz), jnp.float32),
+        ],
+        name="whole",
+    )(here, there, t, k)
 
 
 def extended(block, sides, width):
@@ -141,9 +497,23 @@
     return cycle(adjoint_residual, LEVELS, coefs)
 
 
+def fits(mesh, shape):
+    nx, ny, nz = shape
+    cx, cy, cz = mesh.shape["gx"], mesh.shape["gy"], mesh.shape["gz"]
+    powers = cx & (cx - 1) == 0 and cy & (cy - 1) == 0 and cz == 2
+    blocks = nx % (8 * cx) == 0 and ny % (16 * cy) == 0 and nz == 256
+    return powers and blocks and (nx // 8) * (nz // 8) == 128 and nx * ny * nz <= 2**19
+
+
+def per_block(mesh, *args):
+    counts = (mesh.shape["gx"], mesh.shape["gy"], mesh.shape["gz"])
+    whole = tuple(n * c for n, c in zip(args[0].shape, counts))
+    return (per_device_small if fits(mesh, whole) else per_device)(*args)
+
+
 def solution(mesh):
     return jax.shard_map(
-        per_device,
+        functools.partial(per_block, mesh),
         mesh=mesh,
         in_specs=(
             P("gx", "gy", "gz"),

time: 338 us -> 65.3 us (0.19)
  starting transfers between devices: 112 us -> 10.5 us
  waiting for transfers between devices: 82.6 us -> 14.4 us
  local copies, waits for them, and re-layouts: 55.4 us -> 1.63 us
  other arithmetic: 31.3 us -> 1.77 us
  between operations: 16.5 us -> 0.1 us
  blocking collectives: 38.1 us -> 27.6 us
  Pallas kernels: 0 us -> 8.96 us
    ppermute x57 -> x7, starting transfers between devices: 112 us -> 10.5 us  [the longest x4 9.07 us: doubled_over(): other = lax.ppermute(block, axis, [(i, i ^ step) for i in range(count)])]
    ppermute x57 -> x7, waiting for transfers between devices: 82.6 us -> 14.4 us  [the longest x4 12.5 us: doubled_over(): other = lax.ppermute(block, axis, [(i, i ^ step) for i in range(count)])]
    reshape x10 -> x0, local copies, waits for them, and re-layouts: 44.1 us -> none  [the longest x8 39.8 us: blocked(): values.reshape(values.shape[0] // 2, 2, values.shape[1] // 2, 2, values.s...]
    reduce_sum x38 -> x0, other arithmetic: 29.1 us -> none  [the longest x22 18 us: coarse_face(): summed = jnp.sum(blocked(values), axis=others)]
    all_gather x1 -> x3, blocking collectives: 38.1 us -> 27.6 us  [the longest x2 25.3 us: halves(): return lax.all_gather(taken, 'gz', axis=0)]
    pallas_call x0 -> x2, Pallas kernels: none -> 8.96 us  [the longest x1 6.03 us: per_device_small(): pl.pallas_call(whole_kernel, out_shape=f32(nx, ny, nz), scratch_shapes=[p...]
  transfers between devices with their start and end apart: 57 -> 7, of which waited for: 26 -> 5; matrix products, arithmetic and copies ran while one was open for 17% -> 0% of each run, Pallas kernels for 0% -> 0%
where the time goes in v1:
time: 65.3 us; the launch traced here: 65 us
  blocking collectives  27.6 us (42%)
  waiting for transfers between devices  14.4 us (22%)
  starting transfers between devices  10.5 us (16%)
  Pallas kernels  8.96 us (14%)
  other arithmetic  1.77 us (3%)
  local copies, waits for them, and re-layouts  1.63 us (2%)
    all_gather x2, blocking collectives, halves(): return lax.all_gather(taken, 'gz', axis=0)  25.3 us
    ppermute x4, waiting for transfers between devices, doubled_over(): other = lax.ppermute(block, axis, [(i, i ^ step) for i in range(count)])  12.5 us
    ppermute x4, starting transfers between devices, doubled_over(): other = lax.ppermute(block, axis, [(i, i ^ step) for i in range(count)])  9.07 us
    pallas_call x1, Pallas kernels, per_device_small(): pl.pallas_call(whole_kernel, out_shape=f32(nx, ny, nz), scratch_shapes=[p...  6.03 us
    pallas_call x1, Pallas kernels, per_device_small(): pl.pallas_call(fine_kernel, out_shape=(f32(nx, ny, nz), f32(6, nx, ny, nz...  2.93 us
    all_gather x1, blocking collectives, per_device_small(): own = lax.all_gather(stacked, 'gz', axis=0)  2.3 us
    ppermute x1, waiting for transfers between devices, per_device_small(): there = lax.ppermute(here, 'gz', [(0, 1), (1, 0)])  1.9 us
    unnamed x14, local copies, waits for them, and re-layouts  1.57 us
  transfers between devices with their start and end apart: 7, of which 5 were waited for; matrix products, arithmetic and copies ran while one was open for 0% of the time, Pallas kernels for 0%

profile of v1, /device:TPU:0, one launch (start us, length us, event | category | flops | bytes accessed | tf_op | source)
XLA Modules:
  0.0 65.0 jit_solution(11017025783509709884)
XLA Ops:
  0.0 1.0 %pad_maximum_fusion = f32[4,8,16,128]{3,2,1,0:T(8,128)S(1)} fusion(f32[1,8,16,128]{3,2,1,0:T(8,128)} %bitcast.18, f32[1,8,16,128]{3,2,1,0:T(8,128)} %bitcast.19, f32[1,8,16,128]{3,2,1,0:T(8,128)} %bitcast.20, f32[1,8,16,128]{3,2,1,0:T(8,128)} %bitcast.21), kind=kLoop, calls=%fused_computation.5 | loop fusion | flops 196608 | bytes 524288 | tf_op jit(solution)/shard_map/stack | solution.py:330
  1.0 2.3 %all-gather = f32[8,8,16,128]{3,2,1,0:T(8,128)S(1)} all-gather(f32[4,8,16,128]{3,2,1,0:T(8,128)S(1)} %pad_maximum_fusion), channel_id=2, replica_groups=mesh['gx'=4,'gy'=4,'gz'=2] {'gz'}, dimensions={0}, use_global_device_ids=true | all-gather | bytes 786432 | tf_op jit(solution)/shard_map/all_gather | solution.py:331
  3.3 0.0 copy-start
  3.3 0.7 %collective-permute-start = (f32[2,4,3,16,128]{4,3,2,1,0:T(8,128)S(1)}, f32[2,4,3,16,128]{4,3,2,1,0:T(8,128)S(1)}, u32[]{:S(2)}, u32[]{:S(2)}) collective-permute-start(f32[2,4,3,16,128]{4,3,2,1,0:T(8,128)S(1)} %constant_dynamic-slice_fusion), channel_id=1, source_target_pairs={{1,8},{8,1},{9,16},{16,9},{17,24},{24,17},{3,10},{10,3},{11,18},{1... | collective-permute-start | bytes 589832 | tf_op jit(solution)/shard_map/ppermute | solution.py:310
  4.0 0.0 collective-permute-done
  4.0 9.3 %all-gather.1 = f32[4,4,3,16,128]{4,3,2,1,0:T(8,128)S(1)} all-gather(f32[2,4,3,16,128]{4,3,2,1,0:T(8,128)S(1)} %collective-permute-done), channel_id=3, replica_groups=mesh['gx'=4,'gy'=4,'gz'=2] {'gz'}, dimensions={0}, use_global_device_ids=true | all-gather | bytes 589824 | tf_op jit(solution)/shard_map/all_gather | solution.py:311
  13.3 0.0 copy-start.1
  13.3 0.7 %copy-done.1 = f32[4,4,3,16,128]{4,3,2,1,0:T(8,128)} copy-done((f32[4,4,3,16,128]{4,3,2,1,0:T(8,128)}, f32[4,4,3,16,128]{4,3,2,1,0:T(8,128)S(1)}, u32[]{:S(2)}) %copy-start.1) | copy-done | bytes 393240
  14.1 0.0 copy-done
  14.1 0.7 %collective-permute-start.1 = (f32[2,4,14,8,128]{4,3,2,1,0:T(8,128)S(1)}, f32[2,4,14,8,128]{4,3,2,1,0:T(8,128)S(1)}, u32[]{:S(2)}, u32[]{:S(2)}) collective-permute-start(f32[2,4,14,8,128]{4,3,2,1,0:T(8,128)S(1)} %fusion.1), channel_id=1, source_target_pairs={{1,2},{2,1},{3,4},{4,3},{5,6},{6,5},{9,10},{10,9},{11,12},{12,11},... | collective-permute-start | bytes 1376264 | tf_op jit(solution)/shard_map/ppermute | solution.py:310
  14.8 0.0 collective-permute-done.1
  14.8 16.0 %all-gather.2 = f32[4,4,14,8,128]{4,3,2,1,0:T(8,128)} all-gather(f32[2,4,14,8,128]{4,3,2,1,0:T(8,128)S(1)} %collective-permute-done.1), channel_id=4, replica_groups=mesh['gx'=4,'gy'=4,'gz'=2] {'gz'}, dimensions={0}, use_global_device_ids=true | all-gather | bytes 1376256 | tf_op jit(solution)/shard_map/all_gather | solution.py:311
  30.8 2.9 %fine.1 = (f32[8,16,128]{2,1,0:T(8,128)}, f32[6,8,16,128]{3,2,1,0:T(8,128)}, f32[2,4,8,128]{3,2,1,0:T(8,128)}) custom-call(f32[2,4,8,16,128]{4,3,2,1,0:T(8,128)} %bitcast.11, f32[2,2,4,3,16,128]{5,4,3,2,1,0:T(8,128)} %bitcast.13, f32[2,2,4,14,8,128]{5,4,3,2,1,0:T(8,128)} %bitcast.12), custom_call_target="tpu_custom_call" | custom-call | tf_op jit(solution)/shard_map/fine/pallas_call | solution.py:337
  33.7 0.0 copy-start.4
  33.7 1.7 %collective-permute-start.2 = (f32[1,2,4,8,128]{4,3,2,1,0:T(8,128)}, f32[1,2,4,8,128]{4,3,2,1,0:T(8,128)S(1)}, u32[]{:S(2)}, u32[]{:S(2)}) collective-permute-start(f32[1,2,4,8,128]{4,3,2,1,0:T(8,128)} %bitcast.14), channel_id=1, source_target_pairs={{0,8},{8,0},{16,24},{24,16},{1,9},{9,1},{17,25},{25,17},{2,10},{10... | collective-permute-start | bytes 98312 | tf_op jit(solution)/shard_map/ppermute | solution.py:318
  35.4 2.4 %collective-permute-done.2 = f32[1,2,4,8,128]{4,3,2,1,0:T(8,128)S(1)} collective-permute-done((f32[1,2,4,8,128]{4,3,2,1,0:T(8,128)}, f32[1,2,4,8,128]{4,3,2,1,0:T(8,128)S(1)}, u32[]{:S(2)}, u32[]{:S(2)}) %collective-permute-start.2) | collective-permute-done | bytes 32800 | tf_op jit(solution)/shard_map/ppermute | solution.py:318
  37.9 0.8 %pad_maximum_fusion.3 = f32[2,2,4,8,128]{4,3,2,1,0:T(8,128)S(1)} fusion(f32[1,2,4,8,128]{4,3,2,1,0:T(8,128)S(1)} %collective-permute-done.2, f32[1,2,4,8,128]{4,3,2,1,0:T(8,128)} %bitcast.15), kind=kLoop, calls=%fused_computation.8 | loop fusion | flops 16384 | bytes 131072 | tf_op jit(solution)/shard_map/concatenate | solution.py:319
  38.6 2.7 %collective-permute-start.3 = (f32[2,2,4,8,128]{4,3,2,1,0:T(8,128)S(1)}, f32[2,2,4,8,128]{4,3,2,1,0:T(8,128)S(1)}, u32[]{:S(2)}, u32[]{:S(2)}) collective-permute-start(f32[2,2,4,8,128]{4,3,2,1,0:T(8,128)S(1)} %pad_maximum_fusion.3), channel_id=1, source_target_pairs={{0,16},{8,24},{16,0},{24,8},{1,17},{9,25},{17,1},{25,9},{2,18},{10... | collective-permute-start | bytes 196616 | tf_op jit(solution)/shard_map/ppermute | solution.py:318
  41.3 2.5 %collective-permute-done.3 = f32[2,2,4,8,128]{4,3,2,1,0:T(8,128)S(1)} collective-permute-done((f32[2,2,4,8,128]{4,3,2,1,0:T(8,128)S(1)}, f32[2,2,4,8,128]{4,3,2,1,0:T(8,128)S(1)}, u32[]{:S(2)}, u32[]{:S(2)}) %collective-permute-start.3) | collective-permute-done | bytes 65568 | tf_op jit(solution)/shard_map/ppermute | solution.py:318
  43.9 0.0 copy-done.4
  43.9 2.8 %collective-permute-start.4 = (f32[4,2,4,8,128]{4,3,2,1,0:T(8,128)S(1)}, f32[4,2,4,8,128]{4,3,2,1,0:T(8,128)S(1)}, u32[]{:S(2)}, u32[]{:S(2)}) collective-permute-start(f32[4,2,4,8,128]{4,3,2,1,0:T(8,128)S(1)} %pad_maximum_fusion.2), channel_id=1, source_target_pairs={{0,2},{2,0},{4,6},{6,4},{1,3},{3,1},{5,7},{7,5},{8,10},{10,8},{12,... | collective-permute-start | bytes 393224 | tf_op jit(solution)/shard_map/ppermute | solution.py:318
  46.8 2.9 %collective-permute-done.4 = f32[4,2,4,8,128]{4,3,2,1,0:T(8,128)S(1)} collective-permute-done((f32[4,2,4,8,128]{4,3,2,1,0:T(8,128)S(1)}, f32[4,2,4,8,128]{4,3,2,1,0:T(8,128)S(1)}, u32[]{:S(2)}, u32[]{:S(2)}) %collective-permute-start.4) | collective-permute-done | bytes 131104 | tf_op jit(solution)/shard_map/ppermute | solution.py:318
  49.7 1.8 %collective-permute-start.5 = (f32[8,2,4,8,128]{4,3,2,1,0:T(8,128)S(1)}, f32[8,2,4,8,128]{4,3,2,1,0:T(8,128)S(1)}, u32[]{:S(2)}, u32[]{:S(2)}) collective-permute-start(f32[8,2,4,8,128]{4,3,2,1,0:T(8,128)S(1)} %pad_maximum_fusion.1), channel_id=1, source_target_pairs={{0,4},{2,6},{4,0},{6,2},{1,5},{3,7},{5,1},{7,3},{8,12},{10,14},{12... | collective-permute-start | bytes 786440 | tf_op jit(solution)/shard_map/ppermute | solution.py:318
  51.6 4.6 %collective-permute-done.5 = f32[8,2,4,8,128]{4,3,2,1,0:T(8,128)S(1)} collective-permute-done((f32[8,2,4,8,128]{4,3,2,1,0:T(8,128)S(1)}, f32[8,2,4,8,128]{4,3,2,1,0:T(8,128)S(1)}, u32[]{:S(2)}, u32[]{:S(2)}) %collective-permute-start.5) | collective-permute-done | bytes 262176 | tf_op jit(solution)/shard_map/ppermute | solution.py:318
  56.2 0.0 copy-start.2
  56.2 0.1 collective-permute-start.6
  56.3 1.9 %collective-permute-done.6.there = f32[16,2,4,8,128]{4,3,2,1,0:T(8,128)S(1)} collective-permute-done((f32[16,2,4,8,128]{4,3,2,1,0:T(8,128)S(1)}, f32[16,2,4,8,128]{4,3,2,1,0:T(8,128)S(1)}, u32[]{:S(2)}, u32[]{:S(2)}) %collective-permute-start.6) | collective-permute-done | bytes 524320 | tf_op jit(solution)/shard_map/ppermute | solution.py:351
  58.2 0.0 copy-start.3
  58.2 0.0 copy-done.2
  58.2 0.8 %copy-done.3 = f32[16,2,4,8,128]{4,3,2,1,0:T(8,128)} copy-done((f32[16,2,4,8,128]{4,3,2,1,0:T(8,128)}, f32[16,2,4,8,128]{4,3,2,1,0:T(8,128)S(1)}, u32[]{:S(2)}) %copy-start.3) | copy-done | bytes 524312
  59.0 6.0 %whole.1 = f32[8,16,128]{2,1,0:T(8,128)} custom-call(f32[16,2,4,8,128]{4,3,2,1,0:T(8,128)} %copy-done.2, f32[16,2,4,8,128]{4,3,2,1,0:T(8,128)} %copy-done.3, f32[8,16,128]{2,1,0:T(8,128)} %get-tuple-element.9.t_in, f32[6,8,16,128]{3,2,1,0:T(8,128)} %get-tuple-element.10.k_in), custom_call_target="tpu_custom_call" | custom-call | tf_op jit(solution)/shard_map/whole/pallas_call | solution.py:354
  (10 shorter events, 0.1 us)
Async XLA Ops:
  3.3 10.8 %copy-start = (f32[8,8,16,128]{3,2,1,0:T(8,128)}, f32[8,8,16,128]{3,2,1,0:T(8,128)S(1)}, u32[]{:S(2)}) copy-start(f32[8,8,16,128]{3,2,1,0:T(8,128)S(1)} %all-gather) | copy-start | bytes 1572868
  3.3 0.7 %collective-permute-start = (f32[2,4,3,16,128]{4,3,2,1,0:T(8,128)S(1)}, f32[2,4,3,16,128]{4,3,2,1,0:T(8,128)S(1)}, u32[]{:S(2)}, u32[]{:S(2)}) collective-permute-start(f32[2,4,3,16,128]{4,3,2,1,0:T(8,128)S(1)} %constant_dynamic-slice_fusion), channel_id=1, source_target_pairs={{1,8},{8,1},{9,16},{16,9},{17,24},{24,17},{3,10},{10,3},{11,18},{1... | collective-permute-start | bytes 589832 | tf_op jit(solution)/shard_map/ppermute | solution.py:310
  13.3 0.8 %copy-start.1 = (f32[4,4,3,16,128]{4,3,2,1,0:T(8,128)}, f32[4,4,3,16,128]{4,3,2,1,0:T(8,128)S(1)}, u32[]{:S(2)}) copy-start(f32[4,4,3,16,128]{4,3,2,1,0:T(8,128)S(1)} %all-gather.1) | copy-start | bytes 1179652
  14.1 0.7 %collective-permute-start.1 = (f32[2,4,14,8,128]{4,3,2,1,0:T(8,128)S(1)}, f32[2,4,14,8,128]{4,3,2,1,0:T(8,128)S(1)}, u32[]{:S(2)}, u32[]{:S(2)}) collective-permute-start(f32[2,4,14,8,128]{4,3,2,1,0:T(8,128)S(1)} %fusion.1), channel_id=1, source_target_pairs={{1,2},{2,1},{3,4},{4,3},{5,6},{6,5},{9,10},{10,9},{11,12},{12,11},... | collective-permute-start | bytes 1376264 | tf_op jit(solution)/shard_map/ppermute | solution.py:310
  33.7 10.2 %copy-start.4 = (f32[2,4,8,128]{3,2,1,0:T(8,128)S(1)}, f32[2,4,8,128]{3,2,1,0:T(8,128)}, u32[]{:S(2)}) copy-start(f32[2,4,8,128]{3,2,1,0:T(8,128)} %get-tuple-element.8) | copy-start | bytes 98308
  33.7 4.1 %collective-permute-start.2 = (f32[1,2,4,8,128]{4,3,2,1,0:T(8,128)}, f32[1,2,4,8,128]{4,3,2,1,0:T(8,128)S(1)}, u32[]{:S(2)}, u32[]{:S(2)}) collective-permute-start(f32[1,2,4,8,128]{4,3,2,1,0:T(8,128)} %bitcast.14), channel_id=1, source_target_pairs={{0,8},{8,0},{16,24},{24,16},{1,9},{9,1},{17,25},{25,17},{2,10},{10... | collective-permute-start | bytes 98312 | tf_op jit(solution)/shard_map/ppermute | solution.py:318
  38.6 5.3 %collective-permute-start.3 = (f32[2,2,4,8,128]{4,3,2,1,0:T(8,128)S(1)}, f32[2,2,4,8,128]{4,3,2,1,0:T(8,128)S(1)}, u32[]{:S(2)}, u32[]{:S(2)}) collective-permute-start(f32[2,2,4,8,128]{4,3,2,1,0:T(8,128)S(1)} %pad_maximum_fusion.3), channel_id=1, source_target_pairs={{0,16},{8,24},{16,0},{24,8},{1,17},{9,25},{17,1},{25,9},{2,18},{10... | collective-permute-start | bytes 196616 | tf_op jit(solution)/shard_map/ppermute | solution.py:318
  43.9 5.8 %collective-permute-start.4 = (f32[4,2,4,8,128]{4,3,2,1,0:T(8,128)S(1)}, f32[4,2,4,8,128]{4,3,2,1,0:T(8,128)S(1)}, u32[]{:S(2)}, u32[]{:S(2)}) collective-permute-start(f32[4,2,4,8,128]{4,3,2,1,0:T(8,128)S(1)} %pad_maximum_fusion.2), channel_id=1, source_target_pairs={{0,2},{2,0},{4,6},{6,4},{1,3},{3,1},{5,7},{7,5},{8,10},{10,8},{12,... | collective-permute-start | bytes 393224 | tf_op jit(solution)/shard_map/ppermute | solution.py:318
  49.7 6.4 %collective-permute-start.5 = (f32[8,2,4,8,128]{4,3,2,1,0:T(8,128)S(1)}, f32[8,2,4,8,128]{4,3,2,1,0:T(8,128)S(1)}, u32[]{:S(2)}, u32[]{:S(2)}) collective-permute-start(f32[8,2,4,8,128]{4,3,2,1,0:T(8,128)S(1)} %pad_maximum_fusion.1), channel_id=1, source_target_pairs={{0,4},{2,6},{4,0},{6,2},{1,5},{3,7},{5,1},{7,3},{8,12},{10,14},{12... | collective-permute-start | bytes 786440 | tf_op jit(solution)/shard_map/ppermute | solution.py:318
  56.2 2.0 %copy-start.2 = (f32[16,2,4,8,128]{4,3,2,1,0:T(8,128)}, f32[16,2,4,8,128]{4,3,2,1,0:T(8,128)S(1)}, u32[]{:S(2)}) copy-start(f32[16,2,4,8,128]{4,3,2,1,0:T(8,128)S(1)} %constant_dynamic-update-slice_fusion.here) | copy-start | bytes 1572868
  56.2 2.0 %collective-permute-start.6 = (f32[16,2,4,8,128]{4,3,2,1,0:T(8,128)S(1)}, f32[16,2,4,8,128]{4,3,2,1,0:T(8,128)S(1)}, u32[]{:S(2)}, u32[]{:S(2)}) collective-permute-start(f32[16,2,4,8,128]{4,3,2,1,0:T(8,128)S(1)} %constant_dynamic-update-slice_fusion.here), channel_id=1, source_target_pairs={{0,1},{1,0},{2,3},{3,2},{4,5},{5,4},{6,7},{7,6},{8,9},{9,8},{10,11... | collective-permute-start | bytes 1572872 | tf_op jit(solution)/shard_map/ppermute | solution.py:351
  58.2 0.8 %copy-start.3 = (f32[16,2,4,8,128]{4,3,2,1,0:T(8,128)}, f32[16,2,4,8,128]{4,3,2,1,0:T(8,128)S(1)}, u32[]{:S(2)}) copy-start(f32[16,2,4,8,128]{4,3,2,1,0:T(8,128)S(1)} %collective-permute-done.6.there) | copy-start | bytes 1572868

commit v2 on v1

--- a/solution.py
+++ b/solution.py
@@ -46,19 +46,83 @@
     return jnp.where(diagonal > 0.0, damping / jnp.where(diagonal > 0.0, diagonal, 1.0), 0.0)
 
 
-def fine_kernel(own, side_x, side_y, t_out, k_out, m_out, ext, e1, rd, dg, e2, rows):
+def pack_kernel(own, x_out, y_out, c0_out, c1_out):
+    nx, ny = own.shape[2], own.shape[3]
+    gx, gy, gz = lax.axis_index("gx"), lax.axis_index("gy"), lax.axis_index("gz")
+
+    def start(kind):
+        return jnp.where((gx + kind) % 2 == 0, nx - 2, 0)
+
+    ahead = (gy + gz) % 2 == 0
+
+    def edge(h, a, i):
+        return jnp.where(ahead, own[h, a, i, ny - 2 :, :], own[h, a, i, :2, :])
+
+    for h in range(2):
+        for a in range(4):
+            for n in range(2):
+                x_out[h, 2 * a + n] = own[h, a, start(gz) + n]
+            for i in range(nx):
+                y_out[h, (a * nx + i) * 2 : (a * nx + i) * 2 + 2] = edge(h, a, i)
+            for n in range(2):
+                for kind, out in enumerate((c0_out, c1_out)):
+                    out[h, (2 * a + n) * 2 : (2 * a + n) * 2 + 2] = edge(h, a, start(kind) + n)
+        x_out[h, 8] = own[h, 1, 2]
+        for i in range(nx):
+            y_out[h, 8 * nx + i : 8 * nx + i + 1] = own[h, 2, i, 2:3, :]
+
+
+def fine_kernel(own, shared, t_out, k_out, m_out, ext, e1, rd, dg, e2, rows):
     nx, ny = own.shape[2], own.shape[3]
     nz = 2 * own.shape[4]
     half = own.shape[4]
     gx, gy, gz = lax.axis_index("gx"), lax.axis_index("gy"), lax.axis_index("gz")
+    first = {
+        "x": 0,
+        "y": 2 * 9 * ny,
+        "c": 2 * 9 * ny + 2 * 9 * nx,
+    }
+    for a in range(4):
+        for p in range(nx + 2 * REACH):
+            edge = p < REACH or p >= REACH + nx
+            spans = [slice(0, ny + 2 * TILE)] if edge else [slice(0, TILE), slice(TILE + ny, ny + 2 * TILE)]
+            for span in spans:
+                ext[a, p, span] = jnp.zeros((span.stop - span.start, nz), jnp.float32)
+    sides_x = (
+        (REACH - 2, jnp.where(gx > 0, 1.0, 0.0), 1 - gx % 2),
+        (REACH + nx, jnp.where(gx < lax.axis_size("gx") - 1, 1.0, 0.0), gx % 2),
+    )
+    sides_y = (
+        (TILE - 2, jnp.where(gy > 0, 1.0, 0.0), 1 - gy % 2),
+        (TILE + ny, jnp.where(gy < lax.axis_size("gy") - 1, 1.0, 0.0), gy % 2),
+    )
     for h in range(2):
         z = slice(h * half, (h + 1) * half)
         for a in range(4):
             ext[a, REACH : REACH + nx, TILE : TILE + ny, z] = own[h, a]
-            ext[a, :REACH, TILE : TILE + ny, z] = side_x[0, h, a]
-            ext[a, REACH + nx :, TILE : TILE + ny, z] = side_x[1, h, a]
-            ext[a, :, :TILE, z] = side_y[0, h, a]
-            ext[a, :, TILE + ny :, z] = side_y[1, h, a]
+        for p, keep, kind in sides_x:
+            for n in range(9):
+                a, l = (n // 2, n % 2) if n < 8 else (1, 2)
+                at = first["x"] + (9 * h + n) * ny
+                if n < 8 or p > REACH:
+                    ext[a, p + l, TILE : TILE + ny, z] = keep * shared[kind, at : at + ny]
+        for r, keep, kind in sides_y:
+            for i in range(nx):
+                for a in range(4):
+                    at = first["y"] + 9 * nx * h + (a * nx + i) * 2
+                    ext[a, REACH + i, r : r + 2, z] = keep * shared[kind, at : at + 2]
+                if r > TILE:
+                    at = first["y"] + 9 * nx * h + 8 * nx + i
+                    ext[2, REACH + i, r + 2 : r + 3, z] = keep * shared[kind, at : at + 1]
+        for p, keep_x, kind_x in sides_x:
+            for r, keep_y, kind_y in sides_y:
+                keep = keep_x * keep_y
+                at = pl.multiple_of(first["c"] + 32 * kind_x + 16 * h, 8)
+                lines = keep * shared[kind_y, pl.ds(at, 16)]
+                for a in range(4):
+                    for l in range(2):
+                        n = (2 * a + l) * 2
+                        ext[a, p + l, r : r + 2, z] = lines[n : n + 2]
     shape = (ny + 2 * TILE, nz)
     row, lane = iota(shape, 0), iota(shape, 1)
     inner_z = lane > 0
@@ -300,25 +364,25 @@
         out[i] = value + k_in[4, i] * at(2, i, 0) + k_in[5, i] * at(1, i, 0)
 
 
-def halves(block, axis, dim, width, reach):
-    count, core = lax.axis_size(axis), lax.axis_index("gz")
-    start = core * (block.shape[dim] - width)
-    slab = lax.dynamic_slice_in_dim(block, start, width, dim)
+def pair(i, kind, count):
+    return i ^ 1 if kind == 0 else (i + 1 if i % 2 else i - 1) % count
+
+
+def swap(block, to):
+    cx, cy, cz = (lax.axis_size(axis) for axis in ("gx", "gy", "gz"))
     route = []
-    for i in range(count - 1):
-        route += [(2 * i + 1, 2 * i + 2), (2 * i + 2, 2 * i + 1)]
-    taken = lax.ppermute(slab, (axis, "gz"), route)
-    return lax.all_gather(taken, "gz", axis=0)
-
-
-def doubled_over(block, axis):
+    for i in range(cx):
+        for j in range(cy):
+            for c in range(cz):
+                x, y, z = to(i, j, c)
+                route.append(((i * cy + j) * cz + c, (x * cy + y) * cz + z))
+    return lax.ppermute(block, ("gx", "gy", "gz"), route)
+
+
+def gathered(block, axis):
     count = lax.axis_size(axis)
-    step = 1
-    while step < count:
-        other = lax.ppermute(block, axis, [(i, i ^ step) for i in range(count)])
-        block = jnp.concatenate([block, other], 0)
-        step *= 2
-    return block
+    parts = [lax.ppermute(block, axis, [(i, i ^ k) for i in range(count)]) for k in range(1, count)]
+    return jnp.concatenate([block] + parts, 0)
 
 
 def f32(*shape):
@@ -329,9 +393,20 @@
     nx, ny, nz = adjoint_residual.shape
     stacked = jnp.stack((adjoint_residual, face_x, face_y, face_z))
     own = lax.all_gather(stacked, "gz", axis=0)
-    side_x = halves(own, "gx", 2, REACH, REACH)
-    tall = jnp.concatenate([side_x[0], own, side_x[1]], 2)
-    side_y = halves(tall, "gy", 3, TILE, REACH)
+    cx, cy = lax.axis_size("gx"), lax.axis_size("gy")
+    packed = pl.pallas_call(
+        pack_kernel,
+        out_shape=(f32(2, 9, ny, nz), f32(2, 9 * nx, nz), f32(2, 16, nz), f32(2, 16, nz)),
+        name="pack",
+    )(own)
+    routes = (
+        lambda i, j, c: (pair(i, c, cx), j, c),
+        lambda i, j, c: (i, pair(j, c, cy), c),
+        lambda i, j, c: (pair(i, 0, cx), pair(j, c, cy), c),
+        lambda i, j, c: (pair(i, 1, cx), pair(j, c, cy), c),
+    )
+    taken = [swap(block.reshape(-1, nz), route) for block, route in zip(packed, routes)]
+    shared = lax.all_gather(jnp.concatenate(taken, 0), "gz", axis=0)
     ext_x, ext_y, wide = nx + 2 * REACH, ny + 2 * TILE, 2 * nz
     field = pltpu.VMEM((ext_x, ext_y, wide), jnp.float32)
     t, k, m = pl.pallas_call(
@@ -346,8 +421,8 @@
             pltpu.VMEM((2 * nx * ny, nz), jnp.float32),
         ],
         name="fine",
-    )(own, side_x, side_y)
-    here = doubled_over(doubled_over(m[None], "gx"), "gy")
+    )(own, shared)
+    here = gathered(gathered(m[None], "gx"), "gy")
     there = lax.ppermute(here, "gz", [(0, 1), (1, 0)])
     n1, m1 = here.shape[2] * lax.axis_size("gx"), here.shape[3] * lax.axis_size("gy")
     tall = (nx // 2 + 2) * (ny // 2 + 2 * TILE)

time: 65.3 us -> 49.8 us (0.76)
  blocking collectives: 27.6 us -> 5.87 us
  starting transfers between devices: 10.5 us -> 16.5 us
  Pallas kernels: 8.96 us -> 10.7 us
  other arithmetic: 1.77 us -> 0.98 us
    all_gather x2 -> x1, blocking collectives: 25.3 us -> 3.44 us  [per_device_small(): shared = lax.all_gather(jnp.concatenate(taken, 0), 'gz', axis=0)]
    ppermute x6 -> x10, starting transfers between devices: 10.4 us -> 16.4 us  [the longest x4 8.48 us: swap(): return lax.ppermute(block, ('gx', 'gy', 'gz'), route)]
    pallas_call x0 -> x1, Pallas kernels: none -> 1.82 us  [per_device_small(): pl.pallas_call(pack_kernel, out_shape=(f32(2, 9, ny, nz), f32(2, 9 * nx,...]
    concatenate x4 -> x2, other arithmetic: 0.82 us -> 0.03 us  [the longest x1 0.02 us: per_device_small(): shared = lax.all_gather(jnp.concatenate(taken, 0), 'gz', axis=0)]
    ppermute x6 -> x10, waiting for transfers between devices: 12.5 us -> 11.9 us  [the longest x6 8.47 us: gathered(): lax.ppermute(block, axis, [(i, i ^ k) for i in range(count)])]
    unnamed x14 -> x12, local copies, waits for them, and re-layouts: 1.57 us -> 1.63 us
  transfers between devices with their start and end apart: 7 -> 11, of which waited for: 5 -> 7; matrix products, arithmetic and copies ran while one was open for 0% -> 2% of each run, Pallas kernels for 0% -> 0%
where the time goes in v2:
time: 49.8 us; the launch traced here: 49.5 us
  starting transfers between devices  16.5 us (33%)
  waiting for transfers between devices  13.8 us (28%)
  Pallas kernels  10.7 us (21%)
  blocking collectives  5.87 us (12%)
  local copies, waits for them, and re-layouts  1.64 us (3%)
  other arithmetic  0.98 us (2%)
    ppermute x4, starting transfers between devices, swap(): return lax.ppermute(block, ('gx', 'gy', 'gz'), route)  8.48 us
    ppermute x6, waiting for transfers between devices, gathered(): lax.ppermute(block, axis, [(i, i ^ k) for i in range(count)])  8.47 us
    ppermute x6, starting transfers between devices, gathered(): lax.ppermute(block, axis, [(i, i ^ k) for i in range(count)])  7.94 us
    pallas_call x1, Pallas kernels, per_device_small(): pl.pallas_call(whole_kernel, out_shape=f32(nx, ny, nz), scratch_shapes=[p...  6.02 us
    all_gather x1, blocking collectives, per_device_small(): shared = lax.all_gather(jnp.concatenate(taken, 0), 'gz', axis=0)  3.44 us
    ppermute x4, waiting for transfers between devices, swap(): return lax.ppermute(block, ('gx', 'gy', 'gz'), route)  3.41 us
    pallas_call x1, Pallas kernels, per_device_small(): pl.pallas_call(fine_kernel, out_shape=(f32(nx, ny, nz), f32(6, nx, ny, nz...  2.83 us
    all_gather x1, blocking collectives, per_device_small(): own = lax.all_gather(stacked, 'gz', axis=0)  2.43 us
  transfers between devices with their start and end apart: 11, of which 7 were waited for; matrix products, arithmetic and copies ran while one was open for 2% of the time, Pallas kernels for 0%

profile of v2, /device:TPU:0, one launch (start us, length us, event | category | flops | bytes accessed | tf_op | source)
XLA Modules:
  0.0 49.5 jit_solution(13299142164712840695)
XLA Ops:
  0.0 1.0 %pad_maximum_fusion = f32[4,8,16,128]{3,2,1,0:T(8,128)S(1)} fusion(f32[1,8,16,128]{3,2,1,0:T(8,128)} %bitcast.19, f32[1,8,16,128]{3,2,1,0:T(8,128)} %bitcast.20, f32[1,8,16,128]{3,2,1,0:T(8,128)} %bitcast.21, f32[1,8,16,128]{3,2,1,0:T(8,128)} %bitcast.22), kind=kLoop, calls=%fused_computation | loop fusion | flops 196608 | bytes 524288 | tf_op jit(solution)/shard_map/stack | solution.py:394
  1.0 2.4 %all-gather = f32[8,8,16,128]{3,2,1,0:T(8,128)} all-gather(f32[4,8,16,128]{3,2,1,0:T(8,128)S(1)} %pad_maximum_fusion), channel_id=2, replica_groups=mesh['gx'=4,'gy'=4,'gz'=2] {'gz'}, dimensions={0}, use_global_device_ids=true | all-gather | bytes 786432 | tf_op jit(solution)/shard_map/all_gather | solution.py:395
  3.4 1.8 %pack.1 = (f32[2,9,16,128]{3,2,1,0:T(8,128)}, f32[2,72,128]{2,1,0:T(8,128)}, f32[2,16,128]{2,1,0:T(8,128)}, f32[2,16,128]{2,1,0:T(8,128)}) custom-call(f32[2,4,8,16,128]{4,3,2,1,0:T(8,128)} %bitcast.12), custom_call_target="tpu_custom_call" | custom-call | tf_op jit(solution)/shard_map/pack/pallas_call | solution.py:397
  5.2 2.9 %collective-permute-start = (f32[288,128]{1,0:T(8,128)}, f32[288,128]{1,0:T(8,128)S(1)}, u32[]{:S(2)}, u32[]{:S(2)}) collective-permute-start(f32[288,128]{1,0:T(8,128)} %bitcast.23), channel_id=1, source_target_pairs={{0,8},{1,25},{2,10},{3,27},{4,12},{5,29},{6,14},{7,31},{8,0},{9,17... | collective-permute-start | bytes 442376 | tf_op jit(solution)/shard_map/ppermute | solution.py:379
  8.1 1.5 %collective-permute-start.1 = (f32[144,128]{1,0:T(8,128)}, f32[144,128]{1,0:T(8,128)S(1)}, u32[]{:S(2)}, u32[]{:S(2)}) collective-permute-start(f32[144,128]{1,0:T(8,128)} %bitcast.24), channel_id=1, source_target_pairs={{0,2},{1,7},{2,0},{3,5},{4,6},{5,3},{6,4},{7,1},{8,10},{9,15},{10,... | collective-permute-start | bytes 221192 | tf_op jit(solution)/shard_map/ppermute | solution.py:379
  9.6 2.4 %collective-permute-start.3 = (f32[32,128]{1,0:T(8,128)}, f32[32,128]{1,0:T(8,128)S(1)}, u32[]{:S(2)}, u32[]{:S(2)}) collective-permute-start(f32[32,128]{1,0:T(8,128)} %bitcast.26), channel_id=1, source_target_pairs={{0,26},{1,31},{2,24},{3,29},{4,30},{5,27},{6,28},{7,25},{8,18},{9,... | collective-permute-start | bytes 49160 | tf_op jit(solution)/shard_map/ppermute | solution.py:379
  12.1 1.6 %collective-permute-start.2 = (f32[32,128]{1,0:T(8,128)}, f32[32,128]{1,0:T(8,128)S(1)}, u32[]{:S(2)}, u32[]{:S(2)}) collective-permute-start(f32[32,128]{1,0:T(8,128)} %bitcast.25), channel_id=1, source_target_pairs={{0,10},{1,15},{2,8},{3,13},{4,14},{5,11},{6,12},{7,9},{8,2},{9,7},... | collective-permute-start | bytes 49160 | tf_op jit(solution)/shard_map/ppermute | solution.py:379
  13.7 2.6 %collective-permute-done.3 = f32[32,128]{1,0:T(8,128)S(1)} collective-permute-done((f32[32,128]{1,0:T(8,128)}, f32[32,128]{1,0:T(8,128)S(1)}, u32[]{:S(2)}, u32[]{:S(2)}) %collective-permute-start.3) | collective-permute-done | bytes 16416 | tf_op jit(solution)/shard_map/ppermute | solution.py:379
  16.3 0.8 %collective-permute-done.2 = f32[32,128]{1,0:T(8,128)S(1)} collective-permute-done((f32[32,128]{1,0:T(8,128)}, f32[32,128]{1,0:T(8,128)S(1)}, u32[]{:S(2)}, u32[]{:S(2)}) %collective-permute-start.2) | collective-permute-done | bytes 16416 | tf_op jit(solution)/shard_map/ppermute | solution.py:379
  17.1 0.0 collective-permute-done.1
  17.1 0.0 collective-permute-done
  17.1 3.4 %all-gather.1 = f32[992,128]{1,0:T(8,128)} all-gather(f32[496,128]{1,0:T(8,128)S(1)} %pad_maximum_fusion.1), channel_id=3, replica_groups=mesh['gx'=4,'gy'=4,'gz'=2] {'gz'}, dimensions={0}, use_global_device_ids=true | all-gather | bytes 761856 | tf_op jit(solution)/shard_map/all_gather | solution.py:409
  20.6 2.8 %fine.1 = (f32[8,16,128]{2,1,0:T(8,128)}, f32[6,8,16,128]{3,2,1,0:T(8,128)}, f32[2,4,8,128]{3,2,1,0:T(8,128)}) custom-call(f32[2,4,8,16,128]{4,3,2,1,0:T(8,128)} %bitcast.13, f32[2,496,128]{2,1,0:T(8,128)} %bitcast.14), custom_call_target="tpu_custom_call" | custom-call | tf_op jit(solution)/shard_map/fine/pallas_call | solution.py:412
  23.4 0.0 collective-permute-start.4
  23.4 2.2 %collective-permute-start.5 = (f32[1,2,4,8,128]{4,3,2,1,0:T(8,128)}, f32[1,2,4,8,128]{4,3,2,1,0:T(8,128)S(1)}, u32[]{:S(2)}, u32[]{:S(2)}) collective-permute-start(f32[1,2,4,8,128]{4,3,2,1,0:T(8,128)} %bitcast.16), channel_id=1, source_target_pairs={{0,16},{8,24},{16,0},{24,8},{1,17},{9,25},{17,1},{25,9},{2,18},{10... | collective-permute-start | bytes 98312 | tf_op jit(solution)/shard_map/ppermute | solution.py:384
  25.6 2.2 %collective-permute-start.6 = (f32[1,2,4,8,128]{4,3,2,1,0:T(8,128)}, f32[1,2,4,8,128]{4,3,2,1,0:T(8,128)S(1)}, u32[]{:S(2)}, u32[]{:S(2)}) collective-permute-start(f32[1,2,4,8,128]{4,3,2,1,0:T(8,128)} %bitcast.17), channel_id=1, source_target_pairs={{0,24},{8,16},{16,8},{24,0},{1,25},{9,17},{17,9},{25,1},{2,26},{10... | collective-permute-start | bytes 98312 | tf_op jit(solution)/shard_map/ppermute | solution.py:384
  27.8 0.8 %constant_dynamic-update-slice_fusion.6 = f32[16,2,4,8,128]{4,3,2,1,0:T(8,128)S(1)} fusion(f32[2,4,8,128]{3,2,1,0:T(8,128)} %get-tuple-element.16), kind=kLoop, calls=%fused_computation.9 | loop fusion | bytes 65536
  28.6 0.0 collective-permute-done.4
  28.6 0.1 collective-permute-done.5
  28.6 2.9 %collective-permute-done.6 = f32[1,2,4,8,128]{4,3,2,1,0:T(8,128)S(1)} collective-permute-done((f32[1,2,4,8,128]{4,3,2,1,0:T(8,128)}, f32[1,2,4,8,128]{4,3,2,1,0:T(8,128)S(1)}, u32[]{:S(2)}, u32[]{:S(2)}) %collective-permute-start.6) | collective-permute-done | bytes 32800 | tf_op jit(solution)/shard_map/ppermute | solution.py:384
  31.5 0.0 copy-done.2
  31.5 1.6 %collective-permute-start.7 = (f32[4,2,4,8,128]{4,3,2,1,0:T(8,128)S(1)}, f32[4,2,4,8,128]{4,3,2,1,0:T(8,128)S(1)}, u32[]{:S(2)}, u32[]{:S(2)}) collective-permute-start(f32[4,2,4,8,128]{4,3,2,1,0:T(8,128)S(1)} %pad_maximum_fusion.2), channel_id=1, source_target_pairs={{0,2},{2,0},{4,6},{6,4},{1,3},{3,1},{5,7},{7,5},{8,10},{10,8},{12,... | collective-permute-start | bytes 393224 | tf_op jit(solution)/shard_map/ppermute | solution.py:384
  33.1 1.5 %collective-permute-start.8 = (f32[4,2,4,8,128]{4,3,2,1,0:T(8,128)S(1)}, f32[4,2,4,8,128]{4,3,2,1,0:T(8,128)S(1)}, u32[]{:S(2)}, u32[]{:S(2)}) collective-permute-start(f32[4,2,4,8,128]{4,3,2,1,0:T(8,128)S(1)} %pad_maximum_fusion.2), channel_id=1, source_target_pairs={{0,4},{2,6},{4,0},{6,2},{1,5},{3,7},{5,1},{7,3},{8,12},{10,14},{12... | collective-permute-start | bytes 393224 | tf_op jit(solution)/shard_map/ppermute | solution.py:384
  34.6 0.5 collective-permute-start.9
  35.1 2.8 %collective-permute-done.7 = f32[4,2,4,8,128]{4,3,2,1,0:T(8,128)S(1)} collective-permute-done((f32[4,2,4,8,128]{4,3,2,1,0:T(8,128)S(1)}, f32[4,2,4,8,128]{4,3,2,1,0:T(8,128)S(1)}, u32[]{:S(2)}, u32[]{:S(2)}) %collective-permute-start.7) | collective-permute-done | bytes 131104 | tf_op jit(solution)/shard_map/ppermute | solution.py:384
  37.9 2.7 %collective-permute-done.8 = f32[4,2,4,8,128]{4,3,2,1,0:T(8,128)S(1)} collective-permute-done((f32[4,2,4,8,128]{4,3,2,1,0:T(8,128)S(1)}, f32[4,2,4,8,128]{4,3,2,1,0:T(8,128)S(1)}, u32[]{:S(2)}, u32[]{:S(2)}) %collective-permute-start.8) | collective-permute-done | bytes 131104 | tf_op jit(solution)/shard_map/ppermute | solution.py:384
  40.7 0.0 collective-permute-done.9
  40.7 0.0 copy-start
  40.7 0.1 collective-permute-start.10
  40.8 1.9 %collective-permute-done.10.there = f32[16,2,4,8,128]{4,3,2,1,0:T(8,128)S(1)} collective-permute-done((f32[16,2,4,8,128]{4,3,2,1,0:T(8,128)S(1)}, f32[16,2,4,8,128]{4,3,2,1,0:T(8,128)S(1)}, u32[]{:S(2)}, u32[]{:S(2)}) %collective-permute-start.10) | collective-permute-done | bytes 524320 | tf_op jit(solution)/shard_map/ppermute | solution.py:426
  42.7 0.8 %copy-done.1 = f32[16,2,4,8,128]{4,3,2,1,0:T(8,128)} copy-done((f32[16,2,4,8,128]{4,3,2,1,0:T(8,128)}, f32[16,2,4,8,128]{4,3,2,1,0:T(8,128)S(1)}, u32[]{:S(2)}) %copy-start.1) | copy-done | bytes 524312
  43.5 6.0 %whole.1 = f32[8,16,128]{2,1,0:T(8,128)} custom-call(f32[16,2,4,8,128]{4,3,2,1,0:T(8,128)} %copy-done, f32[16,2,4,8,128]{4,3,2,1,0:T(8,128)} %copy-done.1, f32[8,16,128]{2,1,0:T(8,128)} %get-tuple-element.17.t_in, f32[6,8,16,128]{3,2,1,0:T(8,128)} %get-tuple-element.18.k_in), custom_call_target="tpu_custom_call" | custom-call | tf_op jit(solution)/shard_map/whole/pallas_call | solution.py:429
  (11 shorter events, 0.1 us)
Async XLA Ops:
  5.2 11.9 %collective-permute-start = (f32[288,128]{1,0:T(8,128)}, f32[288,128]{1,0:T(8,128)S(1)}, u32[]{:S(2)}, u32[]{:S(2)}) collective-permute-start(f32[288,128]{1,0:T(8,128)} %bitcast.23), channel_id=1, source_target_pairs={{0,8},{1,25},{2,10},{3,27},{4,12},{5,29},{6,14},{7,31},{8,0},{9,17... | collective-permute-start | bytes 442376 | tf_op jit(solution)/shard_map/ppermute | solution.py:379
  8.1 8.9 %collective-permute-start.1 = (f32[144,128]{1,0:T(8,128)}, f32[144,128]{1,0:T(8,128)S(1)}, u32[]{:S(2)}, u32[]{:S(2)}) collective-permute-start(f32[144,128]{1,0:T(8,128)} %bitcast.24), channel_id=1, source_target_pairs={{0,2},{1,7},{2,0},{3,5},{4,6},{5,3},{6,4},{7,1},{8,10},{9,15},{10,... | collective-permute-start | bytes 221192 | tf_op jit(solution)/shard_map/ppermute | solution.py:379
  9.6 6.6 %collective-permute-start.3 = (f32[32,128]{1,0:T(8,128)}, f32[32,128]{1,0:T(8,128)S(1)}, u32[]{:S(2)}, u32[]{:S(2)}) collective-permute-start(f32[32,128]{1,0:T(8,128)} %bitcast.26), channel_id=1, source_target_pairs={{0,26},{1,31},{2,24},{3,29},{4,30},{5,27},{6,28},{7,25},{8,18},{9,... | collective-permute-start | bytes 49160 | tf_op jit(solution)/shard_map/ppermute | solution.py:379
  12.1 5.0 %collective-permute-start.2 = (f32[32,128]{1,0:T(8,128)}, f32[32,128]{1,0:T(8,128)S(1)}, u32[]{:S(2)}, u32[]{:S(2)}) collective-permute-start(f32[32,128]{1,0:T(8,128)} %bitcast.25), channel_id=1, source_target_pairs={{0,10},{1,15},{2,8},{3,13},{4,14},{5,11},{6,12},{7,9},{8,2},{9,7},... | collective-permute-start | bytes 49160 | tf_op jit(solution)/shard_map/ppermute | solution.py:379
  23.4 8.1 %copy-start.2 = (f32[2,4,8,128]{3,2,1,0:T(8,128)S(1)}, f32[2,4,8,128]{3,2,1,0:T(8,128)}, u32[]{:S(2)}) copy-start(f32[2,4,8,128]{3,2,1,0:T(8,128)} %get-tuple-element.16) | copy-start | bytes 98308
  23.4 5.2 %collective-permute-start.4 = (f32[1,2,4,8,128]{4,3,2,1,0:T(8,128)}, f32[1,2,4,8,128]{4,3,2,1,0:T(8,128)S(1)}, u32[]{:S(2)}, u32[]{:S(2)}) collective-permute-start(f32[1,2,4,8,128]{4,3,2,1,0:T(8,128)} %bitcast.15), channel_id=1, source_target_pairs={{0,8},{8,0},{16,24},{24,16},{1,9},{9,1},{17,25},{25,17},{2,10},{10... | collective-permute-start | bytes 98312 | tf_op jit(solution)/shard_map/ppermute | solution.py:384
  23.4 5.2 %collective-permute-start.5 = (f32[1,2,4,8,128]{4,3,2,1,0:T(8,128)}, f32[1,2,4,8,128]{4,3,2,1,0:T(8,128)S(1)}, u32[]{:S(2)}, u32[]{:S(2)}) collective-permute-start(f32[1,2,4,8,128]{4,3,2,1,0:T(8,128)} %bitcast.16), channel_id=1, source_target_pairs={{0,16},{8,24},{16,0},{24,8},{1,17},{9,25},{17,1},{25,9},{2,18},{10... | collective-permute-start | bytes 98312 | tf_op jit(solution)/shard_map/ppermute | solution.py:384
  25.6 5.9 %collective-permute-start.6 = (f32[1,2,4,8,128]{4,3,2,1,0:T(8,128)}, f32[1,2,4,8,128]{4,3,2,1,0:T(8,128)S(1)}, u32[]{:S(2)}, u32[]{:S(2)}) collective-permute-start(f32[1,2,4,8,128]{4,3,2,1,0:T(8,128)} %bitcast.17), channel_id=1, source_target_pairs={{0,24},{8,16},{16,8},{24,0},{1,25},{9,17},{17,9},{25,1},{2,26},{10... | collective-permute-start | bytes 98312 | tf_op jit(solution)/shard_map/ppermute | solution.py:384
  31.5 6.3 %collective-permute-start.7 = (f32[4,2,4,8,128]{4,3,2,1,0:T(8,128)S(1)}, f32[4,2,4,8,128]{4,3,2,1,0:T(8,128)S(1)}, u32[]{:S(2)}, u32[]{:S(2)}) collective-permute-start(f32[4,2,4,8,128]{4,3,2,1,0:T(8,128)S(1)} %pad_maximum_fusion.2), channel_id=1, source_target_pairs={{0,2},{2,0},{4,6},{6,4},{1,3},{3,1},{5,7},{7,5},{8,10},{10,8},{12,... | collective-permute-start | bytes 393224 | tf_op jit(solution)/shard_map/ppermute | solution.py:384
  33.1 7.6 %collective-permute-start.8 = (f32[4,2,4,8,128]{4,3,2,1,0:T(8,128)S(1)}, f32[4,2,4,8,128]{4,3,2,1,0:T(8,128)S(1)}, u32[]{:S(2)}, u32[]{:S(2)}) collective-permute-start(f32[4,2,4,8,128]{4,3,2,1,0:T(8,128)S(1)} %pad_maximum_fusion.2), channel_id=1, source_target_pairs={{0,4},{2,6},{4,0},{6,2},{1,5},{3,7},{5,1},{7,3},{8,12},{10,14},{12... | collective-permute-start | bytes 393224 | tf_op jit(solution)/shard_map/ppermute | solution.py:384
  34.6 6.0 %collective-permute-start.9 = (f32[4,2,4,8,128]{4,3,2,1,0:T(8,128)S(1)}, f32[4,2,4,8,128]{4,3,2,1,0:T(8,128)S(1)}, u32[]{:S(2)}, u32[]{:S(2)}) collective-permute-start(f32[4,2,4,8,128]{4,3,2,1,0:T(8,128)S(1)} %pad_maximum_fusion.2), channel_id=1, source_target_pairs={{0,6},{2,4},{4,2},{6,0},{1,7},{3,5},{5,3},{7,1},{8,14},{10,12},{12... | collective-permute-start | bytes 393224 | tf_op jit(solution)/shard_map/ppermute | solution.py:384
  40.7 2.0 %copy-start = (f32[16,2,4,8,128]{4,3,2,1,0:T(8,128)}, f32[16,2,4,8,128]{4,3,2,1,0:T(8,128)S(1)}, u32[]{:S(2)}) copy-start(f32[16,2,4,8,128]{4,3,2,1,0:T(8,128)S(1)} %constant_dynamic-update-slice_fusion.here) | copy-start | bytes 1572868
  40.7 2.0 %collective-permute-start.10 = (f32[16,2,4,8,128]{4,3,2,1,0:T(8,128)S(1)}, f32[16,2,4,8,128]{4,3,2,1,0:T(8,128)S(1)}, u32[]{:S(2)}, u32[]{:S(2)}) collective-permute-start(f32[16,2,4,8,128]{4,3,2,1,0:T(8,128)S(1)} %constant_dynamic-update-slice_fusion.here), channel_id=1, source_target_pairs={{0,1},{1,0},{2,3},{3,2},{4,5},{5,4},{6,7},{7,6},{8,9},{9,8},{10,11... | collective-permute-start | bytes 1572872 | tf_op jit(solution)/shard_map/ppermute | solution.py:426
  42.7 0.8 %copy-start.1 = (f32[16,2,4,8,128]{4,3,2,1,0:T(8,128)}, f32[16,2,4,8,128]{4,3,2,1,0:T(8,128)S(1)}, u32[]{:S(2)}) copy-start(f32[16,2,4,8,128]{4,3,2,1,0:T(8,128)S(1)} %collective-permute-done.10.there) | copy-start | bytes 1572868

commit v3 on v2

--- a/solution.py
+++ b/solution.py
@@ -15,6 +15,7 @@
 
 REACH = 3
 TILE = 8
+PARAMS = pltpu.CompilerParams(vmem_limit_bytes=16 * 2**20)
 
 
 def up(v, axis):
@@ -397,6 +398,7 @@
     packed = pl.pallas_call(
         pack_kernel,
         out_shape=(f32(2, 9, ny, nz), f32(2, 9 * nx, nz), f32(2, 16, nz), f32(2, 16, nz)),
+        compiler_params=PARAMS,
         name="pack",
     )(own)
     routes = (
@@ -420,6 +422,7 @@
             field,
             pltpu.VMEM((2 * nx * ny, nz), jnp.float32),
         ],
+        compiler_params=PARAMS,
         name="fine",
     )(own, shared)
     here = gathered(gathered(m[None], "gx"), "gy")
@@ -437,6 +440,7 @@
             pltpu.VMEM((n1 + 2, m1 + 2 * TILE, nz), jnp.float32),
             pltpu.VMEM((3, 2 * tall, nz), jnp.float32),
         ],
+        compiler_params=PARAMS,
         name="whole",
     )(here, there, t, k)
 

time: 49.8 us -> 43.4 us (0.87)
  Pallas kernels: 10.7 us -> 5.78 us
  local copies, waits for them, and re-layouts: 1.64 us -> 0.05 us
    pallas_call x1, Pallas kernels: 2.83 us -> 1.01 us  [per_device_small(): pl.pallas_call(fine_kernel, out_shape=(f32(nx, ny, nz), f32(6, nx, ny, nz...]
    pallas_call x1, Pallas kernels: 1.82 us -> 0.07 us  [per_device_small(): pl.pallas_call(pack_kernel, out_shape=(f32(2, 9, ny, nz), f32(2, 9 * nx,...]
    unnamed x12 -> x6, local copies, waits for them, and re-layouts: 1.63 us -> 0.04 us
    pallas_call x1, Pallas kernels: 6.02 us -> 4.7 us  [per_device_small(): pl.pallas_call(whole_kernel, out_shape=f32(nx, ny, nz), scratch_shapes=[p...]
    ppermute x6, waiting for transfers between devices: 8.47 us -> 9.06 us  [gathered(): lax.ppermute(block, axis, [(i, i ^ k) for i in range(count)])]
  transfers between devices with their start and end apart: 11 -> 11, of which waited for: 7 -> 7; matrix products, arithmetic and copies ran while one was open for 2% -> 0% of each run, Pallas kernels for 0% -> 0%
where the time goes in v3:
time: 43.4 us; the launch traced here: 43.3 us
  starting transfers between devices  16.6 us (38%)
  waiting for transfers between devices  14.1 us (32%)
  Pallas kernels  5.78 us (13%)
  blocking collectives  5.68 us (13%)
  other arithmetic  0.98 us (2%)
    ppermute x6, waiting for transfers between devices, gathered(): lax.ppermute(block, axis, [(i, i ^ k) for i in range(count)])  9.06 us
    ppermute x4, starting transfers between devices, swap(): return lax.ppermute(block, ('gx', 'gy', 'gz'), route)  8.54 us
    ppermute x6, starting transfers between devices, gathered(): lax.ppermute(block, axis, [(i, i ^ k) for i in range(count)])  8 us
    pallas_call x1, Pallas kernels, per_device_small(): pl.pallas_call(whole_kernel, out_shape=f32(nx, ny, nz), scratch_shapes=[p...  4.7 us
    all_gather x1, blocking collectives, per_device_small(): shared = lax.all_gather(jnp.concatenate(taken, 0), 'gz', axis=0)  3.38 us
    ppermute x4, waiting for transfers between devices, swap(): return lax.ppermute(block, ('gx', 'gy', 'gz'), route)  3.12 us
    all_gather x1, blocking collectives, per_device_small(): own = lax.all_gather(stacked, 'gz', axis=0)  2.3 us
    ppermute x1, waiting for transfers between devices, per_device_small(): there = lax.ppermute(here, 'gz', [(0, 1), (1, 0)])  1.9 us
  transfers between devices with their start and end apart: 11, of which 7 were waited for; matrix products, arithmetic and copies ran while one was open for 0% of the time, Pallas kernels for 0%

profile of v3, /device:TPU:0, one launch (start us, length us, event | category | flops | bytes accessed | tf_op | source)
XLA Modules:
  0.0 43.3 jit_solution(8512197471055850110)
XLA Ops:
  0.0 1.0 %pad_maximum_fusion = f32[4,8,16,128]{3,2,1,0:T(8,128)S(1)} fusion(f32[1,8,16,128]{3,2,1,0:T(8,128)} %bitcast.23, f32[1,8,16,128]{3,2,1,0:T(8,128)} %bitcast.24, f32[1,8,16,128]{3,2,1,0:T(8,128)} %bitcast.25, f32[1,8,16,128]{3,2,1,0:T(8,128)} %bitcast.26), kind=kLoop, calls=%fused_computation | loop fusion | flops 196608 | bytes 524288 | tf_op jit(solution)/shard_map/stack | solution.py:395
  1.0 2.3 %all-gather = f32[8,8,16,128]{3,2,1,0:T(8,128)S(1)} all-gather(f32[4,8,16,128]{3,2,1,0:T(8,128)S(1)} %pad_maximum_fusion), channel_id=2, replica_groups=mesh['gx'=4,'gy'=4,'gz'=2] {'gz'}, dimensions={0}, use_global_device_ids=true | all-gather | bytes 786432 | tf_op jit(solution)/shard_map/all_gather | solution.py:396
  3.3 0.1 pack.1
  3.3 3.0 %collective-permute-start = (f32[288,128]{1,0:T(8,128)S(1)}, f32[288,128]{1,0:T(8,128)S(1)}, u32[]{:S(2)}, u32[]{:S(2)}) collective-permute-start(f32[288,128]{1,0:T(8,128)S(1)} %bitcast.19), channel_id=1, source_target_pairs={{0,8},{1,25},{2,10},{3,27},{4,12},{5,29},{6,14},{7,31},{8,0},{9,17... | collective-permute-start | bytes 442376 | tf_op jit(solution)/shard_map/ppermute | solution.py:380
  6.3 1.5 %collective-permute-start.1 = (f32[144,128]{1,0:T(8,128)S(1)}, f32[144,128]{1,0:T(8,128)S(1)}, u32[]{:S(2)}, u32[]{:S(2)}) collective-permute-start(f32[144,128]{1,0:T(8,128)S(1)} %bitcast.20), channel_id=1, source_target_pairs={{0,2},{1,7},{2,0},{3,5},{4,6},{5,3},{6,4},{7,1},{8,10},{9,15},{10,... | collective-permute-start | bytes 221192 | tf_op jit(solution)/shard_map/ppermute | solution.py:380
  7.8 2.4 %collective-permute-start.3 = (f32[32,128]{1,0:T(8,128)S(1)}, f32[32,128]{1,0:T(8,128)S(1)}, u32[]{:S(2)}, u32[]{:S(2)}) collective-permute-start(f32[32,128]{1,0:T(8,128)S(1)} %bitcast.22), channel_id=1, source_target_pairs={{0,26},{1,31},{2,24},{3,29},{4,30},{5,27},{6,28},{7,25},{8,18},{9,... | collective-permute-start | bytes 49160 | tf_op jit(solution)/shard_map/ppermute | solution.py:380
  10.3 1.6 %collective-permute-start.2 = (f32[32,128]{1,0:T(8,128)S(1)}, f32[32,128]{1,0:T(8,128)S(1)}, u32[]{:S(2)}, u32[]{:S(2)}) collective-permute-start(f32[32,128]{1,0:T(8,128)S(1)} %bitcast.21), channel_id=1, source_target_pairs={{0,10},{1,15},{2,8},{3,13},{4,14},{5,11},{6,12},{7,9},{8,2},{9,7},... | collective-permute-start | bytes 49160 | tf_op jit(solution)/shard_map/ppermute | solution.py:380
  11.9 2.4 %collective-permute-done.3 = f32[32,128]{1,0:T(8,128)S(1)} collective-permute-done((f32[32,128]{1,0:T(8,128)S(1)}, f32[32,128]{1,0:T(8,128)S(1)}, u32[]{:S(2)}, u32[]{:S(2)}) %collective-permute-start.3) | collective-permute-done | bytes 16416 | tf_op jit(solution)/shard_map/ppermute | solution.py:380
  14.3 0.7 %collective-permute-done.2 = f32[32,128]{1,0:T(8,128)S(1)} collective-permute-done((f32[32,128]{1,0:T(8,128)S(1)}, f32[32,128]{1,0:T(8,128)S(1)}, u32[]{:S(2)}, u32[]{:S(2)}) %collective-permute-start.2) | collective-permute-done | bytes 16416 | tf_op jit(solution)/shard_map/ppermute | solution.py:380
  15.0 0.0 collective-permute-done.1
  15.0 0.0 collective-permute-done
  15.0 3.4 %all-gather.1 = f32[992,128]{1,0:T(8,128)S(1)} all-gather(f32[496,128]{1,0:T(8,128)S(1)} %pad_maximum_fusion.1), channel_id=3, replica_groups=mesh['gx'=4,'gy'=4,'gz'=2] {'gz'}, dimensions={0}, use_global_device_ids=true | all-gather | bytes 761856 | tf_op jit(solution)/shard_map/all_gather | solution.py:411
  18.4 1.0 %fine.1 = (f32[8,16,128]{2,1,0:T(8,128)S(1)}, f32[6,8,16,128]{3,2,1,0:T(8,128)S(1)}, f32[2,4,8,128]{3,2,1,0:T(8,128)S(1)}) custom-call(f32[2,4,8,16,128]{4,3,2,1,0:T(8,128)S(1)} %bitcast.13, f32[2,496,128]{2,1,0:T(8,128)S(1)} %bitcast.14), custom_call_target="tpu_custom_call" | custom-call | tf_op jit(solution)/shard_map/fine/pallas_call | solution.py:414
  19.4 0.1 collective-permute-start.4
  19.5 2.2 %collective-permute-start.5 = (f32[1,2,4,8,128]{4,3,2,1,0:T(8,128)S(1)}, f32[1,2,4,8,128]{4,3,2,1,0:T(8,128)S(1)}, u32[]{:S(2)}, u32[]{:S(2)}) collective-permute-start(f32[1,2,4,8,128]{4,3,2,1,0:T(8,128)S(1)} %bitcast.16), channel_id=1, source_target_pairs={{0,16},{8,24},{16,0},{24,8},{1,17},{9,25},{17,1},{25,9},{2,18},{10... | collective-permute-start | bytes 98312 | tf_op jit(solution)/shard_map/ppermute | solution.py:385
  21.7 2.2 %collective-permute-start.6 = (f32[1,2,4,8,128]{4,3,2,1,0:T(8,128)S(1)}, f32[1,2,4,8,128]{4,3,2,1,0:T(8,128)S(1)}, u32[]{:S(2)}, u32[]{:S(2)}) collective-permute-start(f32[1,2,4,8,128]{4,3,2,1,0:T(8,128)S(1)} %bitcast.17), channel_id=1, source_target_pairs={{0,24},{8,16},{16,8},{24,0},{1,25},{9,17},{17,9},{25,1},{2,26},{10... | collective-permute-start | bytes 98312 | tf_op jit(solution)/shard_map/ppermute | solution.py:385
  23.9 0.0 collective-permute-done.4
  23.9 1.1 %collective-permute-done.5 = f32[1,2,4,8,128]{4,3,2,1,0:T(8,128)S(1)} collective-permute-done((f32[1,2,4,8,128]{4,3,2,1,0:T(8,128)S(1)}, f32[1,2,4,8,128]{4,3,2,1,0:T(8,128)S(1)}, u32[]{:S(2)}, u32[]{:S(2)}) %collective-permute-start.5) | collective-permute-done | bytes 32800 | tf_op jit(solution)/shard_map/ppermute | solution.py:385
  25.0 2.4 %collective-permute-done.6 = f32[1,2,4,8,128]{4,3,2,1,0:T(8,128)S(1)} collective-permute-done((f32[1,2,4,8,128]{4,3,2,1,0:T(8,128)S(1)}, f32[1,2,4,8,128]{4,3,2,1,0:T(8,128)S(1)}, u32[]{:S(2)}, u32[]{:S(2)}) %collective-permute-start.6) | collective-permute-done | bytes 32800 | tf_op jit(solution)/shard_map/ppermute | solution.py:385
  27.4 1.6 %collective-permute-start.7 = (f32[4,2,4,8,128]{4,3,2,1,0:T(8,128)S(1)}, f32[4,2,4,8,128]{4,3,2,1,0:T(8,128)S(1)}, u32[]{:S(2)}, u32[]{:S(2)}) collective-permute-start(f32[4,2,4,8,128]{4,3,2,1,0:T(8,128)S(1)} %pad_maximum_fusion.2), channel_id=1, source_target_pairs={{0,2},{2,0},{4,6},{6,4},{1,3},{3,1},{5,7},{7,5},{8,10},{10,8},{12,... | collective-permute-start | bytes 393224 | tf_op jit(solution)/shard_map/ppermute | solution.py:385
  29.0 1.5 %collective-permute-start.8 = (f32[4,2,4,8,128]{4,3,2,1,0:T(8,128)S(1)}, f32[4,2,4,8,128]{4,3,2,1,0:T(8,128)S(1)}, u32[]{:S(2)}, u32[]{:S(2)}) collective-permute-start(f32[4,2,4,8,128]{4,3,2,1,0:T(8,128)S(1)} %pad_maximum_fusion.2), channel_id=1, source_target_pairs={{0,4},{2,6},{4,0},{6,2},{1,5},{3,7},{5,1},{7,3},{8,12},{10,14},{12... | collective-permute-start | bytes 393224 | tf_op jit(solution)/shard_map/ppermute | solution.py:385
  30.5 0.5 %collective-permute-start.9 = (f32[4,2,4,8,128]{4,3,2,1,0:T(8,128)S(1)}, f32[4,2,4,8,128]{4,3,2,1,0:T(8,128)S(1)}, u32[]{:S(2)}, u32[]{:S(2)}) collective-permute-start(f32[4,2,4,8,128]{4,3,2,1,0:T(8,128)S(1)} %pad_maximum_fusion.2), channel_id=1, source_target_pairs={{0,6},{2,4},{4,2},{6,0},{1,7},{3,5},{5,3},{7,1},{8,14},{10,12},{12... | collective-permute-start | bytes 393224 | tf_op jit(solution)/shard_map/ppermute | solution.py:385
  31.0 2.8 %collective-permute-done.7 = f32[4,2,4,8,128]{4,3,2,1,0:T(8,128)S(1)} collective-permute-done((f32[4,2,4,8,128]{4,3,2,1,0:T(8,128)S(1)}, f32[4,2,4,8,128]{4,3,2,1,0:T(8,128)S(1)}, u32[]{:S(2)}, u32[]{:S(2)}) %collective-permute-start.7) | collective-permute-done | bytes 131104 | tf_op jit(solution)/shard_map/ppermute | solution.py:385
  33.8 2.8 %collective-permute-done.8 = f32[4,2,4,8,128]{4,3,2,1,0:T(8,128)S(1)} collective-permute-done((f32[4,2,4,8,128]{4,3,2,1,0:T(8,128)S(1)}, f32[4,2,4,8,128]{4,3,2,1,0:T(8,128)S(1)}, u32[]{:S(2)}, u32[]{:S(2)}) %collective-permute-start.8) | collective-permute-done | bytes 131104 | tf_op jit(solution)/shard_map/ppermute | solution.py:385
  36.5 0.0 collective-permute-done.9
  36.6 0.1 collective-permute-start.10
  36.7 1.9 %collective-permute-done.10.there = f32[16,2,4,8,128]{4,3,2,1,0:T(8,128)S(1)} collective-permute-done((f32[16,2,4,8,128]{4,3,2,1,0:T(8,128)S(1)}, f32[16,2,4,8,128]{4,3,2,1,0:T(8,128)S(1)}, u32[]{:S(2)}, u32[]{:S(2)}) %collective-permute-start.10) | collective-permute-done | bytes 524320 | tf_op jit(solution)/shard_map/ppermute | solution.py:429
  38.6 4.7 %whole.1 = f32[8,16,128]{2,1,0:T(8,128)} custom-call(f32[16,2,4,8,128]{4,3,2,1,0:T(8,128)S(1)} %constant_dynamic-update-slice_fusion.here, f32[16,2,4,8,128]{4,3,2,1,0:T(8,128)S(1)} %collective-permute-done.10.there, f32[8,16,128]{2,1,0:T(8,128)S(1)} %get-tuple-element.17.t_in, f32[6,8,16,128]{3,2,1,0:T(8,128)S(1)} %get-tuple-element.18.k_in), custom_call_target="tpu_custom_call" | custom-call | tf_op jit(solution)/shard_map/whole/pallas_call | solution.py:432
  (9 shorter events, 0.1 us)
Async XLA Ops:
  3.3 11.7 %collective-permute-start = (f32[288,128]{1,0:T(8,128)S(1)}, f32[288,128]{1,0:T(8,128)S(1)}, u32[]{:S(2)}, u32[]{:S(2)}) collective-permute-start(f32[288,128]{1,0:T(8,128)S(1)} %bitcast.19), channel_id=1, source_target_pairs={{0,8},{1,25},{2,10},{3,27},{4,12},{5,29},{6,14},{7,31},{8,0},{9,17... | collective-permute-start | bytes 442376 | tf_op jit(solution)/shard_map/ppermute | solution.py:380
  6.3 8.7 %collective-permute-start.1 = (f32[144,128]{1,0:T(8,128)S(1)}, f32[144,128]{1,0:T(8,128)S(1)}, u32[]{:S(2)}, u32[]{:S(2)}) collective-permute-start(f32[144,128]{1,0:T(8,128)S(1)} %bitcast.20), channel_id=1, source_target_pairs={{0,2},{1,7},{2,0},{3,5},{4,6},{5,3},{6,4},{7,1},{8,10},{9,15},{10,... | collective-permute-start | bytes 221192 | tf_op jit(solution)/shard_map/ppermute | solution.py:380
  7.8 6.4 %collective-permute-start.3 = (f32[32,128]{1,0:T(8,128)S(1)}, f32[32,128]{1,0:T(8,128)S(1)}, u32[]{:S(2)}, u32[]{:S(2)}) collective-permute-start(f32[32,128]{1,0:T(8,128)S(1)} %bitcast.22), channel_id=1, source_target_pairs={{0,26},{1,31},{2,24},{3,29},{4,30},{5,27},{6,28},{7,25},{8,18},{9,... | collective-permute-start | bytes 49160 | tf_op jit(solution)/shard_map/ppermute | solution.py:380
  10.3 4.7 %collective-permute-start.2 = (f32[32,128]{1,0:T(8,128)S(1)}, f32[32,128]{1,0:T(8,128)S(1)}, u32[]{:S(2)}, u32[]{:S(2)}) collective-permute-start(f32[32,128]{1,0:T(8,128)S(1)} %bitcast.21), channel_id=1, source_target_pairs={{0,10},{1,15},{2,8},{3,13},{4,14},{5,11},{6,12},{7,9},{8,2},{9,7},... | collective-permute-start | bytes 49160 | tf_op jit(solution)/shard_map/ppermute | solution.py:380
  19.4 4.5 %collective-permute-start.4 = (f32[1,2,4,8,128]{4,3,2,1,0:T(8,128)S(1)}, f32[1,2,4,8,128]{4,3,2,1,0:T(8,128)S(1)}, u32[]{:S(2)}, u32[]{:S(2)}) collective-permute-start(f32[1,2,4,8,128]{4,3,2,1,0:T(8,128)S(1)} %bitcast.15), channel_id=1, source_target_pairs={{0,8},{8,0},{16,24},{24,16},{1,9},{9,1},{17,25},{25,17},{2,10},{10... | collective-permute-start | bytes 98312 | tf_op jit(solution)/shard_map/ppermute | solution.py:385
  19.5 5.5 %collective-permute-start.5 = (f32[1,2,4,8,128]{4,3,2,1,0:T(8,128)S(1)}, f32[1,2,4,8,128]{4,3,2,1,0:T(8,128)S(1)}, u32[]{:S(2)}, u32[]{:S(2)}) collective-permute-start(f32[1,2,4,8,128]{4,3,2,1,0:T(8,128)S(1)} %bitcast.16), channel_id=1, source_target_pairs={{0,16},{8,24},{16,0},{24,8},{1,17},{9,25},{17,1},{25,9},{2,18},{10... | collective-permute-start | bytes 98312 | tf_op jit(solution)/shard_map/ppermute | solution.py:385
  21.7 5.7 %collective-permute-start.6 = (f32[1,2,4,8,128]{4,3,2,1,0:T(8,128)S(1)}, f32[1,2,4,8,128]{4,3,2,1,0:T(8,128)S(1)}, u32[]{:S(2)}, u32[]{:S(2)}) collective-permute-start(f32[1,2,4,8,128]{4,3,2,1,0:T(8,128)S(1)} %bitcast.17), channel_id=1, source_target_pairs={{0,24},{8,16},{16,8},{24,0},{1,25},{9,17},{17,9},{25,1},{2,26},{10... | collective-permute-start | bytes 98312 | tf_op jit(solution)/shard_map/ppermute | solution.py:385
  27.4 6.3 %collective-permute-start.7 = (f32[4,2,4,8,128]{4,3,2,1,0:T(8,128)S(1)}, f32[4,2,4,8,128]{4,3,2,1,0:T(8,128)S(1)}, u32[]{:S(2)}, u32[]{:S(2)}) collective-permute-start(f32[4,2,4,8,128]{4,3,2,1,0:T(8,128)S(1)} %pad_maximum_fusion.2), channel_id=1, source_target_pairs={{0,2},{2,0},{4,6},{6,4},{1,3},{3,1},{5,7},{7,5},{8,10},{10,8},{12,... | collective-permute-start | bytes 393224 | tf_op jit(solution)/shard_map/ppermute | solution.py:385
  29.0 7.6 %collective-permute-start.8 = (f32[4,2,4,8,128]{4,3,2,1,0:T(8,128)S(1)}, f32[4,2,4,8,128]{4,3,2,1,0:T(8,128)S(1)}, u32[]{:S(2)}, u32[]{:S(2)}) collective-permute-start(f32[4,2,4,8,128]{4,3,2,1,0:T(8,128)S(1)} %pad_maximum_fusion.2), channel_id=1, source_target_pairs={{0,4},{2,6},{4,0},{6,2},{1,5},{3,7},{5,1},{7,3},{8,12},{10,14},{12... | collective-permute-start | bytes 393224 | tf_op jit(solution)/shard_map/ppermute | solution.py:385
  30.5 6.1 %collective-permute-start.9 = (f32[4,2,4,8,128]{4,3,2,1,0:T(8,128)S(1)}, f32[4,2,4,8,128]{4,3,2,1,0:T(8,128)S(1)}, u32[]{:S(2)}, u32[]{:S(2)}) collective-permute-start(f32[4,2,4,8,128]{4,3,2,1,0:T(8,128)S(1)} %pad_maximum_fusion.2), channel_id=1, source_target_pairs={{0,6},{2,4},{4,2},{6,0},{1,7},{3,5},{5,3},{7,1},{8,14},{10,12},{12... | collective-permute-start | bytes 393224 | tf_op jit(solution)/shard_map/ppermute | solution.py:385
  36.6 2.0 %collective-permute-start.10 = (f32[16,2,4,8,128]{4,3,2,1,0:T(8,128)S(1)}, f32[16,2,4,8,128]{4,3,2,1,0:T(8,128)S(1)}, u32[]{:S(2)}, u32[]{:S(2)}) collective-permute-start(f32[16,2,4,8,128]{4,3,2,1,0:T(8,128)S(1)} %constant_dynamic-update-slice_fusion.here), channel_id=1, source_target_pairs={{0,1},{1,0},{2,3},{3,2},{4,5},{5,4},{6,7},{7,6},{8,9},{9,8},{10,11... | collective-permute-start | bytes 1572872 | tf_op jit(solution)/shard_map/ppermute | solution.py:429

commit v4 on v1

--- a/solution.py
+++ b/solution.py
@@ -15,6 +15,7 @@
 
 REACH = 3
 TILE = 8
+PARAMS = pltpu.CompilerParams(vmem_limit_bytes=16 * 2**20)
 
 
 def up(v, axis):
@@ -46,22 +47,112 @@
     return jnp.where(diagonal > 0.0, damping / jnp.where(diagonal > 0.0, diagonal, 1.0), 0.0)
 
 
-def fine_kernel(own, side_x, side_y, t_out, k_out, m_out, ext, e1, rd, dg, e2, rows):
-    nx, ny = own.shape[2], own.shape[3]
-    nz = 2 * own.shape[4]
-    half = own.shape[4]
+def side(axis):
+    here = lax.axis_index(axis)
+    first = jnp.where(here > 0, 1.0, 0.0)
+    last = jnp.where(here < lax.axis_size(axis) - 1, 1.0, 0.0)
+    return (here % 2 == 1, first), (here % 2 == 0, last)
+
+
+def x_kernel(own, *slabs):
+    nx, gx = own.shape[1], lax.axis_index("gx")
+    for kind, out in enumerate(slabs):
+        start = jnp.where((gx + kind) % 2 == 0, nx - 2, 0)
+        for a in range(4):
+            for n in range(2):
+                out[2 * a + n] = own[a, start + n]
+        out[8] = own[1, 2]
+
+
+def sides_x(slabs, before, behind):
+    for (even, keep), out in zip(side("gx"), (before, behind)):
+        for n in range(9):
+            out[n] = keep * jnp.where(even, slabs[0][n], slabs[1][n])
+
+
+def y_kernel(own, s0, s1, o0, o1, before, behind):
+    nx, ny = own.shape[1], own.shape[2]
+    gy = lax.axis_index("gy")
+    sides_x((s0, s1), before, behind)
+    for kind, out in enumerate((o0, o1)):
+        ahead = (gy + kind) % 2 == 0
+        for p in range(nx + 4):
+            for a in range(4):
+                if p < 2:
+                    v = before[2 * a + p]
+                elif p < nx + 2:
+                    v = own[a, p - 2]
+                else:
+                    v = behind[2 * a + p - nx - 2]
+                at = (a * (nx + 4) + p) * 2
+                out[at : at + 2] = jnp.where(ahead, v[ny - 2 :], v[:2])
+                if a == 2:
+                    out[8 * (nx + 4) + p : 8 * (nx + 4) + p + 1] = v[2:3]
+        used = 9 * (nx + 4)
+        out[used:] = jnp.zeros((out.shape[0] - used, out.shape[1]), jnp.float32)
+
+
+def z_kernel(own, s0, s1, o0, o1, ext, edge, before, behind, lines):
+    nx, ny, nz = own.shape[1:]
+    gz = lax.axis_index("gz")
+    sides_x((s0, s1), before, behind)
+    zero = jnp.zeros((TILE, nz), jnp.float32)
+    empty = jnp.zeros((ny + 2 * TILE, nz), jnp.float32)
+    for a in range(4):
+        for p in range(nx + 2 * REACH):
+            q = p - REACH
+            if 0 <= q < nx:
+                v = own[a, q]
+            elif -2 <= q < 0:
+                v = before[2 * a + q + 2]
+            elif nx <= q < nx + 2:
+                v = behind[2 * a + q - nx]
+            elif q == nx + 2 and a == 1:
+                v = behind[8]
+            else:
+                ext[a, p] = empty
+                continue
+            ext[a, p, :TILE] = zero
+            ext[a, p, TILE + ny :] = zero
+            ext[a, p, TILE : TILE + ny] = v
+    for (even, keep), r in zip(side("gy"), (TILE - 2, TILE + ny)):
+        lines[...] = keep * jnp.where(even, o0[...], o1[...])
+        for p in range(nx + 4):
+            for a in range(4):
+                at = (a * (nx + 4) + p) * 2
+                ext[a, 1 + p, r : r + 2] = lines[at : at + 2]
+            if r > TILE:
+                at = 8 * (nx + 4) + p
+                ext[2, 1 + p, r + 2 : r + 3] = lines[at : at + 1]
+    lane = iota((ny + 2 * TILE, nz), 1)
+    for p in range(nx + 4):
+        packed = ext[0, 1 + p]
+        for a in range(1, 4):
+            first = jnp.where(gz == 0, nz - 3 - 3 * a, 3 * a)
+            moved = pltpu.roll(ext[a, 1 + p], jnp.where(gz == 0, nz - 3 * a, 3 * a), 1)
+            packed = jnp.where((lane >= first) & (lane < first + 3), moved, packed)
+        edge[p] = packed
+
+
+def fine_kernel(local, edges, t_out, k_out, m_out, ext, e1, rd, dg, e2, rows):
+    nx, ny, half = t_out.shape
+    nz = 2 * half
     gx, gy, gz = lax.axis_index("gx"), lax.axis_index("gy"), lax.axis_index("gz")
-    for h in range(2):
-        z = slice(h * half, (h + 1) * half)
+    spot = iota((ny + 2 * TILE, half), 1)
+    given = jnp.logical_or((gz == 0) & (spot < 3), (gz == 1) & (spot >= half - 3))
+    for p in range(nx + 2 * REACH):
         for a in range(4):
-            ext[a, REACH : REACH + nx, TILE : TILE + ny, z] = own[h, a]
-            ext[a, :REACH, TILE : TILE + ny, z] = side_x[0, h, a]
-            ext[a, REACH + nx :, TILE : TILE + ny, z] = side_x[1, h, a]
-            ext[a, :, :TILE, z] = side_y[0, h, a]
-            ext[a, :, TILE + ny :, z] = side_y[1, h, a]
+            ext[a, p, :, :half] = local[a, p]
+            if 1 <= p < nx + 5:
+                v = edges[1 - gz, p - 1]
+                if a > 0:
+                    v = pltpu.roll(v, jnp.where(gz == 0, half - 3 * a, 3 * a), 1)
+                ext[a, p, :, half:] = jnp.where(given, v, 0.0)
+            else:
+                ext[a, p, :, half:] = jnp.zeros((ny + 2 * TILE, half), jnp.float32)
     shape = (ny + 2 * TILE, nz)
     row, lane = iota(shape, 0), iota(shape, 1)
-    inner_z = lane > 0
+    inner_z = jnp.logical_or(lane > 0, gz > 0)
     in_y = jnp.logical_and(
         jnp.logical_or(gy > 0, row >= TILE),
         jnp.logical_or(gy < lax.axis_size("gy") - 1, row < TILE + ny),
@@ -90,8 +181,7 @@
         e2[p] = jnp.where(inside, value, 0.0)
 
     def mine(v):
-        v = v[TILE : TILE + ny]
-        return jnp.where(gz == 0, v[:, :half], v[:, half:])
+        return v[TILE : TILE + ny, :half]
 
     sums = []
     for i in range(nx):
@@ -102,26 +192,27 @@
         t_out[i] = mine(e2[p] + inv * q)
         for n, k in enumerate((ext[1, p], ext[1, p + 1], fy, up(fy, 0), fz, up(fz, 1))):
             k_out[n, i] = mine(inv * k)
-        sums.append(q[TILE : TILE + ny])
-    inner = slice(TILE, TILE + ny)
+        sums.append(mine(q))
+    def face(d, i):
+        return 0.5 * ext[d, REACH + i, TILE : TILE + ny, :half]
+
     pairs = range(0, nx, 2)
-    wide = [sums[i] + sums[i + 1] for i in pairs]
-    wide += [0.5 * ext[1, REACH + i, inner] for i in pairs]
-    wide += [0.5 * (ext[2, REACH + i, inner] + ext[2, REACH + i + 1, inner]) for i in pairs]
-    thin = [0.5 * (ext[3, REACH + i, inner] + ext[3, REACH + i + 1, inner]) for i in pairs]
-    fine, coarse = iota((nz, half), 0), iota((nz, half), 1)
-    summed = select_dot(jnp.concatenate(wide, 0), chosen(fine // 2 == coarse))
-    picked = select_dot(jnp.concatenate(thin, 0), chosen(fine == 2 * coarse))
+    fine, coarse = iota((half, half), 0), iota((half, half), 1)
+    both_low, both_high = chosen(fine // 2 == coarse), chosen(fine // 2 + half // 2 == coarse)
+    even_high = chosen(fine + half == 2 * coarse)
     count = len(pairs) * ny
-    rows[: 3 * count] = summed
-    rows[3 * count :] = picked
+    rows[:count] = select_dot(jnp.concatenate([sums[i] + sums[i + 1] for i in pairs], 0), both_low) + select_dot(
+        jnp.concatenate([face(1, i) for i in pairs], 0), both_high
+    )
+    rows[count:] = select_dot(jnp.concatenate([face(2, i) + face(2, i + 1) for i in pairs], 0), both_low) + select_dot(
+        jnp.concatenate([face(3, i) + face(3, i + 1) for i in pairs], 0), even_high
+    )
     part = count // 2
-    even = rows[pl.ds(0, 4 * part, stride=2)]
-    odd = rows[pl.ds(1, 4 * part, stride=2)]
-    kept = [even[:part] + odd[:part], even[part : 2 * part] + odd[part : 2 * part]]
-    kept += [even[2 * part : 3 * part], even[3 * part :] + odd[3 * part :]]
-    for a in range(2):
-        m_out[a] = jnp.where(gz == 0, kept[a], kept[2 + a]).reshape(m_out.shape[1:])
+    even = rows[pl.ds(0, 2 * part, stride=2)]
+    odd = rows[pl.ds(1, 2 * part, stride=2)]
+    spot = iota((part, half), 1)
+    m_out[0] = (even[:part] + odd[:part]).reshape(m_out.shape[1:])
+    m_out[1] = (even[part:] + jnp.where(spot < half // 2, 0.0, odd[part:])).reshape(m_out.shape[1:])
 
 
 def planes_of(ref):
@@ -206,12 +297,18 @@
     gx, gy, gz = lax.axis_index("gx"), lax.axis_index("gy"), lax.axis_index("gz")
     cx, cy = lax.axis_size("gx"), lax.axis_size("gy")
     bx, by = here.shape[2], here.shape[3]
+    w1 = here.shape[4]
     for k in range(cx * cy):
         x = jnp.bitwise_xor(gx, k % cx) * bx
         y = pl.multiple_of(jnp.bitwise_xor(gy, k // cx) * by, by)
         for a in range(2):
-            grid[2 * gz + a, pl.ds(x, bx), pl.ds(y, by), :] = here[k, a]
-            grid[2 * (1 - gz) + a, pl.ds(x, bx), pl.ds(y, by), :] = there[k, a]
+            low = jnp.where(gz == 0, here[k, a], there[k, a]).reshape(bx * by, w1)
+            top = jnp.where(gz == 0, there[k, a], here[k, a]).reshape(bx * by, w1)
+            left = iota((bx * by, w1), 1) < w1 // 2
+            one = jnp.where(left, low, pltpu.roll(top, w1 // 2, 1))
+            two = jnp.where(left, pltpu.roll(low, w1 // 2, 1), top)
+            grid[2 * a, pl.ds(x, bx), pl.ds(y, by), :] = one.reshape(bx, by, w1)
+            grid[2 * a + 1, pl.ds(x, bx), pl.ds(y, by), :] = two.reshape(bx, by, w1)
     n1, m1, w1 = grid.shape[1:]
     b1, fx1, fy1, fz1 = (planes_of(grid.at[a]) for a in range(4))
     diagonal1, inv1, off1 = level_parts(fx1, fy1, fz1)
@@ -300,15 +397,24 @@
         out[i] = value + k_in[4, i] * at(2, i, 0) + k_in[5, i] * at(1, i, 0)
 
 
-def halves(block, axis, dim, width, reach):
-    count, core = lax.axis_size(axis), lax.axis_index("gz")
-    start = core * (block.shape[dim] - width)
-    slab = lax.dynamic_slice_in_dim(block, start, width, dim)
-    route = []
-    for i in range(count - 1):
-        route += [(2 * i + 1, 2 * i + 2), (2 * i + 2, 2 * i + 1)]
-    taken = lax.ppermute(slab, (axis, "gz"), route)
-    return lax.all_gather(taken, "gz", axis=0)
+def traded(blocks, axis):
+    count, cores = lax.axis_size(axis), lax.axis_size("gz")
+    taken = []
+    for kind, block in enumerate(blocks):
+        route = []
+        for i in range(count):
+            other = i + 1 if (i + kind) % 2 == 0 else i - 1
+            for c in range(cores):
+                to = other * cores + c if 0 <= other < count else i * cores + cores - 1 - c
+                route.append((i * cores + c, to))
+        taken.append(lax.ppermute(block, (axis, "gz"), route))
+    return taken
+
+
+def gathered(block, axis):
+    count = lax.axis_size(axis)
+    parts = [lax.ppermute(block, axis, [(i, i ^ k) for i in range(count)]) for k in range(1, count)]
+    return jnp.concatenate([block] + parts, 0)
 
 
 def doubled_over(block, axis):
@@ -327,11 +433,32 @@
 
 def per_device_small(adjoint_residual, face_x, face_y, face_z):
     nx, ny, nz = adjoint_residual.shape
-    stacked = jnp.stack((adjoint_residual, face_x, face_y, face_z))
-    own = lax.all_gather(stacked, "gz", axis=0)
-    side_x = halves(own, "gx", 2, REACH, REACH)
-    tall = jnp.concatenate([side_x[0], own, side_x[1]], 2)
-    side_y = halves(tall, "gy", 3, TILE, REACH)
+    near = [pltpu.VMEM((9, ny, nz), jnp.float32)] * 2
+    own = jnp.stack((adjoint_residual, face_x, face_y, face_z))
+    slabs = pl.pallas_call(
+        x_kernel,
+        out_shape=(f32(9, ny, nz), f32(9, ny, nz)),
+        compiler_params=PARAMS,
+        name="slabs_x",
+    )(own)
+    slabs = traded(slabs, "gx")
+    count = -(-9 * (nx + 4) // 8) * 8
+    lines = pl.pallas_call(
+        y_kernel,
+        out_shape=(f32(count, nz), f32(count, nz)),
+        scratch_shapes=near,
+        compiler_params=PARAMS,
+        name="slabs_y",
+    )(own, *slabs)
+    lines = traded(lines, "gy")
+    local, edge = pl.pallas_call(
+        z_kernel,
+        out_shape=(f32(4, nx + 2 * REACH, ny + 2 * TILE, nz), f32(nx + 4, ny + 2 * TILE, nz)),
+        scratch_shapes=near + [pltpu.VMEM((count, nz), jnp.float32)],
+        compiler_params=PARAMS,
+        name="edges_z",
+    )(own, *slabs, *lines)
+    edges = lax.all_gather(edge, "gz", axis=0)
     ext_x, ext_y, wide = nx + 2 * REACH, ny + 2 * TILE, 2 * nz
     field = pltpu.VMEM((ext_x, ext_y, wide), jnp.float32)
     t, k, m = pl.pallas_call(
@@ -343,11 +470,12 @@
             field,
             field,
             field,
-            pltpu.VMEM((2 * nx * ny, nz), jnp.float32),
+            pltpu.VMEM((nx * ny, nz), jnp.float32),
         ],
+        compiler_params=PARAMS,
         name="fine",
-    )(own, side_x, side_y)
-    here = doubled_over(doubled_over(m[None], "gx"), "gy")
+    )(local, edges)
+    here = gathered(doubled_over(m[None], "gx"), "gy")
     there = lax.ppermute(here, "gz", [(0, 1), (1, 0)])
     n1, m1 = here.shape[2] * lax.axis_size("gx"), here.shape[3] * lax.axis_size("gy")
     tall = (nx // 2 + 2) * (ny // 2 + 2 * TILE)
@@ -362,6 +490,7 @@
             pltpu.VMEM((n1 + 2, m1 + 2 * TILE, nz), jnp.float32),
             pltpu.VMEM((3, 2 * tall, nz), jnp.float32),
         ],
+        compiler_params=PARAMS,
         name="whole",
     )(here, there, t, k)
 

time: 65.3 us -> 41.7 us (0.64)
  blocking collectives: 27.6 us -> 2.09 us
  starting transfers between devices: 10.5 us -> 17 us
  Pallas kernels: 8.96 us -> 6.04 us
  local copies, waits for them, and re-layouts: 1.63 us -> 0.04 us
  waiting for transfers between devices: 14.4 us -> 15.3 us
  other arithmetic: 1.77 us -> 0.97 us
    all_gather x3 -> x1, blocking collectives: 27.6 us -> 2.09 us  [per_device_small(): edges = lax.all_gather(edge, 'gz', axis=0)]
    ppermute x2 -> x7, waiting for transfers between devices: 0.01 us -> 9.31 us  [the longest x4 4.86 us: traded(): taken.append(lax.ppermute(block, (axis, 'gz'), route))]
    ppermute x2 -> x7, starting transfers between devices: 1.36 us -> 10.2 us  [the longest x4 5.12 us: traded(): taken.append(lax.ppermute(block, (axis, 'gz'), route))]
    ppermute x4 -> x2, waiting for transfers between devices: 12.5 us -> 4.13 us  [doubled_over(): other = lax.ppermute(block, axis, [(i, i ^ step) for i in range(count)])]
    ppermute x4 -> x2, starting transfers between devices: 9.07 us -> 6.74 us  [doubled_over(): other = lax.ppermute(block, axis, [(i, i ^ step) for i in range(count)])]
    pallas_call x1, Pallas kernels: 2.93 us -> 0.78 us  [per_device_small(): pl.pallas_call(fine_kernel, out_shape=(f32(nx, ny, nz), f32(6, nx, ny, nz...]
    unnamed x14 -> x5, local copies, waits for them, and re-layouts: 1.57 us -> 0.03 us
    pallas_call x1, Pallas kernels: 6.03 us -> 4.88 us  [per_device_small(): pl.pallas_call(whole_kernel, out_shape=f32(nx, ny, nz), scratch_shapes=[p...]
  transfers between devices with their start and end apart: 7 -> 10, of which waited for: 5 -> 8; matrix products, arithmetic and copies ran while one was open for 0% -> 0% of each run, Pallas kernels for 0% -> 0%
where the time goes in v4:
time: 41.7 us; the launch traced here: 41.6 us
  starting transfers between devices  17 us (41%)
  waiting for transfers between devices  15.3 us (37%)
  Pallas kernels  6.04 us (14%)
  blocking collectives  2.09 us (5%)
  other arithmetic  0.97 us (2%)
    ppermute x2, starting transfers between devices, doubled_over(): other = lax.ppermute(block, axis, [(i, i ^ step) for i in range(count)])  6.74 us
    ppermute x4, starting transfers between devices, traded(): taken.append(lax.ppermute(block, (axis, 'gz'), route))  5.12 us
    ppermute x3, starting transfers between devices, gathered(): lax.ppermute(block, axis, [(i, i ^ k) for i in range(count)])  5.09 us
    pallas_call x1, Pallas kernels, per_device_small(): pl.pallas_call(whole_kernel, out_shape=f32(nx, ny, nz), scratch_shapes=[p...  4.88 us
    ppermute x4, waiting for transfers between devices, traded(): taken.append(lax.ppermute(block, (axis, 'gz'), route))  4.86 us
    ppermute x3, waiting for transfers between devices, gathered(): lax.ppermute(block, axis, [(i, i ^ k) for i in range(count)])  4.45 us
    ppermute x2, waiting for transfers between devices, doubled_over(): other = lax.ppermute(block, axis, [(i, i ^ step) for i in range(count)])  4.13 us
    all_gather x1, blocking collectives, per_device_small(): edges = lax.all_gather(edge, 'gz', axis=0)  2.09 us
  transfers between devices with their start and end apart: 10, of which 8 were waited for; matrix products, arithmetic and copies ran while one was open for 0% of the time, Pallas kernels for 0%

profile of v4, /device:TPU:0, one launch (start us, length us, event | category | flops | bytes accessed | tf_op | source)
XLA Modules:
  0.0 41.6 jit_solution(14439658113340659156)
XLA Ops:
  0.0 1.0 %pad_maximum_fusion.own = f32[4,8,16,128]{3,2,1,0:T(8,128)S(1)} fusion(f32[1,8,16,128]{3,2,1,0:T(8,128)} %bitcast.11, f32[1,8,16,128]{3,2,1,0:T(8,128)} %bitcast.12, f32[1,8,16,128]{3,2,1,0:T(8,128)} %bitcast.13, f32[1,8,16,128]{3,2,1,0:T(8,128)} %bitcast.14), kind=kLoop, calls=%fused_computation | loop fusion | flops 196608 | bytes 524288 | tf_op jit(solution)/shard_map/stack | solution.py:437
  1.0 3.1 %collective-permute-start = (f32[9,16,128]{2,1,0:T(8,128)S(1)}, f32[9,16,128]{2,1,0:T(8,128)S(1)}, u32[]{:S(2)}, u32[]{:S(2)}) collective-permute-start(f32[9,16,128]{2,1,0:T(8,128)S(1)} %get-tuple-element.14), channel_id=1, source_target_pairs={{0,8},{1,9},{8,0},{9,1},{16,24},{17,25},{24,16},{25,17},{2,10},{3,... | collective-permute-start | bytes 221192 | tf_op jit(solution)/shard_map/ppermute | solution.py:410
  4.1 0.0 collective-permute-start.1
  4.1 2.3 %collective-permute-done.s0 = f32[9,16,128]{2,1,0:T(8,128)S(1)} collective-permute-done((f32[9,16,128]{2,1,0:T(8,128)S(1)}, f32[9,16,128]{2,1,0:T(8,128)S(1)}, u32[]{:S(2)}, u32[]{:S(2)}) %collective-permute-start) | collective-permute-done | bytes 73760 | tf_op jit(solution)/shard_map/ppermute | solution.py:410
  6.4 0.0 collective-permute-done.1.s1
  6.4 0.1 slabs_y.1
  6.5 2.0 %collective-permute-start.2 = (f32[112,128]{1,0:T(8,128)S(1)}, f32[112,128]{1,0:T(8,128)S(1)}, u32[]{:S(2)}, u32[]{:S(2)}) collective-permute-start(f32[112,128]{1,0:T(8,128)S(1)} %get-tuple-element.16), channel_id=1, source_target_pairs={{0,2},{1,3},{2,0},{3,1},{4,6},{5,7},{6,4},{7,5},{8,10},{9,11},{10,... | collective-permute-start | bytes 172040 | tf_op jit(solution)/shard_map/ppermute | solution.py:410
  8.5 0.0 collective-permute-start.3
  8.5 2.5 %collective-permute-done.2.o0 = f32[112,128]{1,0:T(8,128)S(1)} collective-permute-done((f32[112,128]{1,0:T(8,128)S(1)}, f32[112,128]{1,0:T(8,128)S(1)}, u32[]{:S(2)}, u32[]{:S(2)}) %collective-permute-start.2) | collective-permute-done | bytes 57376 | tf_op jit(solution)/shard_map/ppermute | solution.py:410
  11.0 0.0 collective-permute-done.3.o1
  11.1 0.3 edges_z.1
  11.3 2.1 %all-gather = f32[24,32,128]{2,1,0:T(8,128)S(1)} all-gather(f32[12,32,128]{2,1,0:T(8,128)S(1)} %get-tuple-element.19), channel_id=2, replica_groups=mesh['gx'=4,'gy'=4,'gz'=2] {'gz'}, dimensions={0}, use_global_device_ids=true | all-gather | bytes 589824 | tf_op jit(solution)/shard_map/all_gather | solution.py:461
  13.4 0.8 %fine.1 = (f32[8,16,128]{2,1,0:T(8,128)S(1)}, f32[6,8,16,128]{3,2,1,0:T(8,128)S(1)}, f32[2,4,8,128]{3,2,1,0:T(8,128)S(1)}) custom-call(f32[4,14,32,128]{3,2,1,0:T(8,128)S(1)} %get-tuple-element.18.local, f32[2,12,32,128]{3,2,1,0:T(8,128)S(1)} %bitcast.7), custom_call_target="tpu_custom_call" | custom-call | tf_op jit(solution)/shard_map/fine/pallas_call | solution.py:464
  14.2 3.3 %collective-permute-start.4 = (f32[1,2,4,8,128]{4,3,2,1,0:T(8,128)S(1)}, f32[1,2,4,8,128]{4,3,2,1,0:T(8,128)S(1)}, u32[]{:S(2)}, u32[]{:S(2)}) collective-permute-start(f32[1,2,4,8,128]{4,3,2,1,0:T(8,128)S(1)} %bitcast.8), channel_id=1, source_target_pairs={{0,8},{8,0},{16,24},{24,16},{1,9},{9,1},{17,25},{25,17},{2,10},{10... | collective-permute-start | bytes 98312 | tf_op jit(solution)/shard_map/ppermute | solution.py:424
  17.6 1.9 %collective-permute-done.4 = f32[1,2,4,8,128]{4,3,2,1,0:T(8,128)S(1)} collective-permute-done((f32[1,2,4,8,128]{4,3,2,1,0:T(8,128)S(1)}, f32[1,2,4,8,128]{4,3,2,1,0:T(8,128)S(1)}, u32[]{:S(2)}, u32[]{:S(2)}) %collective-permute-start.4) | collective-permute-done | bytes 32800 | tf_op jit(solution)/shard_map/ppermute | solution.py:424
  19.5 3.4 %collective-permute-start.5 = (f32[2,2,4,8,128]{4,3,2,1,0:T(8,128)S(1)}, f32[2,2,4,8,128]{4,3,2,1,0:T(8,128)S(1)}, u32[]{:S(2)}, u32[]{:S(2)}) collective-permute-start(f32[2,2,4,8,128]{4,3,2,1,0:T(8,128)S(1)} %pad_maximum_fusion.2), channel_id=1, source_target_pairs={{0,16},{8,24},{16,0},{24,8},{1,17},{9,25},{17,1},{25,9},{2,18},{10... | collective-permute-start | bytes 196616 | tf_op jit(solution)/shard_map/ppermute | solution.py:424
  22.9 2.2 %collective-permute-done.5 = f32[2,2,4,8,128]{4,3,2,1,0:T(8,128)S(1)} collective-permute-done((f32[2,2,4,8,128]{4,3,2,1,0:T(8,128)S(1)}, f32[2,2,4,8,128]{4,3,2,1,0:T(8,128)S(1)}, u32[]{:S(2)}, u32[]{:S(2)}) %collective-permute-start.5) | collective-permute-done | bytes 65568 | tf_op jit(solution)/shard_map/ppermute | solution.py:424
  25.1 2.8 %collective-permute-start.6 = (f32[4,2,4,8,128]{4,3,2,1,0:T(8,128)S(1)}, f32[4,2,4,8,128]{4,3,2,1,0:T(8,128)S(1)}, u32[]{:S(2)}, u32[]{:S(2)}) collective-permute-start(f32[4,2,4,8,128]{4,3,2,1,0:T(8,128)S(1)} %pad_maximum_fusion.1), channel_id=1, source_target_pairs={{0,2},{2,0},{4,6},{6,4},{1,3},{3,1},{5,7},{7,5},{8,10},{10,8},{12,... | collective-permute-start | bytes 393224 | tf_op jit(solution)/shard_map/ppermute | solution.py:416
  27.9 0.9 %collective-permute-start.7 = (f32[4,2,4,8,128]{4,3,2,1,0:T(8,128)S(1)}, f32[4,2,4,8,128]{4,3,2,1,0:T(8,128)S(1)}, u32[]{:S(2)}, u32[]{:S(2)}) collective-permute-start(f32[4,2,4,8,128]{4,3,2,1,0:T(8,128)S(1)} %pad_maximum_fusion.1), channel_id=1, source_target_pairs={{0,4},{2,6},{4,0},{6,2},{1,5},{3,7},{5,1},{7,3},{8,12},{10,14},{12... | collective-permute-start | bytes 393224 | tf_op jit(solution)/shard_map/ppermute | solution.py:416
  28.8 1.4 %collective-permute-start.8 = (f32[4,2,4,8,128]{4,3,2,1,0:T(8,128)S(1)}, f32[4,2,4,8,128]{4,3,2,1,0:T(8,128)S(1)}, u32[]{:S(2)}, u32[]{:S(2)}) collective-permute-start(f32[4,2,4,8,128]{4,3,2,1,0:T(8,128)S(1)} %pad_maximum_fusion.1), channel_id=1, source_target_pairs={{0,6},{2,4},{4,2},{6,0},{1,7},{3,5},{5,3},{7,1},{8,14},{10,12},{12... | collective-permute-start | bytes 393224 | tf_op jit(solution)/shard_map/ppermute | solution.py:416
  30.2 1.9 %collective-permute-done.6 = f32[4,2,4,8,128]{4,3,2,1,0:T(8,128)S(1)} collective-permute-done((f32[4,2,4,8,128]{4,3,2,1,0:T(8,128)S(1)}, f32[4,2,4,8,128]{4,3,2,1,0:T(8,128)S(1)}, u32[]{:S(2)}, u32[]{:S(2)}) %collective-permute-start.6) | collective-permute-done | bytes 131104 | tf_op jit(solution)/shard_map/ppermute | solution.py:416
  32.2 0.9 %collective-permute-done.7 = f32[4,2,4,8,128]{4,3,2,1,0:T(8,128)S(1)} collective-permute-done((f32[4,2,4,8,128]{4,3,2,1,0:T(8,128)S(1)}, f32[4,2,4,8,128]{4,3,2,1,0:T(8,128)S(1)}, u32[]{:S(2)}, u32[]{:S(2)}) %collective-permute-start.7) | collective-permute-done | bytes 131104 | tf_op jit(solution)/shard_map/ppermute | solution.py:416
  33.1 1.6 %collective-permute-done.8 = f32[4,2,4,8,128]{4,3,2,1,0:T(8,128)S(1)} collective-permute-done((f32[4,2,4,8,128]{4,3,2,1,0:T(8,128)S(1)}, f32[4,2,4,8,128]{4,3,2,1,0:T(8,128)S(1)}, u32[]{:S(2)}, u32[]{:S(2)}) %collective-permute-start.8) | collective-permute-done | bytes 131104 | tf_op jit(solution)/shard_map/ppermute | solution.py:416
  34.7 0.1 collective-permute-start.9
  34.8 1.9 %collective-permute-done.9.there = f32[16,2,4,8,128]{4,3,2,1,0:T(8,128)S(1)} collective-permute-done((f32[16,2,4,8,128]{4,3,2,1,0:T(8,128)S(1)}, f32[16,2,4,8,128]{4,3,2,1,0:T(8,128)S(1)}, u32[]{:S(2)}, u32[]{:S(2)}) %collective-permute-start.9) | collective-permute-done | bytes 524320 | tf_op jit(solution)/shard_map/ppermute | solution.py:479
  36.7 4.9 %whole.1 = f32[8,16,128]{2,1,0:T(8,128)} custom-call(f32[16,2,4,8,128]{4,3,2,1,0:T(8,128)S(1)} %constant_dynamic-update-slice_fusion.here, f32[16,2,4,8,128]{4,3,2,1,0:T(8,128)S(1)} %collective-permute-done.9.there, f32[8,16,128]{2,1,0:T(8,128)S(1)} %get-tuple-element.21.t_in, f32[6,8,16,128]{3,2,1,0:T(8,128)S(1)} %get-tuple-element.22.k_in), custom_call_target="tpu_custom_call" | custom-call | tf_op jit(solution)/shard_map/whole/pallas_call | solution.py:482
  (9 shorter events, 0.1 us)
Async XLA Ops:
  1.0 5.5 %collective-permute-start = (f32[9,16,128]{2,1,0:T(8,128)S(1)}, f32[9,16,128]{2,1,0:T(8,128)S(1)}, u32[]{:S(2)}, u32[]{:S(2)}) collective-permute-start(f32[9,16,128]{2,1,0:T(8,128)S(1)} %get-tuple-element.14), channel_id=1, source_target_pairs={{0,8},{1,9},{8,0},{9,1},{16,24},{17,25},{24,16},{25,17},{2,10},{3,... | collective-permute-start | bytes 221192 | tf_op jit(solution)/shard_map/ppermute | solution.py:410
  4.1 2.3 %collective-permute-start.1 = (f32[9,16,128]{2,1,0:T(8,128)S(1)}, f32[9,16,128]{2,1,0:T(8,128)S(1)}, u32[]{:S(2)}, u32[]{:S(2)}) collective-permute-start(f32[9,16,128]{2,1,0:T(8,128)S(1)} %get-tuple-element.15), channel_id=1, source_target_pairs={{0,1},{1,0},{8,16},{9,17},{16,8},{17,9},{24,25},{25,24},{2,3},{3,2... | collective-permute-start | bytes 221192 | tf_op jit(solution)/shard_map/ppermute | solution.py:410
  6.5 4.5 %collective-permute-start.2 = (f32[112,128]{1,0:T(8,128)S(1)}, f32[112,128]{1,0:T(8,128)S(1)}, u32[]{:S(2)}, u32[]{:S(2)}) collective-permute-start(f32[112,128]{1,0:T(8,128)S(1)} %get-tuple-element.16), channel_id=1, source_target_pairs={{0,2},{1,3},{2,0},{3,1},{4,6},{5,7},{6,4},{7,5},{8,10},{9,11},{10,... | collective-permute-start | bytes 172040 | tf_op jit(solution)/shard_map/ppermute | solution.py:410
  8.5 2.5 %collective-permute-start.3 = (f32[112,128]{1,0:T(8,128)S(1)}, f32[112,128]{1,0:T(8,128)S(1)}, u32[]{:S(2)}, u32[]{:S(2)}) collective-permute-start(f32[112,128]{1,0:T(8,128)S(1)} %get-tuple-element.17), channel_id=1, source_target_pairs={{0,1},{1,0},{2,4},{3,5},{4,2},{5,3},{6,7},{7,6},{8,9},{9,8},{10,12... | collective-permute-start | bytes 172040 | tf_op jit(solution)/shard_map/ppermute | solution.py:410
  14.2 5.2 %collective-permute-start.4 = (f32[1,2,4,8,128]{4,3,2,1,0:T(8,128)S(1)}, f32[1,2,4,8,128]{4,3,2,1,0:T(8,128)S(1)}, u32[]{:S(2)}, u32[]{:S(2)}) collective-permute-start(f32[1,2,4,8,128]{4,3,2,1,0:T(8,128)S(1)} %bitcast.8), channel_id=1, source_target_pairs={{0,8},{8,0},{16,24},{24,16},{1,9},{9,1},{17,25},{25,17},{2,10},{10... | collective-permute-start | bytes 98312 | tf_op jit(solution)/shard_map/ppermute | solution.py:424
  19.5 5.6 %collective-permute-start.5 = (f32[2,2,4,8,128]{4,3,2,1,0:T(8,128)S(1)}, f32[2,2,4,8,128]{4,3,2,1,0:T(8,128)S(1)}, u32[]{:S(2)}, u32[]{:S(2)}) collective-permute-start(f32[2,2,4,8,128]{4,3,2,1,0:T(8,128)S(1)} %pad_maximum_fusion.2), channel_id=1, source_target_pairs={{0,16},{8,24},{16,0},{24,8},{1,17},{9,25},{17,1},{25,9},{2,18},{10... | collective-permute-start | bytes 196616 | tf_op jit(solution)/shard_map/ppermute | solution.py:424
  25.1 7.0 %collective-permute-start.6 = (f32[4,2,4,8,128]{4,3,2,1,0:T(8,128)S(1)}, f32[4,2,4,8,128]{4,3,2,1,0:T(8,128)S(1)}, u32[]{:S(2)}, u32[]{:S(2)}) collective-permute-start(f32[4,2,4,8,128]{4,3,2,1,0:T(8,128)S(1)} %pad_maximum_fusion.1), channel_id=1, source_target_pairs={{0,2},{2,0},{4,6},{6,4},{1,3},{3,1},{5,7},{7,5},{8,10},{10,8},{12,... | collective-permute-start | bytes 393224 | tf_op jit(solution)/shard_map/ppermute | solution.py:416
  27.9 5.2 %collective-permute-start.7 = (f32[4,2,4,8,128]{4,3,2,1,0:T(8,128)S(1)}, f32[4,2,4,8,128]{4,3,2,1,0:T(8,128)S(1)}, u32[]{:S(2)}, u32[]{:S(2)}) collective-permute-start(f32[4,2,4,8,128]{4,3,2,1,0:T(8,128)S(1)} %pad_maximum_fusion.1), channel_id=1, source_target_pairs={{0,4},{2,6},{4,0},{6,2},{1,5},{3,7},{5,1},{7,3},{8,12},{10,14},{12... | collective-permute-start | bytes 393224 | tf_op jit(solution)/shard_map/ppermute | solution.py:416
  28.8 5.9 %collective-permute-start.8 = (f32[4,2,4,8,128]{4,3,2,1,0:T(8,128)S(1)}, f32[4,2,4,8,128]{4,3,2,1,0:T(8,128)S(1)}, u32[]{:S(2)}, u32[]{:S(2)}) collective-permute-start(f32[4,2,4,8,128]{4,3,2,1,0:T(8,128)S(1)} %pad_maximum_fusion.1), channel_id=1, source_target_pairs={{0,6},{2,4},{4,2},{6,0},{1,7},{3,5},{5,3},{7,1},{8,14},{10,12},{12... | collective-permute-start | bytes 393224 | tf_op jit(solution)/shard_map/ppermute | solution.py:416
  34.7 2.0 %collective-permute-start.9 = (f32[16,2,4,8,128]{4,3,2,1,0:T(8,128)S(1)}, f32[16,2,4,8,128]{4,3,2,1,0:T(8,128)S(1)}, u32[]{:S(2)}, u32[]{:S(2)}) collective-permute-start(f32[16,2,4,8,128]{4,3,2,1,0:T(8,128)S(1)} %constant_dynamic-update-slice_fusion.here), channel_id=1, source_target_pairs={{0,1},{1,0},{2,3},{3,2},{4,5},{5,4},{6,7},{7,6},{8,9},{9,8},{10,11... | collective-permute-start | bytes 1572872 | tf_op jit(solution)/shard_map/ppermute | solution.py:479

commit v5 on v4

--- a/solution.py
+++ b/solution.py
@@ -35,12 +35,13 @@
 
 
 def select_dot(values, matrix):
-    high = values.astype(jnp.bfloat16)
-    rest = values - high.astype(jnp.float32)
-    mid = rest.astype(jnp.bfloat16)
-    low = (rest - mid.astype(jnp.float32)).astype(jnp.bfloat16)
-    dot = functools.partial(jnp.dot, preferred_element_type=jnp.float32)
-    return (dot(low, matrix) + dot(mid, matrix)) + dot(high, matrix)
+    count = values.shape[0]
+    high = values.astype(jnp.bfloat16).astype(jnp.float32)
+    rest = values - high
+    mid = rest.astype(jnp.bfloat16).astype(jnp.float32)
+    parts = jnp.concatenate([high, mid, rest - mid], 0).astype(jnp.bfloat16)
+    product = jnp.dot(parts, matrix, preferred_element_type=jnp.float32)
+    return (product[2 * count :] + product[count : 2 * count]) + product[:count]
 
 
 def inverse(diagonal):
@@ -275,21 +276,27 @@
         return result - fzm * down(v, 1) - hz * up(v, 1)
 
     def total(v):
-        return jnp.sum(jnp.sum(v, axis=0, keepdims=True), axis=1, keepdims=True)
-
-    solution = jnp.zeros_like(rhs)
-    remain = rhs
-    search = rhs
-    norm_now = total(remain * remain)
-    for step in range(COARSE_ITERS):
-        image = operate_packed(search)
-        alpha = norm_now / total(search * image)
+        v = jnp.broadcast_to(jnp.sum(v, axis=1, keepdims=True), v.shape)
+        for shift in (4, 2, 1):
+            v = v + pltpu.roll(v, shift, 0)
+        return v
+
+    remain, search = rhs, rhs
+    image = operate_packed(rhs)
+    norm_now, energy = total(rhs * rhs), total(rhs * image)
+    alpha = norm_now / energy
+    solution = alpha * search
+    for step in range(COARSE_ITERS - 1):
+        remain = remain - alpha * image
+        across = operate_packed(remain)
+        norm_next, own, mixed = total(remain * remain), total(remain * across), total(remain * image)
+        beta = norm_next / norm_now
+        energy = own + beta * (2.0 * mixed + beta * energy)
+        search = remain + beta * search
+        image = across + beta * image
+        norm_now = norm_next
+        alpha = norm_now / energy
         solution = solution + alpha * search
-        if step + 1 < COARSE_ITERS:
-            remain = remain - alpha * image
-            norm_next = total(remain * remain)
-            search = remain + norm_next / norm_now * search
-            norm_now = norm_next
     return solution
 
 
@@ -315,42 +322,44 @@
     t1, q1 = before(b1, diagonal1, inv1, off1)
 
     n2, m2 = n1 // 2, m1 // 2
-    fine, coarse = iota((w1, w1), 0), iota((w1, w1), 1)
-    both, even = chosen(fine // 2 == coarse), chosen(fine == 2 * coarse)
     pairs = range(0, n1, 2)
-    wide = [q1[i] + q1[i + 1] for i in pairs] + [0.5 * fx1[i] for i in pairs]
-    wide += [0.5 * (fy1[i] + fy1[i + 1]) for i in pairs]
-    thin = [0.5 * (fz1[i] + fz1[i + 1]) for i in pairs]
-    count = n2 * m1
-    fold1[: 3 * count] = select_dot(jnp.concatenate(wide, 0), both)
-    fold1[3 * count :] = select_dot(jnp.concatenate(thin, 0), even)
+    fold1[...] = jnp.concatenate(
+        [q1[i] + q1[i + 1] for i in pairs]
+        + [0.5 * fx1[i] for i in pairs]
+        + [0.5 * (fy1[i] + fy1[i + 1]) for i in pairs]
+        + [0.5 * (fz1[i] + fz1[i + 1]) for i in pairs],
+        0,
+    )
     half = n2 * m2
     low = fold1[pl.ds(0, 4 * half, stride=2)]
     top = fold1[pl.ds(1, 4 * half, stride=2)]
+    fine, coarse = iota((w1, w1), 0), iota((w1, w1), 1)
+    both, even = chosen(fine // 2 == coarse), chosen(fine == 2 * coarse)
+    summed = jnp.concatenate([low[: 2 * half] + top[: 2 * half], low[2 * half : 3 * half]], 0)
+    summed = select_dot(summed, both)
 
     def part(v):
         return [v[p * m2 : (p + 1) * m2] for p in range(n2)]
 
-    b2 = part(low[:half] + top[:half])
-    fx2 = part(low[half : 2 * half] + top[half : 2 * half])
-    fy2 = part(low[2 * half : 3 * half])
-    fz2 = part(low[3 * half :] + top[3 * half :])
+    b2, fx2, fy2 = (part(summed[i * half : (i + 1) * half]) for i in range(3))
+    fz2 = part(select_dot(low[3 * half :] + top[3 * half :], even))
     diagonal2, inv2, off2 = level_parts(fx2, fy2, fz2)
     t2, q2 = before(b2, diagonal2, inv2, off2)
 
     n3, m3 = n2 // 2, m2 // 2
     depth = w1 // n3
-    packed = [0.0, 0.0, 0.0, 0.0]
-    for i in range(n3):
-        both = chosen((fine // 2 + i * depth == coarse) & (fine < 2 * depth))
-        even = chosen((fine + 2 * i * depth == 2 * coarse) & (fine < 2 * depth))
-        wide = [q2[2 * i] + q2[2 * i + 1], 0.5 * fx2[2 * i], 0.5 * (fy2[2 * i] + fy2[2 * i + 1])]
-        thin = 0.5 * (fz2[2 * i] + fz2[2 * i + 1])
-        summed = select_dot(jnp.concatenate(wide, 0), both)
-        packed[0] = packed[0] + summed[:m2]
-        packed[1] = packed[1] + summed[m2 : 2 * m2]
-        packed[2] = packed[2] + summed[2 * m2 :]
-        packed[3] = packed[3] + select_dot(thin, even)
+    fine, coarse = iota((n3 * w1, w1), 0), iota((n3 * w1, w1), 1)
+    block, fine = fine // w1, fine % w1
+    both = chosen((fine // 2 + block * depth == coarse) & (fine < 2 * depth))
+    even = chosen((fine + 2 * block * depth == 2 * coarse) & (fine < 2 * depth))
+    blocks = range(0, n2, 2)
+    wide = [
+        jnp.concatenate([q2[i] + q2[i + 1] for i in blocks], 1),
+        jnp.concatenate([0.5 * fx2[i] for i in blocks], 1),
+        jnp.concatenate([0.5 * (fy2[i] + fy2[i + 1]) for i in blocks], 1),
+    ]
+    thin = jnp.concatenate([0.5 * (fz2[i] + fz2[i + 1]) for i in blocks], 1)
+    packed = [select_dot(jnp.concatenate(wide, 0), both), select_dot(thin, even)]
     fold2[...] = jnp.concatenate(packed, 0)
     low = fold2[pl.ds(0, 4 * m3, stride=2)]
     top = fold2[pl.ds(1, 4 * m3, stride=2)]
@@ -358,14 +367,17 @@
     fy3, fz3 = low[2 * m3 : 3 * m3], low[3 * m3 :] + top[3 * m3 :]
     c3 = coarse_solution(b3, fx3, fy3, fz3, depth)
 
+    fine, coarse = iota((w1, n3 * w1), 1), iota((w1, n3 * w1), 0)
+    block, fine = fine // w1, fine % w1
+    row = select_dot(c3, chosen((fine // 2 + block * depth == coarse) & (fine < 2 * depth)))
     for i in range(n3):
-        row = select_dot(c3, chosen((coarse // 2 + i * depth == fine) & (coarse < 2 * depth)))
-        spread2[pl.ds(i * m2, m3, stride=2)] = row
-        spread2[pl.ds(i * m2 + 1, m3, stride=2)] = row
+        spread2[pl.ds(i * m2, m3, stride=2)] = row[:, i * w1 : (i + 1) * w1]
+        spread2[pl.ds(i * m2 + 1, m3, stride=2)] = row[:, i * w1 : (i + 1) * w1]
     up2 = [spread2[(p // 2) * m2 : (p // 2 + 1) * m2] for p in range(n2)]
     c2 = after(t2, up2, inv2, off2)
 
-    row = select_dot(jnp.concatenate(c2, 0), chosen(coarse // 2 == fine))
+    fine, coarse = iota((w1, w1), 1), iota((w1, w1), 0)
+    row = select_dot(jnp.concatenate(c2, 0), chosen(fine // 2 == coarse))
     fold1[pl.ds(0, half, stride=2)] = row
     fold1[pl.ds(1, half, stride=2)] = row
     up1 = [fold1[(p // 2) * m1 : (p // 2 + 1) * m1] for p in range(n1)]

time: 41.7 us -> 40.9 us (0.981)
  Pallas kernels: 6.04 us -> 5.24 us
    pallas_call x1, Pallas kernels: 4.88 us -> 4.12 us  [per_device_small(): pl.pallas_call(whole_kernel, out_shape=f32(nx, ny, nz), scratch_shapes=[p...]
where the time goes in v5:
time: 40.9 us; the launch traced here: 40.8 us
  starting transfers between devices  17 us (42%)
  waiting for transfers between devices  15.3 us (37%)
  Pallas kernels  5.24 us (13%)
  blocking collectives  2.09 us (5%)
  other arithmetic  0.97 us (2%)
    ppermute x2, starting transfers between devices, doubled_over(): other = lax.ppermute(block, axis, [(i, i ^ step) for i in range(count)])  6.74 us
    ppermute x4, starting transfers between devices, traded(): taken.append(lax.ppermute(block, (axis, 'gz'), route))  5.12 us
    ppermute x3, starting transfers between devices, gathered(): lax.ppermute(block, axis, [(i, i ^ k) for i in range(count)])  5.09 us
    ppermute x4, waiting for transfers between devices, traded(): taken.append(lax.ppermute(block, (axis, 'gz'), route))  4.86 us
    ppermute x3, waiting for transfers between devices, gathered(): lax.ppermute(block, axis, [(i, i ^ k) for i in range(count)])  4.45 us
    ppermute x2, waiting for transfers between devices, doubled_over(): other = lax.ppermute(block, axis, [(i, i ^ step) for i in range(count)])  4.13 us
    pallas_call x1, Pallas kernels, per_device_small(): pl.pallas_call(whole_kernel, out_shape=f32(nx, ny, nz), scratch_shapes=[p...  4.12 us
    all_gather x1, blocking collectives, per_device_small(): edges = lax.all_gather(edge, 'gz', axis=0)  2.09 us
  transfers between devices with their start and end apart: 10, of which 8 were waited for; matrix products, arithmetic and copies ran while one was open for 0% of the time, Pallas kernels for 0%

profile of v5, /device:TPU:0, one launch (start us, length us, event | category | flops | bytes accessed | tf_op | source)
XLA Modules:
  0.0 40.8 jit_solution(1459670635898852886)
XLA Ops:
  0.0 1.0 %pad_maximum_fusion.own = f32[4,8,16,128]{3,2,1,0:T(8,128)S(1)} fusion(f32[1,8,16,128]{3,2,1,0:T(8,128)} %bitcast.11, f32[1,8,16,128]{3,2,1,0:T(8,128)} %bitcast.12, f32[1,8,16,128]{3,2,1,0:T(8,128)} %bitcast.13, f32[1,8,16,128]{3,2,1,0:T(8,128)} %bitcast.14), kind=kLoop, calls=%fused_computation | loop fusion | flops 196608 | bytes 524288 | tf_op jit(solution)/shard_map/stack | solution.py:449
  1.0 3.1 %collective-permute-start = (f32[9,16,128]{2,1,0:T(8,128)S(1)}, f32[9,16,128]{2,1,0:T(8,128)S(1)}, u32[]{:S(2)}, u32[]{:S(2)}) collective-permute-start(f32[9,16,128]{2,1,0:T(8,128)S(1)} %get-tuple-element.14), channel_id=1, source_target_pairs={{0,8},{1,9},{8,0},{9,1},{16,24},{17,25},{24,16},{25,17},{2,10},{3,... | collective-permute-start | bytes 221192 | tf_op jit(solution)/shard_map/ppermute | solution.py:422
  4.1 0.0 collective-permute-start.1
  4.1 2.3 %collective-permute-done.s0 = f32[9,16,128]{2,1,0:T(8,128)S(1)} collective-permute-done((f32[9,16,128]{2,1,0:T(8,128)S(1)}, f32[9,16,128]{2,1,0:T(8,128)S(1)}, u32[]{:S(2)}, u32[]{:S(2)}) %collective-permute-start) | collective-permute-done | bytes 73760 | tf_op jit(solution)/shard_map/ppermute | solution.py:422
  6.4 0.0 collective-permute-done.1.s1
  6.4 0.1 slabs_y.1
  6.5 2.0 %collective-permute-start.2 = (f32[112,128]{1,0:T(8,128)S(1)}, f32[112,128]{1,0:T(8,128)S(1)}, u32[]{:S(2)}, u32[]{:S(2)}) collective-permute-start(f32[112,128]{1,0:T(8,128)S(1)} %get-tuple-element.16), channel_id=1, source_target_pairs={{0,2},{1,3},{2,0},{3,1},{4,6},{5,7},{6,4},{7,5},{8,10},{9,11},{10,... | collective-permute-start | bytes 172040 | tf_op jit(solution)/shard_map/ppermute | solution.py:422
  8.5 0.0 collective-permute-start.3
  8.5 2.5 %collective-permute-done.2.o0 = f32[112,128]{1,0:T(8,128)S(1)} collective-permute-done((f32[112,128]{1,0:T(8,128)S(1)}, f32[112,128]{1,0:T(8,128)S(1)}, u32[]{:S(2)}, u32[]{:S(2)}) %collective-permute-start.2) | collective-permute-done | bytes 57376 | tf_op jit(solution)/shard_map/ppermute | solution.py:422
  11.0 0.0 collective-permute-done.3.o1
  11.1 0.3 edges_z.1
  11.3 2.1 %all-gather = f32[24,32,128]{2,1,0:T(8,128)S(1)} all-gather(f32[12,32,128]{2,1,0:T(8,128)S(1)} %get-tuple-element.19), channel_id=2, replica_groups=mesh['gx'=4,'gy'=4,'gz'=2] {'gz'}, dimensions={0}, use_global_device_ids=true | all-gather | bytes 589824 | tf_op jit(solution)/shard_map/all_gather | solution.py:473
  13.4 0.7 %fine.1 = (f32[8,16,128]{2,1,0:T(8,128)S(1)}, f32[6,8,16,128]{3,2,1,0:T(8,128)S(1)}, f32[2,4,8,128]{3,2,1,0:T(8,128)S(1)}) custom-call(f32[4,14,32,128]{3,2,1,0:T(8,128)S(1)} %get-tuple-element.18.local, f32[2,12,32,128]{3,2,1,0:T(8,128)S(1)} %bitcast.7), custom_call_target="tpu_custom_call" | custom-call | tf_op jit(solution)/shard_map/fine/pallas_call | solution.py:476
  14.2 3.3 %collective-permute-start.4 = (f32[1,2,4,8,128]{4,3,2,1,0:T(8,128)S(1)}, f32[1,2,4,8,128]{4,3,2,1,0:T(8,128)S(1)}, u32[]{:S(2)}, u32[]{:S(2)}) collective-permute-start(f32[1,2,4,8,128]{4,3,2,1,0:T(8,128)S(1)} %bitcast.8), channel_id=1, source_target_pairs={{0,8},{8,0},{16,24},{24,16},{1,9},{9,1},{17,25},{25,17},{2,10},{10... | collective-permute-start | bytes 98312 | tf_op jit(solution)/shard_map/ppermute | solution.py:436
  17.5 1.9 %collective-permute-done.4 = f32[1,2,4,8,128]{4,3,2,1,0:T(8,128)S(1)} collective-permute-done((f32[1,2,4,8,128]{4,3,2,1,0:T(8,128)S(1)}, f32[1,2,4,8,128]{4,3,2,1,0:T(8,128)S(1)}, u32[]{:S(2)}, u32[]{:S(2)}) %collective-permute-start.4) | collective-permute-done | bytes 32800 | tf_op jit(solution)/shard_map/ppermute | solution.py:436
  19.4 3.4 %collective-permute-start.5 = (f32[2,2,4,8,128]{4,3,2,1,0:T(8,128)S(1)}, f32[2,2,4,8,128]{4,3,2,1,0:T(8,128)S(1)}, u32[]{:S(2)}, u32[]{:S(2)}) collective-permute-start(f32[2,2,4,8,128]{4,3,2,1,0:T(8,128)S(1)} %pad_maximum_fusion.2), channel_id=1, source_target_pairs={{0,16},{8,24},{16,0},{24,8},{1,17},{9,25},{17,1},{25,9},{2,18},{10... | collective-permute-start | bytes 196616 | tf_op jit(solution)/shard_map/ppermute | solution.py:436
  22.8 2.2 %collective-permute-done.5 = f32[2,2,4,8,128]{4,3,2,1,0:T(8,128)S(1)} collective-permute-done((f32[2,2,4,8,128]{4,3,2,1,0:T(8,128)S(1)}, f32[2,2,4,8,128]{4,3,2,1,0:T(8,128)S(1)}, u32[]{:S(2)}, u32[]{:S(2)}) %collective-permute-start.5) | collective-permute-done | bytes 65568 | tf_op jit(solution)/shard_map/ppermute | solution.py:436
  25.1 2.8 %collective-permute-start.6 = (f32[4,2,4,8,128]{4,3,2,1,0:T(8,128)S(1)}, f32[4,2,4,8,128]{4,3,2,1,0:T(8,128)S(1)}, u32[]{:S(2)}, u32[]{:S(2)}) collective-permute-start(f32[4,2,4,8,128]{4,3,2,1,0:T(8,128)S(1)} %pad_maximum_fusion.1), channel_id=1, source_target_pairs={{0,2},{2,0},{4,6},{6,4},{1,3},{3,1},{5,7},{7,5},{8,10},{10,8},{12,... | collective-permute-start | bytes 393224 | tf_op jit(solution)/shard_map/ppermute | solution.py:428
  27.8 0.9 %collective-permute-start.7 = (f32[4,2,4,8,128]{4,3,2,1,0:T(8,128)S(1)}, f32[4,2,4,8,128]{4,3,2,1,0:T(8,128)S(1)}, u32[]{:S(2)}, u32[]{:S(2)}) collective-permute-start(f32[4,2,4,8,128]{4,3,2,1,0:T(8,128)S(1)} %pad_maximum_fusion.1), channel_id=1, source_target_pairs={{0,4},{2,6},{4,0},{6,2},{1,5},{3,7},{5,1},{7,3},{8,12},{10,14},{12... | collective-permute-start | bytes 393224 | tf_op jit(solution)/shard_map/ppermute | solution.py:428
  28.8 1.4 %collective-permute-start.8 = (f32[4,2,4,8,128]{4,3,2,1,0:T(8,128)S(1)}, f32[4,2,4,8,128]{4,3,2,1,0:T(8,128)S(1)}, u32[]{:S(2)}, u32[]{:S(2)}) collective-permute-start(f32[4,2,4,8,128]{4,3,2,1,0:T(8,128)S(1)} %pad_maximum_fusion.1), channel_id=1, source_target_pairs={{0,6},{2,4},{4,2},{6,0},{1,7},{3,5},{5,3},{7,1},{8,14},{10,12},{12... | collective-permute-start | bytes 393224 | tf_op jit(solution)/shard_map/ppermute | solution.py:428
  30.2 1.9 %collective-permute-done.6 = f32[4,2,4,8,128]{4,3,2,1,0:T(8,128)S(1)} collective-permute-done((f32[4,2,4,8,128]{4,3,2,1,0:T(8,128)S(1)}, f32[4,2,4,8,128]{4,3,2,1,0:T(8,128)S(1)}, u32[]{:S(2)}, u32[]{:S(2)}) %collective-permute-start.6) | collective-permute-done | bytes 131104 | tf_op jit(solution)/shard_map/ppermute | solution.py:428
  32.1 0.9 %collective-permute-done.7 = f32[4,2,4,8,128]{4,3,2,1,0:T(8,128)S(1)} collective-permute-done((f32[4,2,4,8,128]{4,3,2,1,0:T(8,128)S(1)}, f32[4,2,4,8,128]{4,3,2,1,0:T(8,128)S(1)}, u32[]{:S(2)}, u32[]{:S(2)}) %collective-permute-start.7) | collective-permute-done | bytes 131104 | tf_op jit(solution)/shard_map/ppermute | solution.py:428
  33.1 1.6 %collective-permute-done.8 = f32[4,2,4,8,128]{4,3,2,1,0:T(8,128)S(1)} collective-permute-done((f32[4,2,4,8,128]{4,3,2,1,0:T(8,128)S(1)}, f32[4,2,4,8,128]{4,3,2,1,0:T(8,128)S(1)}, u32[]{:S(2)}, u32[]{:S(2)}) %collective-permute-start.8) | collective-permute-done | bytes 131104 | tf_op jit(solution)/shard_map/ppermute | solution.py:428
  34.7 0.1 collective-permute-start.9
  34.7 1.9 %collective-permute-done.9.there = f32[16,2,4,8,128]{4,3,2,1,0:T(8,128)S(1)} collective-permute-done((f32[16,2,4,8,128]{4,3,2,1,0:T(8,128)S(1)}, f32[16,2,4,8,128]{4,3,2,1,0:T(8,128)S(1)}, u32[]{:S(2)}, u32[]{:S(2)}) %collective-permute-start.9) | collective-permute-done | bytes 524320 | tf_op jit(solution)/shard_map/ppermute | solution.py:491
  36.6 4.1 %whole.1 = f32[8,16,128]{2,1,0:T(8,128)} custom-call(f32[16,2,4,8,128]{4,3,2,1,0:T(8,128)S(1)} %constant_dynamic-update-slice_fusion.here, f32[16,2,4,8,128]{4,3,2,1,0:T(8,128)S(1)} %collective-permute-done.9.there, f32[8,16,128]{2,1,0:T(8,128)S(1)} %get-tuple-element.21.t_in, f32[6,8,16,128]{3,2,1,0:T(8,128)S(1)} %get-tuple-element.22.k_in), custom_call_target="tpu_custom_call" | custom-call | tf_op jit(solution)/shard_map/whole/pallas_call | solution.py:494
  (9 shorter events, 0.1 us)
Async XLA Ops:
  1.0 5.5 %collective-permute-start = (f32[9,16,128]{2,1,0:T(8,128)S(1)}, f32[9,16,128]{2,1,0:T(8,128)S(1)}, u32[]{:S(2)}, u32[]{:S(2)}) collective-permute-start(f32[9,16,128]{2,1,0:T(8,128)S(1)} %get-tuple-element.14), channel_id=1, source_target_pairs={{0,8},{1,9},{8,0},{9,1},{16,24},{17,25},{24,16},{25,17},{2,10},{3,... | collective-permute-start | bytes 221192 | tf_op jit(solution)/shard_map/ppermute | solution.py:422
  4.1 2.3 %collective-permute-start.1 = (f32[9,16,128]{2,1,0:T(8,128)S(1)}, f32[9,16,128]{2,1,0:T(8,128)S(1)}, u32[]{:S(2)}, u32[]{:S(2)}) collective-permute-start(f32[9,16,128]{2,1,0:T(8,128)S(1)} %get-tuple-element.15), channel_id=1, source_target_pairs={{0,1},{1,0},{8,16},{9,17},{16,8},{17,9},{24,25},{25,24},{2,3},{3,2... | collective-permute-start | bytes 221192 | tf_op jit(solution)/shard_map/ppermute | solution.py:422
  6.5 4.5 %collective-permute-start.2 = (f32[112,128]{1,0:T(8,128)S(1)}, f32[112,128]{1,0:T(8,128)S(1)}, u32[]{:S(2)}, u32[]{:S(2)}) collective-permute-start(f32[112,128]{1,0:T(8,128)S(1)} %get-tuple-element.16), channel_id=1, source_target_pairs={{0,2},{1,3},{2,0},{3,1},{4,6},{5,7},{6,4},{7,5},{8,10},{9,11},{10,... | collective-permute-start | bytes 172040 | tf_op jit(solution)/shard_map/ppermute | solution.py:422
  8.5 2.5 %collective-permute-start.3 = (f32[112,128]{1,0:T(8,128)S(1)}, f32[112,128]{1,0:T(8,128)S(1)}, u32[]{:S(2)}, u32[]{:S(2)}) collective-permute-start(f32[112,128]{1,0:T(8,128)S(1)} %get-tuple-element.17), channel_id=1, source_target_pairs={{0,1},{1,0},{2,4},{3,5},{4,2},{5,3},{6,7},{7,6},{8,9},{9,8},{10,12... | collective-permute-start | bytes 172040 | tf_op jit(solution)/shard_map/ppermute | solution.py:422
  14.2 5.2 %collective-permute-start.4 = (f32[1,2,4,8,128]{4,3,2,1,0:T(8,128)S(1)}, f32[1,2,4,8,128]{4,3,2,1,0:T(8,128)S(1)}, u32[]{:S(2)}, u32[]{:S(2)}) collective-permute-start(f32[1,2,4,8,128]{4,3,2,1,0:T(8,128)S(1)} %bitcast.8), channel_id=1, source_target_pairs={{0,8},{8,0},{16,24},{24,16},{1,9},{9,1},{17,25},{25,17},{2,10},{10... | collective-permute-start | bytes 98312 | tf_op jit(solution)/shard_map/ppermute | solution.py:436
  19.4 5.6 %collective-permute-start.5 = (f32[2,2,4,8,128]{4,3,2,1,0:T(8,128)S(1)}, f32[2,2,4,8,128]{4,3,2,1,0:T(8,128)S(1)}, u32[]{:S(2)}, u32[]{:S(2)}) collective-permute-start(f32[2,2,4,8,128]{4,3,2,1,0:T(8,128)S(1)} %pad_maximum_fusion.2), channel_id=1, source_target_pairs={{0,16},{8,24},{16,0},{24,8},{1,17},{9,25},{17,1},{25,9},{2,18},{10... | collective-permute-start | bytes 196616 | tf_op jit(solution)/shard_map/ppermute | solution.py:436
  25.1 7.0 %collective-permute-start.6 = (f32[4,2,4,8,128]{4,3,2,1,0:T(8,128)S(1)}, f32[4,2,4,8,128]{4,3,2,1,0:T(8,128)S(1)}, u32[]{:S(2)}, u32[]{:S(2)}) collective-permute-start(f32[4,2,4,8,128]{4,3,2,1,0:T(8,128)S(1)} %pad_maximum_fusion.1), channel_id=1, source_target_pairs={{0,2},{2,0},{4,6},{6,4},{1,3},{3,1},{5,7},{7,5},{8,10},{10,8},{12,... | collective-permute-start | bytes 393224 | tf_op jit(solution)/shard_map/ppermute | solution.py:428
  27.8 5.2 %collective-permute-start.7 = (f32[4,2,4,8,128]{4,3,2,1,0:T(8,128)S(1)}, f32[4,2,4,8,128]{4,3,2,1,0:T(8,128)S(1)}, u32[]{:S(2)}, u32[]{:S(2)}) collective-permute-start(f32[4,2,4,8,128]{4,3,2,1,0:T(8,128)S(1)} %pad_maximum_fusion.1), channel_id=1, source_target_pairs={{0,4},{2,6},{4,0},{6,2},{1,5},{3,7},{5,1},{7,3},{8,12},{10,14},{12... | collective-permute-start | bytes 393224 | tf_op jit(solution)/shard_map/ppermute | solution.py:428
  28.8 5.9 %collective-permute-start.8 = (f32[4,2,4,8,128]{4,3,2,1,0:T(8,128)S(1)}, f32[4,2,4,8,128]{4,3,2,1,0:T(8,128)S(1)}, u32[]{:S(2)}, u32[]{:S(2)}) collective-permute-start(f32[4,2,4,8,128]{4,3,2,1,0:T(8,128)S(1)} %pad_maximum_fusion.1), channel_id=1, source_target_pairs={{0,6},{2,4},{4,2},{6,0},{1,7},{3,5},{5,3},{7,1},{8,14},{10,12},{12... | collective-permute-start | bytes 393224 | tf_op jit(solution)/shard_map/ppermute | solution.py:428
  34.7 2.0 %collective-permute-start.9 = (f32[16,2,4,8,128]{4,3,2,1,0:T(8,128)S(1)}, f32[16,2,4,8,128]{4,3,2,1,0:T(8,128)S(1)}, u32[]{:S(2)}, u32[]{:S(2)}) collective-permute-start(f32[16,2,4,8,128]{4,3,2,1,0:T(8,128)S(1)} %constant_dynamic-update-slice_fusion.here), channel_id=1, source_target_pairs={{0,1},{1,0},{2,3},{3,2},{4,5},{5,4},{6,7},{7,6},{8,9},{9,8},{10,11... | collective-permute-start | bytes 1572872 | tf_op jit(solution)/shard_map/ppermute | solution.py:491

commit v6 on v5

--- a/solution.py
+++ b/solution.py
@@ -15,6 +15,7 @@
 
 REACH = 3
 TILE = 8
+PAD = 4
 PARAMS = pltpu.CompilerParams(vmem_limit_bytes=16 * 2**20)
 
 
@@ -97,8 +98,8 @@
     nx, ny, nz = own.shape[1:]
     gz = lax.axis_index("gz")
     sides_x((s0, s1), before, behind)
-    zero = jnp.zeros((TILE, nz), jnp.float32)
-    empty = jnp.zeros((ny + 2 * TILE, nz), jnp.float32)
+    zero = jnp.zeros((PAD, nz), jnp.float32)
+    empty = jnp.zeros((ny + 2 * PAD, nz), jnp.float32)
     for a in range(4):
         for p in range(nx + 2 * REACH):
             q = p - REACH
@@ -113,19 +114,19 @@
             else:
                 ext[a, p] = empty
                 continue
-            ext[a, p, :TILE] = zero
-            ext[a, p, TILE + ny :] = zero
-            ext[a, p, TILE : TILE + ny] = v
-    for (even, keep), r in zip(side("gy"), (TILE - 2, TILE + ny)):
+            ext[a, p, :PAD] = zero
+            ext[a, p, PAD + ny :] = zero
+            ext[a, p, PAD : PAD + ny] = v
+    for (even, keep), r in zip(side("gy"), (PAD - 2, PAD + ny)):
         lines[...] = keep * jnp.where(even, o0[...], o1[...])
         for p in range(nx + 4):
             for a in range(4):
                 at = (a * (nx + 4) + p) * 2
                 ext[a, 1 + p, r : r + 2] = lines[at : at + 2]
-            if r > TILE:
+            if r > PAD:
                 at = 8 * (nx + 4) + p
                 ext[2, 1 + p, r + 2 : r + 3] = lines[at : at + 1]
-    lane = iota((ny + 2 * TILE, nz), 1)
+    lane = iota((ny + 2 * PAD, nz), 1)
     for p in range(nx + 4):
         packed = ext[0, 1 + p]
         for a in range(1, 4):
@@ -139,24 +140,24 @@
     nx, ny, half = t_out.shape
     nz = 2 * half
     gx, gy, gz = lax.axis_index("gx"), lax.axis_index("gy"), lax.axis_index("gz")
-    spot = iota((ny + 2 * TILE, half), 1)
+    spot = iota((ny + 2 * PAD, half), 1)
     given = jnp.logical_or((gz == 0) & (spot < 3), (gz == 1) & (spot >= half - 3))
     for p in range(nx + 2 * REACH):
         for a in range(4):
             ext[a, p, :, :half] = local[a, p]
             if 1 <= p < nx + 5:
-                v = edges[1 - gz, p - 1]
+                v = edges[p - 1]
                 if a > 0:
                     v = pltpu.roll(v, jnp.where(gz == 0, half - 3 * a, 3 * a), 1)
                 ext[a, p, :, half:] = jnp.where(given, v, 0.0)
             else:
-                ext[a, p, :, half:] = jnp.zeros((ny + 2 * TILE, half), jnp.float32)
-    shape = (ny + 2 * TILE, nz)
+                ext[a, p, :, half:] = jnp.zeros((ny + 2 * PAD, half), jnp.float32)
+    shape = (ny + 2 * PAD, nz)
     row, lane = iota(shape, 0), iota(shape, 1)
     inner_z = jnp.logical_or(lane > 0, gz > 0)
     in_y = jnp.logical_and(
-        jnp.logical_or(gy > 0, row >= TILE),
-        jnp.logical_or(gy < lax.axis_size("gy") - 1, row < TILE + ny),
+        jnp.logical_or(gy > 0, row >= PAD),
+        jnp.logical_or(gy < lax.axis_size("gy") - 1, row < PAD + ny),
     )
 
     def off(e, p):
@@ -182,7 +183,7 @@
         e2[p] = jnp.where(inside, value, 0.0)
 
     def mine(v):
-        return v[TILE : TILE + ny, :half]
+        return v[PAD : PAD + ny, :half]
 
     sums = []
     for i in range(nx):
@@ -195,7 +196,7 @@
             k_out[n, i] = mine(inv * k)
         sums.append(mine(q))
     def face(d, i):
-        return 0.5 * ext[d, REACH + i, TILE : TILE + ny, :half]
+        return 0.5 * ext[d, REACH + i, PAD : PAD + ny, :half]
 
     pairs = range(0, nx, 2)
     fine, coarse = iota((half, half), 0), iota((half, half), 1)
@@ -256,25 +257,29 @@
     return [v + (1.0 - damping) * k + r * o for v, k, r, o in zip(t, c, inv, off(c))]
 
 
-def coarse_solution(rhs, fx, fy, fz, depth):
-    shape = rhs.shape
-    row, lane = iota(shape, 0), iota(shape, 1)
+def coarse_operator(fx, fy, fz, depth):
+    row, lane = iota(fx.shape, 0), iota(fx.shape, 1)
     fxm = jnp.where(lane >= depth, fx, 0.0)
     fym = jnp.where(row > 0, fy, 0.0)
     fzm = jnp.where(lane % depth > 0, fz, 0.0)
-    wide = shape[1]
+    wide = fx.shape[1]
 
     def up_x(v):
         return pltpu.roll(v, wide - depth, 1)
 
     hx, hy, hz = up_x(fxm), up(fym, 0), up(fzm, 1)
-    diagonal = fx + hx + fy + hy + fz + hz
+    diagonal = (fx + hx) + (fy + hy) + (fz + hz)
 
     def operate_packed(v):
-        result = diagonal * v - fxm * pltpu.roll(v, depth, 1) - hx * up_x(v)
-        result = result - fym * down(v, 0) - hy * up(v, 0)
-        return result - fzm * down(v, 1) - hz * up(v, 1)
-
+        along_x = fxm * pltpu.roll(v, depth, 1) + hx * up_x(v)
+        along_y = fym * down(v, 0) + hy * up(v, 0)
+        along_z = fzm * down(v, 1) + hz * up(v, 1)
+        return (diagonal * v - along_y) - (along_x + along_z)
+
+    return operate_packed
+
+
+def coarse_solution(rhs, operate_packed):
     def total(v):
         v = jnp.broadcast_to(jnp.sum(v, axis=1, keepdims=True), v.shape)
         for shift in (4, 2, 1):
@@ -287,10 +292,11 @@
     alpha = norm_now / energy
     solution = alpha * search
     for step in range(COARSE_ITERS - 1):
+        inverse_norm = 1.0 / norm_now
         remain = remain - alpha * image
         across = operate_packed(remain)
         norm_next, own, mixed = total(remain * remain), total(remain * across), total(remain * image)
-        beta = norm_next / norm_now
+        beta = norm_next * inverse_norm
         energy = own + beta * (2.0 * mixed + beta * energy)
         search = remain + beta * search
         image = across + beta * image
@@ -300,7 +306,14 @@
     return solution
 
 
-def whole_kernel(here, there, t_in, k_in, out, grid, fold1, fold2, spread2, window, doubled):
+def mirrored(k, count):
+    result = 0
+    while count > 1:
+        result, k, count = 2 * result + k % 2, k // 2, count // 2
+    return result
+
+
+def whole_kernel(here, there, t_in, k_in, out, grid, fold1, folds1, fold2, folds2, spread2, held2, spread1, kept, doubled):
     gx, gy, gz = lax.axis_index("gx"), lax.axis_index("gy"), lax.axis_index("gz")
     cx, cy = lax.axis_size("gx"), lax.axis_size("gy")
     bx, by = here.shape[2], here.shape[3]
@@ -308,64 +321,74 @@
     for k in range(cx * cy):
         x = jnp.bitwise_xor(gx, k % cx) * bx
         y = pl.multiple_of(jnp.bitwise_xor(gy, k // cx) * by, by)
+        other = mirrored(k % cx, cx) + k // cx * cx
         for a in range(2):
             low = jnp.where(gz == 0, here[k, a], there[k, a]).reshape(bx * by, w1)
-            top = jnp.where(gz == 0, there[k, a], here[k, a]).reshape(bx * by, w1)
+            top = jnp.where(gz == 0, there[other, a], here[other, a]).reshape(bx * by, w1)
             left = iota((bx * by, w1), 1) < w1 // 2
             one = jnp.where(left, low, pltpu.roll(top, w1 // 2, 1))
             two = jnp.where(left, pltpu.roll(low, w1 // 2, 1), top)
-            grid[2 * a, pl.ds(x, bx), pl.ds(y, by), :] = one.reshape(bx, by, w1)
-            grid[2 * a + 1, pl.ds(x, bx), pl.ds(y, by), :] = two.reshape(bx, by, w1)
-    n1, m1, w1 = grid.shape[1:]
-    b1, fx1, fy1, fz1 = (planes_of(grid.at[a]) for a in range(4))
-    diagonal1, inv1, off1 = level_parts(fx1, fy1, fz1)
-    t1, q1 = before(b1, diagonal1, inv1, off1)
-
+            spot = (pl.ds(x + 2, bx), pl.ds(y + TILE, by))
+            grid[(2 * a, *spot)] = one.reshape(bx, by, w1)
+            grid[(2 * a + 1, *spot)] = two.reshape(bx, by, w1)
+    n1, m1 = cx * bx, cy * by
+    inner = slice(TILE, TILE + m1)
+    for ref in (grid.at[1], grid.at[2], grid.at[3], kept.at[0], kept.at[1]):
+        for p in range(n1 + 4):
+            if p < 2 or p >= n1 + 2:
+                ref[p] = jnp.zeros((m1 + 2 * TILE, w1), jnp.float32)
+            else:
+                ref[p, :TILE] = jnp.zeros((TILE, w1), jnp.float32)
+                ref[p, TILE + m1 :] = jnp.zeros((TILE, w1), jnp.float32)
+    b1, fx1, fy1, fz1 = ([grid[a, 2 + p, inner] for p in range(n1)] for a in range(4))
     n2, m2 = n1 // 2, m1 // 2
+    half = n2 * m2
     pairs = range(0, n1, 2)
-    fold1[...] = jnp.concatenate(
-        [q1[i] + q1[i + 1] for i in pairs]
-        + [0.5 * fx1[i] for i in pairs]
+    folds1[...] = jnp.concatenate(
+        [0.5 * fx1[i] for i in pairs]
         + [0.5 * (fy1[i] + fy1[i + 1]) for i in pairs]
         + [0.5 * (fz1[i] + fz1[i + 1]) for i in pairs],
         0,
     )
-    half = n2 * m2
-    low = fold1[pl.ds(0, 4 * half, stride=2)]
-    top = fold1[pl.ds(1, 4 * half, stride=2)]
     fine, coarse = iota((w1, w1), 0), iota((w1, w1), 1)
-    both, even = chosen(fine // 2 == coarse), chosen(fine == 2 * coarse)
-    summed = jnp.concatenate([low[: 2 * half] + top[: 2 * half], low[2 * half : 3 * half]], 0)
-    summed = select_dot(summed, both)
+    both1, even = chosen(fine // 2 == coarse), chosen(fine == 2 * coarse)
+    low, top = folds1[pl.ds(0, 3 * half, stride=2)], folds1[pl.ds(1, 3 * half, stride=2)]
+    summed = select_dot(jnp.concatenate([low[:half] + top[:half], low[half : 2 * half]], 0), both1)
 
     def part(v):
         return [v[p * m2 : (p + 1) * m2] for p in range(n2)]
 
-    b2, fx2, fy2 = (part(summed[i * half : (i + 1) * half]) for i in range(3))
-    fz2 = part(select_dot(low[3 * half :] + top[3 * half :], even))
+    fx2, fy2 = part(summed[:half]), part(summed[half:])
+    fz2 = part(select_dot(low[2 * half :] + top[2 * half :], even))
+    diagonal1, inv1, off1 = level_parts(fx1, fy1, fz1)
+    t1, q1 = before(b1, diagonal1, inv1, off1)
+    for p in range(n1):
+        kept[0, 2 + p, inner] = t1[p]
+        kept[1, 2 + p, inner] = inv1[p]
     diagonal2, inv2, off2 = level_parts(fx2, fy2, fz2)
-    t2, q2 = before(b2, diagonal2, inv2, off2)
 
     n3, m3 = n2 // 2, m2 // 2
     depth = w1 // n3
     fine, coarse = iota((n3 * w1, w1), 0), iota((n3 * w1, w1), 1)
     block, fine = fine // w1, fine % w1
-    both = chosen((fine // 2 + block * depth == coarse) & (fine < 2 * depth))
+    both2 = chosen((fine // 2 + block * depth == coarse) & (fine < 2 * depth))
     even = chosen((fine + 2 * block * depth == 2 * coarse) & (fine < 2 * depth))
     blocks = range(0, n2, 2)
     wide = [
-        jnp.concatenate([q2[i] + q2[i + 1] for i in blocks], 1),
         jnp.concatenate([0.5 * fx2[i] for i in blocks], 1),
         jnp.concatenate([0.5 * (fy2[i] + fy2[i + 1]) for i in blocks], 1),
     ]
     thin = jnp.concatenate([0.5 * (fz2[i] + fz2[i + 1]) for i in blocks], 1)
-    packed = [select_dot(jnp.concatenate(wide, 0), both), select_dot(thin, even)]
-    fold2[...] = jnp.concatenate(packed, 0)
-    low = fold2[pl.ds(0, 4 * m3, stride=2)]
-    top = fold2[pl.ds(1, 4 * m3, stride=2)]
-    b3, fx3 = low[:m3] + top[:m3], low[m3 : 2 * m3] + top[m3 : 2 * m3]
-    fy3, fz3 = low[2 * m3 : 3 * m3], low[3 * m3 :] + top[3 * m3 :]
-    c3 = coarse_solution(b3, fx3, fy3, fz3, depth)
+    folds2[: 2 * m2] = select_dot(jnp.concatenate(wide, 0), both2)
+    folds2[2 * m2 :] = select_dot(thin, even)
+    low, top = folds2[pl.ds(0, 3 * m3, stride=2)], folds2[pl.ds(1, 3 * m3, stride=2)]
+    operate3 = coarse_operator(low[:m3] + top[:m3], low[m3 : 2 * m3], low[2 * m3 :] + top[2 * m3 :], depth)
+
+    fold1[...] = jnp.concatenate([q1[i] + q1[i + 1] for i in pairs], 0)
+    b2 = part(select_dot(fold1[pl.ds(0, half, stride=2)] + fold1[pl.ds(1, half, stride=2)], both1))
+    t2, q2 = before(b2, diagonal2, inv2, off2)
+    fold2[...] = select_dot(jnp.concatenate([q2[i] + q2[i + 1] for i in blocks], 1), both2)
+    c3 = coarse_solution(fold2[pl.ds(0, m3, stride=2)] + fold2[pl.ds(1, m3, stride=2)], operate3)
 
     fine, coarse = iota((w1, n3 * w1), 1), iota((w1, n3 * w1), 0)
     block, fine = fine // w1, fine % w1
@@ -376,30 +399,43 @@
     up2 = [spread2[(p // 2) * m2 : (p // 2 + 1) * m2] for p in range(n2)]
     c2 = after(t2, up2, inv2, off2)
 
+    held2[0] = jnp.zeros((m2, w1), jnp.float32)
+    held2[n2 + 1] = jnp.zeros((m2, w1), jnp.float32)
+    for p in range(n2):
+        held2[1 + p] = c2[p]
+    few = bx // 2 + 2
+    near = held2[pl.ds(gx * (bx // 2), few)].reshape(few * m2, w1)
     fine, coarse = iota((w1, w1), 1), iota((w1, w1), 0)
-    row = select_dot(jnp.concatenate(c2, 0), chosen(fine // 2 == coarse))
-    fold1[pl.ds(0, half, stride=2)] = row
-    fold1[pl.ds(1, half, stride=2)] = row
-    up1 = [fold1[(p // 2) * m1 : (p // 2 + 1) * m1] for p in range(n1)]
-    c1 = after(t1, up1, inv1, off1)
-
-    window[...] = jnp.zeros_like(window)
-    for p in range(n1):
-        window[1 + p, TILE : TILE + m1, :] = c1[p]
-    y = pl.multiple_of(gy * by, by)
-    near = window[pl.ds(gx * bx, bx + 2), pl.ds(y, by + 2 * TILE), :]
+    row = select_dot(near, chosen(fine // 2 == coarse))
+    for p in range(few):
+        spread1[p, :TILE] = jnp.zeros((TILE, w1), jnp.float32)
+        spread1[p, TILE + m1 :] = jnp.zeros((TILE, w1), jnp.float32)
+        spread1[p, pl.ds(TILE, m2, stride=2)] = row[p * m2 : (p + 1) * m2]
+        spread1[p, pl.ds(TILE + 1, m2, stride=2)] = row[p * m2 : (p + 1) * m2]
     tall = by + 2 * TILE
-    near = near.reshape((bx + 2) * tall, w1)
+    rows = pl.ds(pl.multiple_of(gy * by, by), tall)
+    inner_z = iota((tall, w1), 1) > 0
+    up1 = [spread1[p, rows] for p in range(few)]
+    near = []
+    for p in range(1, bx + 3):
+        x = gx * bx + p
+        e = up1[p // 2]
+        fy, fz = grid[2, x, rows], jnp.where(inner_z, grid[3, x, rows], 0.0)
+        total = grid[1, x, rows] * up1[(p - 1) // 2] + grid[1, x + 1, rows] * up1[(p + 1) // 2]
+        total = total + fy * down(e, 0) + up(fy * e, 0) + fz * down(e, 1) + up(fz * e, 1)
+        value = kept[0, x, rows] + (1.0 - damping) * e + kept[1, x, rows] * total
+        near.append(value[TILE - 1 : TILE - 1 + by + TILE])
+    tall = by + TILE
     spot = gz * t_in.shape[2] + iota((w1, 3 * w1), 1) % w1 + (iota((w1, 3 * w1), 1) // w1 + 1) % 3 - 1
     wanted = iota((w1, 3 * w1), 0)
-    row = select_dot(near, chosen((2 * wanted == spot) | (2 * wanted + 1 == spot)))
+    row = select_dot(jnp.concatenate(near, 0), chosen((2 * wanted == spot) | (2 * wanted + 1 == spot)))
     for s in range(3):
         doubled[s, pl.ds(0, (bx + 2) * tall, stride=2)] = row[:, s * w1 : (s + 1) * w1]
         doubled[s, pl.ds(1, (bx + 2) * tall, stride=2)] = row[:, s * w1 : (s + 1) * w1]
     ny = t_in.shape[1]
 
     def at(s, i, shift):
-        first = (1 + i // 2) * 2 * tall + 2 * TILE + shift
+        first = (1 + i // 2) * 2 * tall + 2 + shift
         return doubled[s, first : first + ny]
 
     for i in range(t_in.shape[0]):
@@ -430,12 +466,11 @@
 
 
 def doubled_over(block, axis):
-    count = lax.axis_size(axis)
-    step = 1
-    while step < count:
-        other = lax.ppermute(block, axis, [(i, i ^ step) for i in range(count)])
-        block = jnp.concatenate([block, other], 0)
-        step *= 2
+    count, cores = lax.axis_size(axis), lax.axis_size("gz")
+    steps = [1 << n for n in range(count.bit_length() - 1)]
+    for up_step, down_step in zip(steps, reversed(steps)):
+        route = [(i * cores + c, (i ^ (down_step if c else up_step)) * cores + c) for i in range(count) for c in range(cores)]
+        block = jnp.concatenate([block, lax.ppermute(block, (axis, "gz"), route)], 0)
     return block
 
 
@@ -465,13 +500,13 @@
     lines = traded(lines, "gy")
     local, edge = pl.pallas_call(
         z_kernel,
-        out_shape=(f32(4, nx + 2 * REACH, ny + 2 * TILE, nz), f32(nx + 4, ny + 2 * TILE, nz)),
+        out_shape=(f32(4, nx + 2 * REACH, ny + 2 * PAD, nz), f32(nx + 4, ny + 2 * PAD, nz)),
         scratch_shapes=near + [pltpu.VMEM((count, nz), jnp.float32)],
         compiler_params=PARAMS,
         name="edges_z",
     )(own, *slabs, *lines)
-    edges = lax.all_gather(edge, "gz", axis=0)
-    ext_x, ext_y, wide = nx + 2 * REACH, ny + 2 * TILE, 2 * nz
+    edges = lax.ppermute(edge, "gz", [(0, 1), (1, 0)])
+    ext_x, ext_y, wide = nx + 2 * REACH, ny + 2 * PAD, 2 * nz
     field = pltpu.VMEM((ext_x, ext_y, wide), jnp.float32)
     t, k, m = pl.pallas_call(
         fine_kernel,
@@ -490,16 +525,21 @@
     here = gathered(doubled_over(m[None], "gx"), "gy")
     there = lax.ppermute(here, "gz", [(0, 1), (1, 0)])
     n1, m1 = here.shape[2] * lax.axis_size("gx"), here.shape[3] * lax.axis_size("gy")
-    tall = (nx // 2 + 2) * (ny // 2 + 2 * TILE)
+    n2, m2 = n1 // 2, m1 // 2
+    tall = (nx // 2 + 2) * (ny // 2 + TILE)
     return pl.pallas_call(
         whole_kernel,
         out_shape=f32(nx, ny, nz),
         scratch_shapes=[
-            pltpu.VMEM((4, n1, m1, nz), jnp.float32),
-            pltpu.VMEM((2 * n1 * m1, nz), jnp.float32),
-            pltpu.VMEM((2 * m1, nz), jnp.float32),
+            pltpu.VMEM((4, n1 + 4, m1 + 2 * TILE, nz), jnp.float32),
+            pltpu.VMEM((n2 * m1, nz), jnp.float32),
+            pltpu.VMEM((3 * n2 * m1, nz), jnp.float32),
+            pltpu.VMEM((m2, nz), jnp.float32),
+            pltpu.VMEM((3 * m2, nz), jnp.float32),
             pltpu.VMEM((n1 * m1 // 8, nz), jnp.float32),
-            pltpu.VMEM((n1 + 2, m1 + 2 * TILE, nz), jnp.float32),
+            pltpu.VMEM((n2 + 2, m2, nz), jnp.float32),
+            pltpu.VMEM((nx // 4 + 2, m1 + 2 * TILE, nz), jnp.float32),
+            pltpu.VMEM((2, n1 + 4, m1 + 2 * TILE, nz), jnp.float32),
             pltpu.VMEM((3, 2 * tall, nz), jnp.float32),
         ],
         compiler_params=PARAMS,

time: 40.9 us -> 40 us (0.978)
  blocking collectives: 2.09 us -> 0 us
  waiting for transfers between devices: 15.3 us -> 16.7 us
    all_gather x1 -> x0, blocking collectives: 2.09 us -> none  [per_device_small(): edges = lax.all_gather(edge, 'gz', axis=0)]
    ppermute x2 -> x3, waiting for transfers between devices: 4.13 us -> 5.49 us  [the longest x2 4.13 us: doubled_over(): lax.ppermute(block, (axis, 'gz'), route)]
    ppermute x2 -> x3, starting transfers between devices: 6.74 us -> 6.83 us  [the longest x2 6.76 us: doubled_over(): lax.ppermute(block, (axis, 'gz'), route)]
  transfers between devices with their start and end apart: 10 -> 11, of which waited for: 8 -> 9; matrix products, arithmetic and copies ran while one was open for 0% -> 0% of each run, Pallas kernels for 0% -> 0%
where the time goes in v6:
time: 40 us; the launch traced here: 39.9 us
  starting transfers between devices  17.1 us (43%)
  waiting for transfers between devices  16.7 us (42%)
  Pallas kernels  4.96 us (12%)
  other arithmetic  0.97 us (2%)
    ppermute x2, starting transfers between devices, doubled_over(): lax.ppermute(block, (axis, 'gz'), route)  6.76 us
    ppermute x4, starting transfers between devices, traded(): taken.append(lax.ppermute(block, (axis, 'gz'), route))  5.12 us
    ppermute x3, starting transfers between devices, gathered(): lax.ppermute(block, axis, [(i, i ^ k) for i in range(count)])  5.09 us
    ppermute x4, waiting for transfers between devices, traded(): taken.append(lax.ppermute(block, (axis, 'gz'), route))  4.86 us
    ppermute x3, waiting for transfers between devices, gathered(): lax.ppermute(block, axis, [(i, i ^ k) for i in range(count)])  4.45 us
    ppermute x2, waiting for transfers between devices, doubled_over(): lax.ppermute(block, (axis, 'gz'), route)  4.13 us
    pallas_call x1, Pallas kernels, per_device_small(): pl.pallas_call(whole_kernel, out_shape=f32(nx, ny, nz), scratch_shapes=[p...  3.86 us
    ppermute x1, waiting for transfers between devices, per_device_small(): there = lax.ppermute(here, 'gz', [(0, 1), (1, 0)])  1.9 us
  transfers between devices with their start and end apart: 11, of which 9 were waited for; matrix products, arithmetic and copies ran while one was open for 0% of the time, Pallas kernels for 0%

profile of v6, /device:TPU:0, one launch (start us, length us, event | category | flops | bytes accessed | tf_op | source)
XLA Modules:
  0.0 39.9 jit_solution(17048704540842800188)
XLA Ops:
  0.0 1.0 %pad_maximum_fusion.own = f32[4,8,16,128]{3,2,1,0:T(8,128)S(1)} fusion(f32[1,8,16,128]{3,2,1,0:T(8,128)} %bitcast.9, f32[1,8,16,128]{3,2,1,0:T(8,128)} %bitcast.10, f32[1,8,16,128]{3,2,1,0:T(8,128)} %bitcast.11, f32[1,8,16,128]{3,2,1,0:T(8,128)} %bitcast.12), kind=kLoop, calls=%fused_computation | loop fusion | flops 196608 | bytes 524288 | tf_op jit(solution)/shard_map/stack | solution.py:484
  1.0 3.1 %collective-permute-start = (f32[9,16,128]{2,1,0:T(8,128)S(1)}, f32[9,16,128]{2,1,0:T(8,128)S(1)}, u32[]{:S(2)}, u32[]{:S(2)}) collective-permute-start(f32[9,16,128]{2,1,0:T(8,128)S(1)} %get-tuple-element.14), channel_id=1, source_target_pairs={{0,8},{1,9},{8,0},{9,1},{16,24},{17,25},{24,16},{25,17},{2,10},{3,... | collective-permute-start | bytes 221192 | tf_op jit(solution)/shard_map/ppermute | solution.py:458
  4.1 0.0 collective-permute-start.1
  4.1 2.3 %collective-permute-done.s0 = f32[9,16,128]{2,1,0:T(8,128)S(1)} collective-permute-done((f32[9,16,128]{2,1,0:T(8,128)S(1)}, f32[9,16,128]{2,1,0:T(8,128)S(1)}, u32[]{:S(2)}, u32[]{:S(2)}) %collective-permute-start) | collective-permute-done | bytes 73760 | tf_op jit(solution)/shard_map/ppermute | solution.py:458
  6.4 0.0 collective-permute-done.1.s1
  6.4 0.1 slabs_y.1
  6.5 2.0 %collective-permute-start.2 = (f32[112,128]{1,0:T(8,128)S(1)}, f32[112,128]{1,0:T(8,128)S(1)}, u32[]{:S(2)}, u32[]{:S(2)}) collective-permute-start(f32[112,128]{1,0:T(8,128)S(1)} %get-tuple-element.16), channel_id=1, source_target_pairs={{0,2},{1,3},{2,0},{3,1},{4,6},{5,7},{6,4},{7,5},{8,10},{9,11},{10,... | collective-permute-start | bytes 172040 | tf_op jit(solution)/shard_map/ppermute | solution.py:458
  8.5 0.0 collective-permute-start.3
  8.5 2.5 %collective-permute-done.2.o0 = f32[112,128]{1,0:T(8,128)S(1)} collective-permute-done((f32[112,128]{1,0:T(8,128)S(1)}, f32[112,128]{1,0:T(8,128)S(1)}, u32[]{:S(2)}, u32[]{:S(2)}) %collective-permute-start.2) | collective-permute-done | bytes 57376 | tf_op jit(solution)/shard_map/ppermute | solution.py:458
  11.0 0.0 collective-permute-done.3.o1
  11.1 0.3 edges_z.1
  11.3 0.1 collective-permute-start.4
  11.4 1.4 %collective-permute-done.4.edges = f32[12,24,128]{2,1,0:T(8,128)S(1)} collective-permute-done((f32[12,24,128]{2,1,0:T(8,128)S(1)}, f32[12,24,128]{2,1,0:T(8,128)S(1)}, u32[]{:S(2)}, u32[]{:S(2)}) %collective-permute-start.4) | collective-permute-done | bytes 147488 | tf_op jit(solution)/shard_map/ppermute | solution.py:508
  12.7 0.8 %fine.1 = (f32[8,16,128]{2,1,0:T(8,128)S(1)}, f32[6,8,16,128]{3,2,1,0:T(8,128)S(1)}, f32[2,4,8,128]{3,2,1,0:T(8,128)S(1)}) custom-call(f32[4,14,24,128]{3,2,1,0:T(8,128)S(1)} %get-tuple-element.18.local, f32[12,24,128]{2,1,0:T(8,128)S(1)} %collective-permute-done.4.edges), custom_call_target="tpu_custom_call" | custom-call | tf_op jit(solution)/shard_map/fine/pallas_call | solution.py:511
  13.5 3.4 %collective-permute-start.5 = (f32[1,2,4,8,128]{4,3,2,1,0:T(8,128)S(1)}, f32[1,2,4,8,128]{4,3,2,1,0:T(8,128)S(1)}, u32[]{:S(2)}, u32[]{:S(2)}) collective-permute-start(f32[1,2,4,8,128]{4,3,2,1,0:T(8,128)S(1)} %bitcast.6), channel_id=1, source_target_pairs={{0,8},{1,17},{8,0},{9,25},{16,24},{17,1},{24,16},{25,9},{2,10},{3,... | collective-permute-start | bytes 98312 | tf_op jit(solution)/shard_map/ppermute | solution.py:473
  16.9 1.9 %collective-permute-done.5 = f32[1,2,4,8,128]{4,3,2,1,0:T(8,128)S(1)} collective-permute-done((f32[1,2,4,8,128]{4,3,2,1,0:T(8,128)S(1)}, f32[1,2,4,8,128]{4,3,2,1,0:T(8,128)S(1)}, u32[]{:S(2)}, u32[]{:S(2)}) %collective-permute-start.5) | collective-permute-done | bytes 32800 | tf_op jit(solution)/shard_map/ppermute | solution.py:473
  18.8 3.4 %collective-permute-start.6 = (f32[2,2,4,8,128]{4,3,2,1,0:T(8,128)S(1)}, f32[2,2,4,8,128]{4,3,2,1,0:T(8,128)S(1)}, u32[]{:S(2)}, u32[]{:S(2)}) collective-permute-start(f32[2,2,4,8,128]{4,3,2,1,0:T(8,128)S(1)} %pad_maximum_fusion.2), channel_id=1, source_target_pairs={{0,16},{1,9},{8,24},{9,1},{16,0},{17,25},{24,8},{25,17},{2,18},{3,... | collective-permute-start | bytes 196616 | tf_op jit(solution)/shard_map/ppermute | solution.py:473
  22.2 2.2 %collective-permute-done.6 = f32[2,2,4,8,128]{4,3,2,1,0:T(8,128)S(1)} collective-permute-done((f32[2,2,4,8,128]{4,3,2,1,0:T(8,128)S(1)}, f32[2,2,4,8,128]{4,3,2,1,0:T(8,128)S(1)}, u32[]{:S(2)}, u32[]{:S(2)}) %collective-permute-start.6) | collective-permute-done | bytes 65568 | tf_op jit(solution)/shard_map/ppermute | solution.py:473
  24.4 2.8 %collective-permute-start.7 = (f32[4,2,4,8,128]{4,3,2,1,0:T(8,128)S(1)}, f32[4,2,4,8,128]{4,3,2,1,0:T(8,128)S(1)}, u32[]{:S(2)}, u32[]{:S(2)}) collective-permute-start(f32[4,2,4,8,128]{4,3,2,1,0:T(8,128)S(1)} %pad_maximum_fusion.1), channel_id=1, source_target_pairs={{0,2},{2,0},{4,6},{6,4},{1,3},{3,1},{5,7},{7,5},{8,10},{10,8},{12,... | collective-permute-start | bytes 393224 | tf_op jit(solution)/shard_map/ppermute | solution.py:464
  27.2 0.9 %collective-permute-start.8 = (f32[4,2,4,8,128]{4,3,2,1,0:T(8,128)S(1)}, f32[4,2,4,8,128]{4,3,2,1,0:T(8,128)S(1)}, u32[]{:S(2)}, u32[]{:S(2)}) collective-permute-start(f32[4,2,4,8,128]{4,3,2,1,0:T(8,128)S(1)} %pad_maximum_fusion.1), channel_id=1, source_target_pairs={{0,4},{2,6},{4,0},{6,2},{1,5},{3,7},{5,1},{7,3},{8,12},{10,14},{12... | collective-permute-start | bytes 393224 | tf_op jit(solution)/shard_map/ppermute | solution.py:464
  28.1 1.4 %collective-permute-start.9 = (f32[4,2,4,8,128]{4,3,2,1,0:T(8,128)S(1)}, f32[4,2,4,8,128]{4,3,2,1,0:T(8,128)S(1)}, u32[]{:S(2)}, u32[]{:S(2)}) collective-permute-start(f32[4,2,4,8,128]{4,3,2,1,0:T(8,128)S(1)} %pad_maximum_fusion.1), channel_id=1, source_target_pairs={{0,6},{2,4},{4,2},{6,0},{1,7},{3,5},{5,3},{7,1},{8,14},{10,12},{12... | collective-permute-start | bytes 393224 | tf_op jit(solution)/shard_map/ppermute | solution.py:464
  29.5 1.9 %collective-permute-done.7 = f32[4,2,4,8,128]{4,3,2,1,0:T(8,128)S(1)} collective-permute-done((f32[4,2,4,8,128]{4,3,2,1,0:T(8,128)S(1)}, f32[4,2,4,8,128]{4,3,2,1,0:T(8,128)S(1)}, u32[]{:S(2)}, u32[]{:S(2)}) %collective-permute-start.7) | collective-permute-done | bytes 131104 | tf_op jit(solution)/shard_map/ppermute | solution.py:464
  31.5 0.9 %collective-permute-done.8 = f32[4,2,4,8,128]{4,3,2,1,0:T(8,128)S(1)} collective-permute-done((f32[4,2,4,8,128]{4,3,2,1,0:T(8,128)S(1)}, f32[4,2,4,8,128]{4,3,2,1,0:T(8,128)S(1)}, u32[]{:S(2)}, u32[]{:S(2)}) %collective-permute-start.8) | collective-permute-done | bytes 131104 | tf_op jit(solution)/shard_map/ppermute | solution.py:464
  32.4 1.6 %collective-permute-done.9 = f32[4,2,4,8,128]{4,3,2,1,0:T(8,128)S(1)} collective-permute-done((f32[4,2,4,8,128]{4,3,2,1,0:T(8,128)S(1)}, f32[4,2,4,8,128]{4,3,2,1,0:T(8,128)S(1)}, u32[]{:S(2)}, u32[]{:S(2)}) %collective-permute-start.9) | collective-permute-done | bytes 131104 | tf_op jit(solution)/shard_map/ppermute | solution.py:464
  34.0 0.1 collective-permute-start.10
  34.1 1.9 %collective-permute-done.10.there = f32[16,2,4,8,128]{4,3,2,1,0:T(8,128)S(1)} collective-permute-done((f32[16,2,4,8,128]{4,3,2,1,0:T(8,128)S(1)}, f32[16,2,4,8,128]{4,3,2,1,0:T(8,128)S(1)}, u32[]{:S(2)}, u32[]{:S(2)}) %collective-permute-start.10) | collective-permute-done | bytes 524320 | tf_op jit(solution)/shard_map/ppermute | solution.py:526
  36.0 3.9 %whole.1 = f32[8,16,128]{2,1,0:T(8,128)} custom-call(f32[16,2,4,8,128]{4,3,2,1,0:T(8,128)S(1)} %constant_dynamic-update-slice_fusion.here, f32[16,2,4,8,128]{4,3,2,1,0:T(8,128)S(1)} %collective-permute-done.10.there, f32[8,16,128]{2,1,0:T(8,128)S(1)} %get-tuple-element.21.t_in, f32[6,8,16,128]{3,2,1,0:T(8,128)S(1)} %get-tuple-element.22.k_in), custom_call_target="tpu_custom_call" | custom-call | tf_op jit(solution)/shard_map/whole/pallas_call | solution.py:530
  (9 shorter events, 0.1 us)
Async XLA Ops:
  1.0 5.5 %collective-permute-start = (f32[9,16,128]{2,1,0:T(8,128)S(1)}, f32[9,16,128]{2,1,0:T(8,128)S(1)}, u32[]{:S(2)}, u32[]{:S(2)}) collective-permute-start(f32[9,16,128]{2,1,0:T(8,128)S(1)} %get-tuple-element.14), channel_id=1, source_target_pairs={{0,8},{1,9},{8,0},{9,1},{16,24},{17,25},{24,16},{25,17},{2,10},{3,... | collective-permute-start | bytes 221192 | tf_op jit(solution)/shard_map/ppermute | solution.py:458
  4.1 2.3 %collective-permute-start.1 = (f32[9,16,128]{2,1,0:T(8,128)S(1)}, f32[9,16,128]{2,1,0:T(8,128)S(1)}, u32[]{:S(2)}, u32[]{:S(2)}) collective-permute-start(f32[9,16,128]{2,1,0:T(8,128)S(1)} %get-tuple-element.15), channel_id=1, source_target_pairs={{0,1},{1,0},{8,16},{9,17},{16,8},{17,9},{24,25},{25,24},{2,3},{3,2... | collective-permute-start | bytes 221192 | tf_op jit(solution)/shard_map/ppermute | solution.py:458
  6.5 4.5 %collective-permute-start.2 = (f32[112,128]{1,0:T(8,128)S(1)}, f32[112,128]{1,0:T(8,128)S(1)}, u32[]{:S(2)}, u32[]{:S(2)}) collective-permute-start(f32[112,128]{1,0:T(8,128)S(1)} %get-tuple-element.16), channel_id=1, source_target_pairs={{0,2},{1,3},{2,0},{3,1},{4,6},{5,7},{6,4},{7,5},{8,10},{9,11},{10,... | collective-permute-start | bytes 172040 | tf_op jit(solution)/shard_map/ppermute | solution.py:458
  8.5 2.5 %collective-permute-start.3 = (f32[112,128]{1,0:T(8,128)S(1)}, f32[112,128]{1,0:T(8,128)S(1)}, u32[]{:S(2)}, u32[]{:S(2)}) collective-permute-start(f32[112,128]{1,0:T(8,128)S(1)} %get-tuple-element.17), channel_id=1, source_target_pairs={{0,1},{1,0},{2,4},{3,5},{4,2},{5,3},{6,7},{7,6},{8,9},{9,8},{10,12... | collective-permute-start | bytes 172040 | tf_op jit(solution)/shard_map/ppermute | solution.py:458
  11.3 1.4 %collective-permute-start.4 = (f32[12,24,128]{2,1,0:T(8,128)S(1)}, f32[12,24,128]{2,1,0:T(8,128)S(1)}, u32[]{:S(2)}, u32[]{:S(2)}) collective-permute-start(f32[12,24,128]{2,1,0:T(8,128)S(1)} %get-tuple-element.19), channel_id=1, source_target_pairs={{0,1},{1,0},{2,3},{3,2},{4,5},{5,4},{6,7},{7,6},{8,9},{9,8},{10,11... | collective-permute-start | bytes 442376 | tf_op jit(solution)/shard_map/ppermute | solution.py:508
  13.5 5.3 %collective-permute-start.5 = (f32[1,2,4,8,128]{4,3,2,1,0:T(8,128)S(1)}, f32[1,2,4,8,128]{4,3,2,1,0:T(8,128)S(1)}, u32[]{:S(2)}, u32[]{:S(2)}) collective-permute-start(f32[1,2,4,8,128]{4,3,2,1,0:T(8,128)S(1)} %bitcast.6), channel_id=1, source_target_pairs={{0,8},{1,17},{8,0},{9,25},{16,24},{17,1},{24,16},{25,9},{2,10},{3,... | collective-permute-start | bytes 98312 | tf_op jit(solution)/shard_map/ppermute | solution.py:473
  18.8 5.6 %collective-permute-start.6 = (f32[2,2,4,8,128]{4,3,2,1,0:T(8,128)S(1)}, f32[2,2,4,8,128]{4,3,2,1,0:T(8,128)S(1)}, u32[]{:S(2)}, u32[]{:S(2)}) collective-permute-start(f32[2,2,4,8,128]{4,3,2,1,0:T(8,128)S(1)} %pad_maximum_fusion.2), channel_id=1, source_target_pairs={{0,16},{1,9},{8,24},{9,1},{16,0},{17,25},{24,8},{25,17},{2,18},{3,... | collective-permute-start | bytes 196616 | tf_op jit(solution)/shard_map/ppermute | solution.py:473
  24.4 7.0 %collective-permute-start.7 = (f32[4,2,4,8,128]{4,3,2,1,0:T(8,128)S(1)}, f32[4,2,4,8,128]{4,3,2,1,0:T(8,128)S(1)}, u32[]{:S(2)}, u32[]{:S(2)}) collective-permute-start(f32[4,2,4,8,128]{4,3,2,1,0:T(8,128)S(1)} %pad_maximum_fusion.1), channel_id=1, source_target_pairs={{0,2},{2,0},{4,6},{6,4},{1,3},{3,1},{5,7},{7,5},{8,10},{10,8},{12,... | collective-permute-start | bytes 393224 | tf_op jit(solution)/shard_map/ppermute | solution.py:464
  27.2 5.2 %collective-permute-start.8 = (f32[4,2,4,8,128]{4,3,2,1,0:T(8,128)S(1)}, f32[4,2,4,8,128]{4,3,2,1,0:T(8,128)S(1)}, u32[]{:S(2)}, u32[]{:S(2)}) collective-permute-start(f32[4,2,4,8,128]{4,3,2,1,0:T(8,128)S(1)} %pad_maximum_fusion.1), channel_id=1, source_target_pairs={{0,4},{2,6},{4,0},{6,2},{1,5},{3,7},{5,1},{7,3},{8,12},{10,14},{12... | collective-permute-start | bytes 393224 | tf_op jit(solution)/shard_map/ppermute | solution.py:464
  28.1 5.9 %collective-permute-start.9 = (f32[4,2,4,8,128]{4,3,2,1,0:T(8,128)S(1)}, f32[4,2,4,8,128]{4,3,2,1,0:T(8,128)S(1)}, u32[]{:S(2)}, u32[]{:S(2)}) collective-permute-start(f32[4,2,4,8,128]{4,3,2,1,0:T(8,128)S(1)} %pad_maximum_fusion.1), channel_id=1, source_target_pairs={{0,6},{2,4},{4,2},{6,0},{1,7},{3,5},{5,3},{7,1},{8,14},{10,12},{12... | collective-permute-start | bytes 393224 | tf_op jit(solution)/shard_map/ppermute | solution.py:464
  34.0 2.0 %collective-permute-start.10 = (f32[16,2,4,8,128]{4,3,2,1,0:T(8,128)S(1)}, f32[16,2,4,8,128]{4,3,2,1,0:T(8,128)S(1)}, u32[]{:S(2)}, u32[]{:S(2)}) collective-permute-start(f32[16,2,4,8,128]{4,3,2,1,0:T(8,128)S(1)} %constant_dynamic-update-slice_fusion.here), channel_id=1, source_target_pairs={{0,1},{1,0},{2,3},{3,2},{4,5},{5,4},{6,7},{7,6},{8,9},{9,8},{10,11... | collective-permute-start | bytes 1572872 | tf_op jit(solution)/shard_map/ppermute | solution.py:526

commit v7 on v6

--- a/solution.py
+++ b/solution.py
@@ -16,6 +16,7 @@
 REACH = 3
 TILE = 8
 PAD = 4
+SMALL = pl.CostEstimate(flops=2**20, bytes_accessed=2**20, transcendentals=0)
 PARAMS = pltpu.CompilerParams(vmem_limit_bytes=16 * 2**20)
 
 
@@ -136,8 +137,8 @@
         edge[p] = packed
 
 
-def fine_kernel(local, edges, t_out, k_out, m_out, ext, e1, rd, dg, e2, rows):
-    nx, ny, half = t_out.shape
+def fine_kernel(local, edges, faces, e_out, q_out, r_out, m_out, ext, e1, rd, dg, e2, rows):
+    nx, ny, half = e_out.shape
     nz = 2 * half
     gx, gy, gz = lax.axis_index("gx"), lax.axis_index("gy"), lax.axis_index("gz")
     spot = iota((ny + 2 * PAD, half), 1)
@@ -188,24 +189,30 @@
     sums = []
     for i in range(nx):
         p = REACH + i
-        q = ext[0, p] - dg[p] * e2[p] + off(e2, p)
-        fy, fz = ext[2, p], jnp.where(inner_z, ext[3, p], 0.0)
-        inv = rd[p]
-        t_out[i] = mine(e2[p] + inv * q)
-        for n, k in enumerate((ext[1, p], ext[1, p + 1], fy, up(fy, 0), fz, up(fz, 1))):
-            k_out[n, i] = mine(inv * k)
-        sums.append(mine(q))
+        q = mine(ext[0, p] - dg[p] * e2[p] + off(e2, p))
+        e_out[i], q_out[i], r_out[i] = mine(e2[p]), q, mine(rd[p])
+        sums.append(q)
+    pairs = range(0, nx, 2)
+    both_low = chosen(iota((half, half), 0) // 2 == iota((half, half), 1))
+    rows[...] = select_dot(jnp.concatenate([sums[i] + sums[i + 1] for i in pairs], 0), both_low)
+    part = rows.shape[0] // 2
+    total = rows[pl.ds(0, part, stride=2)] + rows[pl.ds(1, part, stride=2)]
+    m_out[0] = faces[0] + total.reshape(m_out.shape[1:])
+    m_out[1] = faces[1]
+
+
+def faces_kernel(own, out, rows):
+    nx, ny, half = own.shape[1:]
+
     def face(d, i):
-        return 0.5 * ext[d, REACH + i, PAD : PAD + ny, :half]
+        return 0.5 * own[d, i]
 
     pairs = range(0, nx, 2)
     fine, coarse = iota((half, half), 0), iota((half, half), 1)
     both_low, both_high = chosen(fine // 2 == coarse), chosen(fine // 2 + half // 2 == coarse)
     even_high = chosen(fine + half == 2 * coarse)
     count = len(pairs) * ny
-    rows[:count] = select_dot(jnp.concatenate([sums[i] + sums[i + 1] for i in pairs], 0), both_low) + select_dot(
-        jnp.concatenate([face(1, i) for i in pairs], 0), both_high
-    )
+    rows[:count] = select_dot(jnp.concatenate([face(1, i) for i in pairs], 0), both_high)
     rows[count:] = select_dot(jnp.concatenate([face(2, i) + face(2, i + 1) for i in pairs], 0), both_low) + select_dot(
         jnp.concatenate([face(3, i) + face(3, i + 1) for i in pairs], 0), even_high
     )
@@ -213,8 +220,43 @@
     even = rows[pl.ds(0, 2 * part, stride=2)]
     odd = rows[pl.ds(1, 2 * part, stride=2)]
     spot = iota((part, half), 1)
-    m_out[0] = (even[:part] + odd[:part]).reshape(m_out.shape[1:])
-    m_out[1] = (even[part:] + jnp.where(spot < half // 2, 0.0, odd[part:])).reshape(m_out.shape[1:])
+    out[0] = (even[:part] + odd[:part]).reshape(out.shape[1:])
+    out[1] = (even[part:] + jnp.where(spot < half // 2, 0.0, odd[part:])).reshape(out.shape[1:])
+
+
+def sweep_kernel(local, edges, e_in, q_in, r_in, t_out, k_out, *matrices):
+    nx, ny, half = t_out.shape
+    gz = lax.axis_index("gz")
+    lane = iota((ny, half), 1)
+    low_z, top_z = jnp.logical_or(lane > 0, gz > 0), lane < half - 1
+    keep = jnp.where(gz == 0, 1.0, 0.0)
+    inner = slice(PAD, PAD + ny)
+    for i in range(nx):
+        p, inv = REACH + i, r_in[i]
+        fz = local[3, p, inner]
+        far = keep * pltpu.roll(edges[p - 1, inner], half - 1 - 9, 1)
+        high_z = jnp.where(top_z, up(fz, 1), far)
+        faces = (local[1, p, inner], local[1, p + 1, inner], local[2, p, inner], local[2, p, PAD + 1 : PAD + 1 + ny])
+        t_out[i] = e_in[i] + inv * q_in[i]
+        for n, k in enumerate(faces + (jnp.where(low_z, fz, 0.0), high_z)):
+            k_out[n, i] = inv * k
+    both1, even1, both2, even2, spread3, spread2, last = matrices
+    fine, coarse = iota(both1.shape, 0), iota(both1.shape, 1)
+    both1[...], even1[...] = chosen(fine // 2 == coarse), chosen(fine == 2 * coarse)
+    spread2[...] = chosen(coarse // 2 == fine)
+    blocks = both2.shape[0] // half
+    depth = half // blocks
+    fine, coarse = iota(both2.shape, 0), iota(both2.shape, 1)
+    block, fine = fine // half, fine % half
+    valid = fine < 2 * depth
+    both2[...] = chosen((fine // 2 + block * depth == coarse) & valid)
+    even2[...] = chosen((fine + 2 * block * depth == 2 * coarse) & valid)
+    fine, coarse = iota(spread3.shape, 1), iota(spread3.shape, 0)
+    block, fine = fine // half, fine % half
+    spread3[...] = chosen((fine // 2 + block * depth == coarse) & (fine < 2 * depth))
+    spot = gz * half + iota(last.shape, 1) % half + (iota(last.shape, 1) // half + 1) % 3 - 1
+    wanted = iota(last.shape, 0)
+    last[...] = chosen((2 * wanted == spot) | (2 * wanted + 1 == spot))
 
 
 def planes_of(ref):
@@ -313,18 +355,20 @@
     return result
 
 
-def whole_kernel(here, there, t_in, k_in, out, grid, fold1, folds1, fold2, folds2, spread2, held2, spread1, kept, doubled):
+def whole_kernel(*refs):
+    count = lax.axis_size("gy")
+    here, there = refs[:count], refs[count : 2 * count]
+    t_in, k_in, both1, even1, both2, even2, spread3, spread21, last, out, grid, fold1, folds1, fold2, folds2, spread2, held2, spread1, kept, doubled = refs[2 * count :]
     gx, gy, gz = lax.axis_index("gx"), lax.axis_index("gy"), lax.axis_index("gz")
     cx, cy = lax.axis_size("gx"), lax.axis_size("gy")
-    bx, by = here.shape[2], here.shape[3]
-    w1 = here.shape[4]
+    bx, by, w1 = here[0].shape[2:]
     for k in range(cx * cy):
         x = jnp.bitwise_xor(gx, k % cx) * bx
         y = pl.multiple_of(jnp.bitwise_xor(gy, k // cx) * by, by)
-        other = mirrored(k % cx, cx) + k // cx * cx
+        mine, other, j = k % cx, mirrored(k % cx, cx), k // cx
         for a in range(2):
-            low = jnp.where(gz == 0, here[k, a], there[k, a]).reshape(bx * by, w1)
-            top = jnp.where(gz == 0, there[other, a], here[other, a]).reshape(bx * by, w1)
+            low = jnp.where(gz == 0, here[j][mine, a], there[j][mine, a]).reshape(bx * by, w1)
+            top = jnp.where(gz == 0, there[j][other, a], here[j][other, a]).reshape(bx * by, w1)
             left = iota((bx * by, w1), 1) < w1 // 2
             one = jnp.where(left, low, pltpu.roll(top, w1 // 2, 1))
             two = jnp.where(left, pltpu.roll(low, w1 // 2, 1), top)
@@ -350,16 +394,14 @@
         + [0.5 * (fz1[i] + fz1[i + 1]) for i in pairs],
         0,
     )
-    fine, coarse = iota((w1, w1), 0), iota((w1, w1), 1)
-    both1, even = chosen(fine // 2 == coarse), chosen(fine == 2 * coarse)
     low, top = folds1[pl.ds(0, 3 * half, stride=2)], folds1[pl.ds(1, 3 * half, stride=2)]
-    summed = select_dot(jnp.concatenate([low[:half] + top[:half], low[half : 2 * half]], 0), both1)
+    summed = select_dot(jnp.concatenate([low[:half] + top[:half], low[half : 2 * half]], 0), both1[...])
 
     def part(v):
         return [v[p * m2 : (p + 1) * m2] for p in range(n2)]
 
     fx2, fy2 = part(summed[:half]), part(summed[half:])
-    fz2 = part(select_dot(low[2 * half :] + top[2 * half :], even))
+    fz2 = part(select_dot(low[2 * half :] + top[2 * half :], even1[...]))
     diagonal1, inv1, off1 = level_parts(fx1, fy1, fz1)
     t1, q1 = before(b1, diagonal1, inv1, off1)
     for p in range(n1):
@@ -369,30 +411,24 @@
 
     n3, m3 = n2 // 2, m2 // 2
     depth = w1 // n3
-    fine, coarse = iota((n3 * w1, w1), 0), iota((n3 * w1, w1), 1)
-    block, fine = fine // w1, fine % w1
-    both2 = chosen((fine // 2 + block * depth == coarse) & (fine < 2 * depth))
-    even = chosen((fine + 2 * block * depth == 2 * coarse) & (fine < 2 * depth))
     blocks = range(0, n2, 2)
     wide = [
         jnp.concatenate([0.5 * fx2[i] for i in blocks], 1),
         jnp.concatenate([0.5 * (fy2[i] + fy2[i + 1]) for i in blocks], 1),
     ]
     thin = jnp.concatenate([0.5 * (fz2[i] + fz2[i + 1]) for i in blocks], 1)
-    folds2[: 2 * m2] = select_dot(jnp.concatenate(wide, 0), both2)
-    folds2[2 * m2 :] = select_dot(thin, even)
+    folds2[: 2 * m2] = select_dot(jnp.concatenate(wide, 0), both2[...])
+    folds2[2 * m2 :] = select_dot(thin, even2[...])
     low, top = folds2[pl.ds(0, 3 * m3, stride=2)], folds2[pl.ds(1, 3 * m3, stride=2)]
     operate3 = coarse_operator(low[:m3] + top[:m3], low[m3 : 2 * m3], low[2 * m3 :] + top[2 * m3 :], depth)
 
     fold1[...] = jnp.concatenate([q1[i] + q1[i + 1] for i in pairs], 0)
-    b2 = part(select_dot(fold1[pl.ds(0, half, stride=2)] + fold1[pl.ds(1, half, stride=2)], both1))
+    b2 = part(select_dot(fold1[pl.ds(0, half, stride=2)] + fold1[pl.ds(1, half, stride=2)], both1[...]))
     t2, q2 = before(b2, diagonal2, inv2, off2)
-    fold2[...] = select_dot(jnp.concatenate([q2[i] + q2[i + 1] for i in blocks], 1), both2)
+    fold2[...] = select_dot(jnp.concatenate([q2[i] + q2[i + 1] for i in blocks], 1), both2[...])
     c3 = coarse_solution(fold2[pl.ds(0, m3, stride=2)] + fold2[pl.ds(1, m3, stride=2)], operate3)
 
-    fine, coarse = iota((w1, n3 * w1), 1), iota((w1, n3 * w1), 0)
-    block, fine = fine // w1, fine % w1
-    row = select_dot(c3, chosen((fine // 2 + block * depth == coarse) & (fine < 2 * depth)))
+    row = select_dot(c3, spread3[...])
     for i in range(n3):
         spread2[pl.ds(i * m2, m3, stride=2)] = row[:, i * w1 : (i + 1) * w1]
         spread2[pl.ds(i * m2 + 1, m3, stride=2)] = row[:, i * w1 : (i + 1) * w1]
@@ -405,8 +441,7 @@
         held2[1 + p] = c2[p]
     few = bx // 2 + 2
     near = held2[pl.ds(gx * (bx // 2), few)].reshape(few * m2, w1)
-    fine, coarse = iota((w1, w1), 1), iota((w1, w1), 0)
-    row = select_dot(near, chosen(fine // 2 == coarse))
+    row = select_dot(near, spread21[...])
     for p in range(few):
         spread1[p, :TILE] = jnp.zeros((TILE, w1), jnp.float32)
         spread1[p, TILE + m1 :] = jnp.zeros((TILE, w1), jnp.float32)
@@ -426,9 +461,7 @@
         value = kept[0, x, rows] + (1.0 - damping) * e + kept[1, x, rows] * total
         near.append(value[TILE - 1 : TILE - 1 + by + TILE])
     tall = by + TILE
-    spot = gz * t_in.shape[2] + iota((w1, 3 * w1), 1) % w1 + (iota((w1, 3 * w1), 1) // w1 + 1) % 3 - 1
-    wanted = iota((w1, 3 * w1), 0)
-    row = select_dot(jnp.concatenate(near, 0), chosen((2 * wanted == spot) | (2 * wanted + 1 == spot)))
+    row = select_dot(jnp.concatenate(near, 0), last[...])
     for s in range(3):
         doubled[s, pl.ds(0, (bx + 2) * tall, stride=2)] = row[:, s * w1 : (s + 1) * w1]
         doubled[s, pl.ds(1, (bx + 2) * tall, stride=2)] = row[:, s * w1 : (s + 1) * w1]
@@ -459,12 +492,6 @@
     return taken
 
 
-def gathered(block, axis):
-    count = lax.axis_size(axis)
-    parts = [lax.ppermute(block, axis, [(i, i ^ k) for i in range(count)]) for k in range(1, count)]
-    return jnp.concatenate([block] + parts, 0)
-
-
 def doubled_over(block, axis):
     count, cores = lax.axis_size(axis), lax.axis_size("gz")
     steps = [1 << n for n in range(count.bit_length() - 1)]
@@ -481,6 +508,7 @@
 def per_device_small(adjoint_residual, face_x, face_y, face_z):
     nx, ny, nz = adjoint_residual.shape
     near = [pltpu.VMEM((9, ny, nz), jnp.float32)] * 2
+    cy = lax.axis_size("gy")
     own = jnp.stack((adjoint_residual, face_x, face_y, face_z))
     slabs = pl.pallas_call(
         x_kernel,
@@ -489,6 +517,14 @@
         name="slabs_x",
     )(own)
     slabs = traded(slabs, "gx")
+    faces = pl.pallas_call(
+        faces_kernel,
+        out_shape=f32(2, nx // 2, ny // 2, nz),
+        scratch_shapes=[pltpu.VMEM((nx * ny, nz), jnp.float32)],
+        compiler_params=PARAMS,
+        cost_estimate=SMALL,
+        name="faces",
+    )(own)
     count = -(-9 * (nx + 4) // 8) * 8
     lines = pl.pallas_call(
         y_kernel,
@@ -508,23 +544,36 @@
     edges = lax.ppermute(edge, "gz", [(0, 1), (1, 0)])
     ext_x, ext_y, wide = nx + 2 * REACH, ny + 2 * PAD, 2 * nz
     field = pltpu.VMEM((ext_x, ext_y, wide), jnp.float32)
-    t, k, m = pl.pallas_call(
+    e, q, r, m = pl.pallas_call(
         fine_kernel,
-        out_shape=(f32(nx, ny, nz), f32(6, nx, ny, nz), f32(2, nx // 2, ny // 2, nz)),
+        out_shape=(f32(nx, ny, nz),) * 3 + (f32(2, nx // 2, ny // 2, nz),),
         scratch_shapes=[
             pltpu.VMEM((4, ext_x, ext_y, wide), jnp.float32),
             field,
             field,
             field,
             field,
-            pltpu.VMEM((nx * ny, nz), jnp.float32),
+            pltpu.VMEM((nx * ny // 2, nz), jnp.float32),
         ],
         compiler_params=PARAMS,
         name="fine",
-    )(local, edges)
-    here = gathered(doubled_over(m[None], "gx"), "gy")
-    there = lax.ppermute(here, "gz", [(0, 1), (1, 0)])
-    n1, m1 = here.shape[2] * lax.axis_size("gx"), here.shape[3] * lax.axis_size("gy")
+    )(local, edges, faces)
+    blocks = nx * lax.axis_size("gx") // 8
+    shapes = ((nz, nz), (nz, nz), (blocks * nz, nz), (blocks * nz, nz), (nz, blocks * nz), (nz, nz), (nz, 3 * nz))
+    t, k, *matrices = pl.pallas_call(
+        sweep_kernel,
+        out_shape=(f32(nx, ny, nz), f32(6, nx, ny, nz))
+        + tuple(jax.ShapeDtypeStruct(shape, jnp.bfloat16) for shape in shapes),
+        compiler_params=PARAMS,
+        cost_estimate=SMALL,
+        name="sweep",
+    )(local, edges, e, q, r)
+    near = doubled_over(m[None], "gx")
+    here = [near] + [
+        lax.ppermute(near, "gy", [(i, i ^ n) for i in range(cy)]) for n in range(1, cy)
+    ]
+    there = [lax.ppermute(block, "gz", [(0, 1), (1, 0)]) for block in here]
+    n1, m1 = m.shape[1] * lax.axis_size("gx"), m.shape[2] * cy
     n2, m2 = n1 // 2, m1 // 2
     tall = (nx // 2 + 2) * (ny // 2 + TILE)
     return pl.pallas_call(
@@ -544,7 +593,7 @@
         ],
         compiler_params=PARAMS,
         name="whole",
-    )(here, there, t, k)
+    )(*here, *there, t, k, *matrices)
 
 
 def extended(block, sides, width):

time: 40 us -> 39.2 us (0.980)
  waiting for transfers between devices: 16.7 us -> 15.7 us
    ppermute x4 -> x7, waiting for transfers between devices: 6.35 us -> 5.52 us  [the longest x3 4.47 us: per_device_small(): lax.ppermute(near, 'gy', [(i, i ^ n) for i in range(cy)])]
    pallas_call x1 -> x3, Pallas kernels: 0.76 us -> 1.16 us  [the longest x1 0.7 us: per_device_small(): pl.pallas_call(fine_kernel, out_shape=(f32(nx, ny, nz),) * 3 + (f32(2, nx...]
    ppermute x4 -> x7, starting transfers between devices: 5.16 us -> 5.1 us  [the longest x3 5.09 us: per_device_small(): lax.ppermute(near, 'gy', [(i, i ^ n) for i in range(cy)])]
  transfers between devices with their start and end apart: 11 -> 14, of which waited for: 9 -> 9; matrix products, arithmetic and copies ran while one was open for 0% -> 0% of each run, Pallas kernels for 0% -> 1%
where the time goes in v7:
time: 39.2 us; the launch traced here: 39.1 us
  starting transfers between devices  17 us (43%)
  waiting for transfers between devices  15.7 us (40%)
  Pallas kernels  5.3 us (14%)
  other arithmetic  0.97 us (2%)
    ppermute x2, starting transfers between devices, doubled_over(): lax.ppermute(block, (axis, 'gz'), route)  6.76 us
    ppermute x4, starting transfers between devices, traded(): taken.append(lax.ppermute(block, (axis, 'gz'), route))  5.12 us
    ppermute x3, starting transfers between devices, per_device_small(): lax.ppermute(near, 'gy', [(i, i ^ n) for i in range(cy)])  5.09 us
    ppermute x4, waiting for transfers between devices, traded(): taken.append(lax.ppermute(block, (axis, 'gz'), route))  4.86 us
    ppermute x3, waiting for transfers between devices, per_device_small(): lax.ppermute(near, 'gy', [(i, i ^ n) for i in range(cy)])  4.47 us
    ppermute x2, waiting for transfers between devices, doubled_over(): lax.ppermute(block, (axis, 'gz'), route)  4.14 us
    pallas_call x1, Pallas kernels, per_device_small(): pl.pallas_call(whole_kernel, out_shape=f32(nx, ny, nz), scratch_shapes=[p...  3.8 us
    ppermute x1, waiting for transfers between devices, per_device_small(): edges = lax.ppermute(edge, 'gz', [(0, 1), (1, 0)])  1.16 us
  transfers between devices with their start and end apart: 14, of which 9 were waited for; matrix products, arithmetic and copies ran while one was open for 0% of the time, Pallas kernels for 1%

profile of v7, /device:TPU:0, one launch (start us, length us, event | category | flops | bytes accessed | tf_op | source)
XLA Modules:
  0.0 39.1 jit_solution(7847335369654384685)
XLA Ops:
  0.0 1.0 %pad_maximum_fusion.own = f32[4,8,16,128]{3,2,1,0:T(8,128)S(1)} fusion(f32[1,8,16,128]{3,2,1,0:T(8,128)} %bitcast.8, f32[1,8,16,128]{3,2,1,0:T(8,128)} %bitcast.9, f32[1,8,16,128]{3,2,1,0:T(8,128)} %bitcast.10, f32[1,8,16,128]{3,2,1,0:T(8,128)} %bitcast.11), kind=kLoop, calls=%fused_computation | loop fusion | flops 196608 | bytes 524288 | tf_op jit(solution)/shard_map/stack | solution.py:512
  1.0 3.1 %collective-permute-start = (f32[9,16,128]{2,1,0:T(8,128)S(1)}, f32[9,16,128]{2,1,0:T(8,128)S(1)}, u32[]{:S(2)}, u32[]{:S(2)}) collective-permute-start(f32[9,16,128]{2,1,0:T(8,128)S(1)} %get-tuple-element.24), channel_id=1, source_target_pairs={{0,8},{1,9},{8,0},{9,1},{16,24},{17,25},{24,16},{25,17},{2,10},{3,... | collective-permute-start | bytes 221192 | tf_op jit(solution)/shard_map/ppermute | solution.py:491
  4.1 0.0 collective-permute-start.1
  4.1 2.3 %collective-permute-done.s0 = f32[9,16,128]{2,1,0:T(8,128)S(1)} collective-permute-done((f32[9,16,128]{2,1,0:T(8,128)S(1)}, f32[9,16,128]{2,1,0:T(8,128)S(1)}, u32[]{:S(2)}, u32[]{:S(2)}) %collective-permute-start) | collective-permute-done | bytes 73760 | tf_op jit(solution)/shard_map/ppermute | solution.py:491
  6.4 0.0 collective-permute-done.1.s1
  6.4 0.1 slabs_y.1
  6.5 2.0 %collective-permute-start.2 = (f32[112,128]{1,0:T(8,128)S(1)}, f32[112,128]{1,0:T(8,128)S(1)}, u32[]{:S(2)}, u32[]{:S(2)}) collective-permute-start(f32[112,128]{1,0:T(8,128)S(1)} %get-tuple-element.26), channel_id=1, source_target_pairs={{0,2},{1,3},{2,0},{3,1},{4,6},{5,7},{6,4},{7,5},{8,10},{9,11},{10,... | collective-permute-start | bytes 172040 | tf_op jit(solution)/shard_map/ppermute | solution.py:491
  8.5 0.0 collective-permute-start.3
  8.5 2.5 %collective-permute-done.2.o0 = f32[112,128]{1,0:T(8,128)S(1)} collective-permute-done((f32[112,128]{1,0:T(8,128)S(1)}, f32[112,128]{1,0:T(8,128)S(1)}, u32[]{:S(2)}, u32[]{:S(2)}) %collective-permute-start.2) | collective-permute-done | bytes 57376 | tf_op jit(solution)/shard_map/ppermute | solution.py:491
  11.1 0.3 edges_z.1
  11.3 0.1 collective-permute-start.4
  11.4 0.2 faces.1
  11.6 1.2 %collective-permute-done.4.edges = f32[12,24,128]{2,1,0:T(8,128)S(1)} collective-permute-done((f32[12,24,128]{2,1,0:T(8,128)S(1)}, f32[12,24,128]{2,1,0:T(8,128)S(1)}, u32[]{:S(2)}, u32[]{:S(2)}) %collective-permute-start.4) | collective-permute-done | bytes 147488 | tf_op jit(solution)/shard_map/ppermute | solution.py:544
  12.7 0.7 %fine.1 = (f32[8,16,128]{2,1,0:T(8,128)S(1)}, f32[8,16,128]{2,1,0:T(8,128)S(1)}, f32[8,16,128]{2,1,0:T(8,128)S(1)}, f32[2,4,8,128]{3,2,1,0:T(8,128)S(1)}) custom-call(f32[4,14,24,128]{3,2,1,0:T(8,128)S(1)} %get-tuple-element.28.local, f32[12,24,128]{2,1,0:T(8,128)S(1)} %collective-permute-done.4.edges, f32[2,4,8,128]{3,2,1,0:T(8,128)S(1)} %faces.1), custom_call_target="tpu_custom_call" | custom-call | tf_op jit(solution)/shard_map/fine/pallas_call | solution.py:547
  13.5 3.4 %collective-permute-start.5 = (f32[1,2,4,8,128]{4,3,2,1,0:T(8,128)S(1)}, f32[1,2,4,8,128]{4,3,2,1,0:T(8,128)S(1)}, u32[]{:S(2)}, u32[]{:S(2)}) collective-permute-start(f32[1,2,4,8,128]{4,3,2,1,0:T(8,128)S(1)} %bitcast.5), channel_id=1, source_target_pairs={{0,8},{1,17},{8,0},{9,25},{16,24},{17,1},{24,16},{25,9},{2,10},{3,... | collective-permute-start | bytes 98312 | tf_op jit(solution)/shard_map/ppermute | solution.py:500
  16.8 1.9 %collective-permute-done.5 = f32[1,2,4,8,128]{4,3,2,1,0:T(8,128)S(1)} collective-permute-done((f32[1,2,4,8,128]{4,3,2,1,0:T(8,128)S(1)}, f32[1,2,4,8,128]{4,3,2,1,0:T(8,128)S(1)}, u32[]{:S(2)}, u32[]{:S(2)}) %collective-permute-start.5) | collective-permute-done | bytes 32800 | tf_op jit(solution)/shard_map/ppermute | solution.py:500
  18.7 3.4 %collective-permute-start.6 = (f32[2,2,4,8,128]{4,3,2,1,0:T(8,128)S(1)}, f32[2,2,4,8,128]{4,3,2,1,0:T(8,128)S(1)}, u32[]{:S(2)}, u32[]{:S(2)}) collective-permute-start(f32[2,2,4,8,128]{4,3,2,1,0:T(8,128)S(1)} %pad_maximum_fusion.2), channel_id=1, source_target_pairs={{0,16},{1,9},{8,24},{9,1},{16,0},{17,25},{24,8},{25,17},{2,18},{3,... | collective-permute-start | bytes 196616 | tf_op jit(solution)/shard_map/ppermute | solution.py:500
  22.1 2.2 %collective-permute-done.6 = f32[2,2,4,8,128]{4,3,2,1,0:T(8,128)S(1)} collective-permute-done((f32[2,2,4,8,128]{4,3,2,1,0:T(8,128)S(1)}, f32[2,2,4,8,128]{4,3,2,1,0:T(8,128)S(1)}, u32[]{:S(2)}, u32[]{:S(2)}) %collective-permute-start.6) | collective-permute-done | bytes 65568 | tf_op jit(solution)/shard_map/ppermute | solution.py:500
  24.4 2.8 %collective-permute-start.7 = (f32[4,2,4,8,128]{4,3,2,1,0:T(8,128)S(1)}, f32[4,2,4,8,128]{4,3,2,1,0:T(8,128)S(1)}, u32[]{:S(2)}, u32[]{:S(2)}) collective-permute-start(f32[4,2,4,8,128]{4,3,2,1,0:T(8,128)S(1)} %pad_maximum_fusion.1.refs_0_), channel_id=1, source_target_pairs={{0,2},{2,0},{4,6},{6,4},{1,3},{3,1},{5,7},{7,5},{8,10},{10,8},{12,... | collective-permute-start | bytes 393224 | tf_op jit(solution)/shard_map/ppermute | solution.py:573
  27.1 0.9 %collective-permute-start.8 = (f32[4,2,4,8,128]{4,3,2,1,0:T(8,128)S(1)}, f32[4,2,4,8,128]{4,3,2,1,0:T(8,128)S(1)}, u32[]{:S(2)}, u32[]{:S(2)}) collective-permute-start(f32[4,2,4,8,128]{4,3,2,1,0:T(8,128)S(1)} %pad_maximum_fusion.1.refs_0_), channel_id=1, source_target_pairs={{0,4},{2,6},{4,0},{6,2},{1,5},{3,7},{5,1},{7,3},{8,12},{10,14},{12... | collective-permute-start | bytes 393224 | tf_op jit(solution)/shard_map/ppermute | solution.py:573
  28.1 1.4 %collective-permute-start.9 = (f32[4,2,4,8,128]{4,3,2,1,0:T(8,128)S(1)}, f32[4,2,4,8,128]{4,3,2,1,0:T(8,128)S(1)}, u32[]{:S(2)}, u32[]{:S(2)}) collective-permute-start(f32[4,2,4,8,128]{4,3,2,1,0:T(8,128)S(1)} %pad_maximum_fusion.1.refs_0_), channel_id=1, source_target_pairs={{0,6},{2,4},{4,2},{6,0},{1,7},{3,5},{5,3},{7,1},{8,14},{10,12},{12... | collective-permute-start | bytes 393224 | tf_op jit(solution)/shard_map/ppermute | solution.py:573
  29.5 0.0 collective-permute-start.10
  29.5 1.9 %collective-permute-done.7.refs_1_ = f32[4,2,4,8,128]{4,3,2,1,0:T(8,128)S(1)} collective-permute-done((f32[4,2,4,8,128]{4,3,2,1,0:T(8,128)S(1)}, f32[4,2,4,8,128]{4,3,2,1,0:T(8,128)S(1)}, u32[]{:S(2)}, u32[]{:S(2)}) %collective-permute-start.7) | collective-permute-done | bytes 131104 | tf_op jit(solution)/shard_map/ppermute | solution.py:573
  31.4 0.0 collective-permute-start.11
  31.4 1.0 %collective-permute-done.8.refs_2_ = f32[4,2,4,8,128]{4,3,2,1,0:T(8,128)S(1)} collective-permute-done((f32[4,2,4,8,128]{4,3,2,1,0:T(8,128)S(1)}, f32[4,2,4,8,128]{4,3,2,1,0:T(8,128)S(1)}, u32[]{:S(2)}, u32[]{:S(2)}) %collective-permute-start.8) | collective-permute-done | bytes 131104 | tf_op jit(solution)/shard_map/ppermute | solution.py:573
  32.4 0.0 collective-permute-start.12
  32.4 1.6 %collective-permute-done.9.refs_3_ = f32[4,2,4,8,128]{4,3,2,1,0:T(8,128)S(1)} collective-permute-done((f32[4,2,4,8,128]{4,3,2,1,0:T(8,128)S(1)}, f32[4,2,4,8,128]{4,3,2,1,0:T(8,128)S(1)}, u32[]{:S(2)}, u32[]{:S(2)}) %collective-permute-start.9) | collective-permute-done | bytes 131104 | tf_op jit(solution)/shard_map/ppermute | solution.py:573
  33.9 0.0 collective-permute-start.13
  33.9 0.3 sweep.1
  34.2 0.0 collective-permute-done.10.refs_4_
  34.2 1.0 %collective-permute-done.13.refs_7_ = f32[4,2,4,8,128]{4,3,2,1,0:T(8,128)S(1)} collective-permute-done((f32[4,2,4,8,128]{4,3,2,1,0:T(8,128)S(1)}, f32[4,2,4,8,128]{4,3,2,1,0:T(8,128)S(1)}, u32[]{:S(2)}, u32[]{:S(2)}) %collective-permute-start.13) | collective-permute-done | bytes 131104 | tf_op jit(solution)/shard_map/ppermute | solution.py:575
  35.3 3.8 %whole.1 = f32[8,16,128]{2,1,0:T(8,128)} custom-call(f32[4,2,4,8,128]{4,3,2,1,0:T(8,128)S(1)} %pad_maximum_fusion.1.refs_0_, f32[4,2,4,8,128]{4,3,2,1,0:T(8,128)S(1)} %collective-permute-done.7.refs_1_, f32[4,2,4,8,128]{4,3,2,1,0:T(8,128)S(1)} %collective-permute-done.8.refs_2_, f32[4,2,4,8,128]{4,3,2,1,0:T(8,128)S(1)} %collective-permute-done.9.refs_3_, ...), custom_call_target="tpu_custom_call" | custom-call | tf_op jit(solution)/shard_map/whole/pallas_call | solution.py:579
  (6 shorter events, 0.0 us)
Async XLA Ops:
  1.0 5.5 %collective-permute-start = (f32[9,16,128]{2,1,0:T(8,128)S(1)}, f32[9,16,128]{2,1,0:T(8,128)S(1)}, u32[]{:S(2)}, u32[]{:S(2)}) collective-permute-start(f32[9,16,128]{2,1,0:T(8,128)S(1)} %get-tuple-element.24), channel_id=1, source_target_pairs={{0,8},{1,9},{8,0},{9,1},{16,24},{17,25},{24,16},{25,17},{2,10},{3,... | collective-permute-start | bytes 221192 | tf_op jit(solution)/shard_map/ppermute | solution.py:491
  4.1 2.3 %collective-permute-start.1 = (f32[9,16,128]{2,1,0:T(8,128)S(1)}, f32[9,16,128]{2,1,0:T(8,128)S(1)}, u32[]{:S(2)}, u32[]{:S(2)}) collective-permute-start(f32[9,16,128]{2,1,0:T(8,128)S(1)} %get-tuple-element.25), channel_id=1, source_target_pairs={{0,1},{1,0},{8,16},{9,17},{16,8},{17,9},{24,25},{25,24},{2,3},{3,2... | collective-permute-start | bytes 221192 | tf_op jit(solution)/shard_map/ppermute | solution.py:491
  6.5 4.5 %collective-permute-start.2 = (f32[112,128]{1,0:T(8,128)S(1)}, f32[112,128]{1,0:T(8,128)S(1)}, u32[]{:S(2)}, u32[]{:S(2)}) collective-permute-start(f32[112,128]{1,0:T(8,128)S(1)} %get-tuple-element.26), channel_id=1, source_target_pairs={{0,2},{1,3},{2,0},{3,1},{4,6},{5,7},{6,4},{7,5},{8,10},{9,11},{10,... | collective-permute-start | bytes 172040 | tf_op jit(solution)/shard_map/ppermute | solution.py:491
  8.5 2.5 %collective-permute-start.3 = (f32[112,128]{1,0:T(8,128)S(1)}, f32[112,128]{1,0:T(8,128)S(1)}, u32[]{:S(2)}, u32[]{:S(2)}) collective-permute-start(f32[112,128]{1,0:T(8,128)S(1)} %get-tuple-element.27), channel_id=1, source_target_pairs={{0,1},{1,0},{2,4},{3,5},{4,2},{5,3},{6,7},{7,6},{8,9},{9,8},{10,12... | collective-permute-start | bytes 172040 | tf_op jit(solution)/shard_map/ppermute | solution.py:491
  11.3 1.4 %collective-permute-start.4 = (f32[12,24,128]{2,1,0:T(8,128)S(1)}, f32[12,24,128]{2,1,0:T(8,128)S(1)}, u32[]{:S(2)}, u32[]{:S(2)}) collective-permute-start(f32[12,24,128]{2,1,0:T(8,128)S(1)} %get-tuple-element.29), channel_id=1, source_target_pairs={{0,1},{1,0},{2,3},{3,2},{4,5},{5,4},{6,7},{7,6},{8,9},{9,8},{10,11... | collective-permute-start | bytes 442376 | tf_op jit(solution)/shard_map/ppermute | solution.py:544
  13.5 5.3 %collective-permute-start.5 = (f32[1,2,4,8,128]{4,3,2,1,0:T(8,128)S(1)}, f32[1,2,4,8,128]{4,3,2,1,0:T(8,128)S(1)}, u32[]{:S(2)}, u32[]{:S(2)}) collective-permute-start(f32[1,2,4,8,128]{4,3,2,1,0:T(8,128)S(1)} %bitcast.5), channel_id=1, source_target_pairs={{0,8},{1,17},{8,0},{9,25},{16,24},{17,1},{24,16},{25,9},{2,10},{3,... | collective-permute-start | bytes 98312 | tf_op jit(solution)/shard_map/ppermute | solution.py:500
  18.7 5.6 %collective-permute-start.6 = (f32[2,2,4,8,128]{4,3,2,1,0:T(8,128)S(1)}, f32[2,2,4,8,128]{4,3,2,1,0:T(8,128)S(1)}, u32[]{:S(2)}, u32[]{:S(2)}) collective-permute-start(f32[2,2,4,8,128]{4,3,2,1,0:T(8,128)S(1)} %pad_maximum_fusion.2), channel_id=1, source_target_pairs={{0,16},{1,9},{8,24},{9,1},{16,0},{17,25},{24,8},{25,17},{2,18},{3,... | collective-permute-start | bytes 196616 | tf_op jit(solution)/shard_map/ppermute | solution.py:500
  24.4 7.0 %collective-permute-start.7 = (f32[4,2,4,8,128]{4,3,2,1,0:T(8,128)S(1)}, f32[4,2,4,8,128]{4,3,2,1,0:T(8,128)S(1)}, u32[]{:S(2)}, u32[]{:S(2)}) collective-permute-start(f32[4,2,4,8,128]{4,3,2,1,0:T(8,128)S(1)} %pad_maximum_fusion.1.refs_0_), channel_id=1, source_target_pairs={{0,2},{2,0},{4,6},{6,4},{1,3},{3,1},{5,7},{7,5},{8,10},{10,8},{12,... | collective-permute-start | bytes 393224 | tf_op jit(solution)/shard_map/ppermute | solution.py:573
  27.1 5.2 %collective-permute-start.8 = (f32[4,2,4,8,128]{4,3,2,1,0:T(8,128)S(1)}, f32[4,2,4,8,128]{4,3,2,1,0:T(8,128)S(1)}, u32[]{:S(2)}, u32[]{:S(2)}) collective-permute-start(f32[4,2,4,8,128]{4,3,2,1,0:T(8,128)S(1)} %pad_maximum_fusion.1.refs_0_), channel_id=1, source_target_pairs={{0,4},{2,6},{4,0},{6,2},{1,5},{3,7},{5,1},{7,3},{8,12},{10,14},{12... | collective-permute-start | bytes 393224 | tf_op jit(solution)/shard_map/ppermute | solution.py:573
  28.1 5.9 %collective-permute-start.9 = (f32[4,2,4,8,128]{4,3,2,1,0:T(8,128)S(1)}, f32[4,2,4,8,128]{4,3,2,1,0:T(8,128)S(1)}, u32[]{:S(2)}, u32[]{:S(2)}) collective-permute-start(f32[4,2,4,8,128]{4,3,2,1,0:T(8,128)S(1)} %pad_maximum_fusion.1.refs_0_), channel_id=1, source_target_pairs={{0,6},{2,4},{4,2},{6,0},{1,7},{3,5},{5,3},{7,1},{8,14},{10,12},{12... | collective-permute-start | bytes 393224 | tf_op jit(solution)/shard_map/ppermute | solution.py:573
  29.5 4.8 %collective-permute-start.10 = (f32[4,2,4,8,128]{4,3,2,1,0:T(8,128)S(1)}, f32[4,2,4,8,128]{4,3,2,1,0:T(8,128)S(1)}, u32[]{:S(2)}, u32[]{:S(2)}) collective-permute-start(f32[4,2,4,8,128]{4,3,2,1,0:T(8,128)S(1)} %pad_maximum_fusion.1.refs_0_), channel_id=1, source_target_pairs={{0,1},{1,0},{2,3},{3,2},{4,5},{5,4},{6,7},{7,6},{8,9},{9,8},{10,11... | collective-permute-start | bytes 393224 | tf_op jit(solution)/shard_map/ppermute | solution.py:575
  31.4 2.8 %collective-permute-start.11 = (f32[4,2,4,8,128]{4,3,2,1,0:T(8,128)S(1)}, f32[4,2,4,8,128]{4,3,2,1,0:T(8,128)S(1)}, u32[]{:S(2)}, u32[]{:S(2)}) collective-permute-start(f32[4,2,4,8,128]{4,3,2,1,0:T(8,128)S(1)} %collective-permute-done.7.refs_1_), channel_id=1, source_target_pairs={{0,1},{1,0},{2,3},{3,2},{4,5},{5,4},{6,7},{7,6},{8,9},{9,8},{10,11... | collective-permute-start | bytes 393224 | tf_op jit(solution)/shard_map/ppermute | solution.py:575
  32.4 1.9 %collective-permute-start.12 = (f32[4,2,4,8,128]{4,3,2,1,0:T(8,128)S(1)}, f32[4,2,4,8,128]{4,3,2,1,0:T(8,128)S(1)}, u32[]{:S(2)}, u32[]{:S(2)}) collective-permute-start(f32[4,2,4,8,128]{4,3,2,1,0:T(8,128)S(1)} %collective-permute-done.8.refs_2_), channel_id=1, source_target_pairs={{0,1},{1,0},{2,3},{3,2},{4,5},{5,4},{6,7},{7,6},{8,9},{9,8},{10,11... | collective-permute-start | bytes 393224 | tf_op jit(solution)/shard_map/ppermute | solution.py:575
  33.9 1.3 %collective-permute-start.13 = (f32[4,2,4,8,128]{4,3,2,1,0:T(8,128)S(1)}, f32[4,2,4,8,128]{4,3,2,1,0:T(8,128)S(1)}, u32[]{:S(2)}, u32[]{:S(2)}) collective-permute-start(f32[4,2,4,8,128]{4,3,2,1,0:T(8,128)S(1)} %collective-permute-done.9.refs_3_), channel_id=1, source_target_pairs={{0,1},{1,0},{2,3},{3,2},{4,5},{5,4},{6,7},{7,6},{8,9},{9,8},{10,11... | collective-permute-start | bytes 393224 | tf_op jit(solution)/shard_map/ppermute | solution.py:575

commit v8 on v7

--- a/solution.py
+++ b/solution.py
@@ -95,7 +95,7 @@
         out[used:] = jnp.zeros((out.shape[0] - used, out.shape[1]), jnp.float32)
 
 
-def z_kernel(own, s0, s1, o0, o1, ext, edge, before, behind, lines):
+def z_kernel(own, s0, s1, o0, o1, ext, before, behind, lines):
     nx, ny, nz = own.shape[1:]
     gz = lax.axis_index("gz")
     sides_x((s0, s1), before, behind)
@@ -127,32 +127,69 @@
             if r > PAD:
                 at = 8 * (nx + 4) + p
                 ext[2, 1 + p, r + 2 : r + 3] = lines[at : at + 1]
-    lane = iota((ny + 2 * PAD, nz), 1)
+
+
+def side_by_side(values):
+    gz, nz = lax.axis_index("gz"), values[0].shape[1]
+    lane, packed = iota(values[0].shape, 1), values[0]
+    for a in range(1, 4):
+        first = jnp.where(gz == 0, nz - 3 - 3 * a, 3 * a)
+        moved = pltpu.roll(values[a], jnp.where(gz == 0, nz - 3 * a, 3 * a), 1)
+        packed = jnp.where((lane >= first) & (lane < first + 3), moved, packed)
+    return packed
+
+
+def edge_x_kernel(own, s0, s1, out, before, behind):
+    nx, ny, nz = own.shape[1:]
+    sides_x((s0, s1), before, behind)
     for p in range(nx + 4):
-        packed = ext[0, 1 + p]
-        for a in range(1, 4):
-            first = jnp.where(gz == 0, nz - 3 - 3 * a, 3 * a)
-            moved = pltpu.roll(ext[a, 1 + p], jnp.where(gz == 0, nz - 3 * a, 3 * a), 1)
-            packed = jnp.where((lane >= first) & (lane < first + 3), moved, packed)
-        edge[p] = packed
-
-
-def fine_kernel(local, edges, faces, e_out, q_out, r_out, m_out, ext, e1, rd, dg, e2, rows):
+        if p < 2:
+            values = [before[2 * a + p] for a in range(4)]
+        elif p < nx + 2:
+            values = [own[a, p - 2] for a in range(4)]
+        else:
+            values = [behind[2 * a + p - nx - 2] for a in range(4)]
+        out[p, :PAD] = jnp.zeros((PAD, nz), jnp.float32)
+        out[p, PAD + ny :] = jnp.zeros((PAD, nz), jnp.float32)
+        out[p, PAD : PAD + ny] = side_by_side(values)
+
+
+def edge_y_kernel(o0, o1, out):
+    planes, nz = out.shape[0], o0.shape[1]
+    out[...] = jnp.zeros_like(out)
+    for (even, keep), r in zip(side("gy"), (PAD - 2, 2 * TILE - PAD)):
+        each = 2 * planes
+        lines = [
+            keep * jnp.where(even, o0[a * each : (a + 1) * each], o1[a * each : (a + 1) * each]) for a in range(4)
+        ]
+        packed = side_by_side(lines)
+        for p in range(planes):
+            out[p, r : r + 2] = packed[2 * p : 2 * p + 2]
+
+
+def fine_kernel(local, edges_x, edges_y, faces, e_out, q_out, r_out, m_out, halo, e1, rd, dg, e2, rows):
     nx, ny, half = e_out.shape
     nz = 2 * half
     gx, gy, gz = lax.axis_index("gx"), lax.axis_index("gy"), lax.axis_index("gz")
     spot = iota((ny + 2 * PAD, half), 1)
     given = jnp.logical_or((gz == 0) & (spot < 3), (gz == 1) & (spot >= half - 3))
+    gap = jnp.zeros((ny + 2 * PAD - 2 * TILE, half), jnp.float32)
+    edge = {
+        1 + p: edges_x[p] + jnp.concatenate([edges_y[p, :TILE], gap, edges_y[p, TILE:]], 0) for p in range(nx + 4)
+    }
     for p in range(nx + 2 * REACH):
         for a in range(4):
-            ext[a, p, :, :half] = local[a, p]
             if 1 <= p < nx + 5:
-                v = edges[p - 1]
+                v = edge[p]
                 if a > 0:
                     v = pltpu.roll(v, jnp.where(gz == 0, half - 3 * a, 3 * a), 1)
-                ext[a, p, :, half:] = jnp.where(given, v, 0.0)
+                halo[a, p] = jnp.where(given, v, 0.0)
             else:
-                ext[a, p, :, half:] = jnp.zeros((ny + 2 * PAD, half), jnp.float32)
+                halo[a, p] = jnp.zeros((ny + 2 * PAD, half), jnp.float32)
+
+    def ext(a, p):
+        return jnp.concatenate([local[a, p], halo[a, p]], 1)
+
     shape = (ny + 2 * PAD, nz)
     row, lane = iota(shape, 0), iota(shape, 1)
     inner_z = jnp.logical_or(lane > 0, gz > 0)
@@ -162,18 +199,18 @@
     )
 
     def off(e, p):
-        fy, fz = ext[2, p], jnp.where(inner_z, ext[3, p], 0.0)
+        fy, fz = ext(2, p), jnp.where(inner_z, ext(3, p), 0.0)
         here = e[p]
-        total = ext[1, p] * e[p - 1] + ext[1, p + 1] * e[p + 1]
+        total = ext(1, p) * e[p - 1] + ext(1, p + 1) * e[p + 1]
         total = total + fy * down(here, 0) + up(fy * here, 0)
         return total + fz * down(here, 1) + up(fz * here, 1)
 
     for p in range(1, nx + 2 * REACH - 1):
-        fy, fz = ext[2, p], ext[3, p]
-        diagonal = ext[1, p] + ext[1, p + 1] + fy + up(fy, 0) + fz + up(jnp.where(inner_z, fz, 0.0), 1)
+        fy, fz = ext(2, p), ext(3, p)
+        diagonal = ext(1, p) + ext(1, p + 1) + fy + up(fy, 0) + fz + up(jnp.where(inner_z, fz, 0.0), 1)
         inv = inverse(diagonal)
         dg[p], rd[p] = diagonal, inv
-        e1[p] = ext[0, p] * inv
+        e1[p] = ext(0, p) * inv
     for p in range(2, nx + 2 * REACH - 2):
         value = (2.0 - damping) * e1[p] + rd[p] * off(e1, p)
         inside = in_y
@@ -189,7 +226,7 @@
     sums = []
     for i in range(nx):
         p = REACH + i
-        q = mine(ext[0, p] - dg[p] * e2[p] + off(e2, p))
+        q = mine(ext(0, p) - dg[p] * e2[p] + off(e2, p))
         e_out[i], q_out[i], r_out[i] = mine(e2[p]), q, mine(rd[p])
         sums.append(q)
     pairs = range(0, nx, 2)
@@ -224,7 +261,7 @@
     out[1] = (even[part:] + jnp.where(spot < half // 2, 0.0, odd[part:])).reshape(out.shape[1:])
 
 
-def sweep_kernel(local, edges, e_in, q_in, r_in, t_out, k_out, *matrices):
+def sweep_kernel(local, edges_x, e_in, q_in, r_in, t_out, k_out, *matrices):
     nx, ny, half = t_out.shape
     gz = lax.axis_index("gz")
     lane = iota((ny, half), 1)
@@ -234,7 +271,7 @@
     for i in range(nx):
         p, inv = REACH + i, r_in[i]
         fz = local[3, p, inner]
-        far = keep * pltpu.roll(edges[p - 1, inner], half - 1 - 9, 1)
+        far = keep * pltpu.roll(edges_x[p - 1, inner], half - 1 - 9, 1)
         high_z = jnp.where(top_z, up(fz, 1), far)
         faces = (local[1, p, inner], local[1, p + 1, inner], local[2, p, inner], local[2, p, PAD + 1 : PAD + 1 + ny])
         t_out[i] = e_in[i] + inv * q_in[i]
@@ -533,22 +570,39 @@
         compiler_params=PARAMS,
         name="slabs_y",
     )(own, *slabs)
+    edge = pl.pallas_call(
+        edge_x_kernel,
+        out_shape=f32(nx + 4, ny + 2 * PAD, nz),
+        scratch_shapes=near,
+        compiler_params=PARAMS,
+        cost_estimate=SMALL,
+        name="edges_x",
+    )(own, *slabs)
+    swap = [(0, 1), (1, 0)]
     lines = traded(lines, "gy")
-    local, edge = pl.pallas_call(
+    edges_x = lax.ppermute(edge, "gz", swap)
+    edge = pl.pallas_call(
+        edge_y_kernel,
+        out_shape=f32(nx + 4, 2 * TILE, nz),
+        compiler_params=PARAMS,
+        name="edges_y",
+    )(*lines)
+    edges_y = lax.ppermute(edge, "gz", swap)
+    local = pl.pallas_call(
         z_kernel,
-        out_shape=(f32(4, nx + 2 * REACH, ny + 2 * PAD, nz), f32(nx + 4, ny + 2 * PAD, nz)),
+        out_shape=f32(4, nx + 2 * REACH, ny + 2 * PAD, nz),
         scratch_shapes=near + [pltpu.VMEM((count, nz), jnp.float32)],
         compiler_params=PARAMS,
-        name="edges_z",
+        cost_estimate=SMALL,
+        name="extend",
     )(own, *slabs, *lines)
-    edges = lax.ppermute(edge, "gz", [(0, 1), (1, 0)])
     ext_x, ext_y, wide = nx + 2 * REACH, ny + 2 * PAD, 2 * nz
     field = pltpu.VMEM((ext_x, ext_y, wide), jnp.float32)
     e, q, r, m = pl.pallas_call(
         fine_kernel,
         out_shape=(f32(nx, ny, nz),) * 3 + (f32(2, nx // 2, ny // 2, nz),),
         scratch_shapes=[
-            pltpu.VMEM((4, ext_x, ext_y, wide), jnp.float32),
+            pltpu.VMEM((4, ext_x, ext_y, nz), jnp.float32),
             field,
             field,
             field,
@@ -557,7 +611,7 @@
         ],
         compiler_params=PARAMS,
         name="fine",
-    )(local, edges, faces)
+    )(local, edges_x, edges_y, faces)
     blocks = nx * lax.axis_size("gx") // 8
     shapes = ((nz, nz), (nz, nz), (blocks * nz, nz), (blocks * nz, nz), (nz, blocks * nz), (nz, nz), (nz, 3 * nz))
     t, k, *matrices = pl.pallas_call(
@@ -567,7 +621,7 @@
         compiler_params=PARAMS,
         cost_estimate=SMALL,
         name="sweep",
-    )(local, edges, e, q, r)
+    )(local, edges_x, e, q, r)
     near = doubled_over(m[None], "gx")
     here = [near] + [
         lax.ppermute(near, "gy", [(i, i ^ n) for i in range(cy)]) for n in range(1, cy)

time: 39.2 us -> 39 us (level)
  waiting for transfers between devices: 15.7 us -> 14.8 us
  starting transfers between devices: 17 us -> 17.6 us
    ppermute x4, waiting for transfers between devices: 4.86 us -> 4.13 us  [traded(): taken.append(lax.ppermute(block, (axis, 'gz'), route))]
    ppermute x1 -> x2, starting transfers between devices: 0.07 us -> 0.64 us  [the longest x1 0.57 us: per_device_small(): edges_x = lax.ppermute(edge, 'gz', swap)]
    ppermute x1 -> x2, waiting for transfers between devices: 1.16 us -> 0.96 us  [the longest x1 0.96 us: per_device_small(): edges_y = lax.ppermute(edge, 'gz', swap)]
  transfers between devices with their start and end apart: 14 -> 15, of which waited for: 9 -> 9; matrix products, arithmetic and copies ran while one was open for 0% -> 0% of each run, Pallas kernels for 1% -> 2%
where the time goes in v8:
time: 39 us; the launch traced here: 38.8 us
  starting transfers between devices  17.6 us (45%)
  waiting for transfers between devices  14.8 us (38%)
  Pallas kernels  5.4 us (14%)
  other arithmetic  0.97 us (2%)
    ppermute x2, starting transfers between devices, doubled_over(): lax.ppermute(block, (axis, 'gz'), route)  6.76 us
    ppermute x4, starting transfers between devices, traded(): taken.append(lax.ppermute(block, (axis, 'gz'), route))  5.12 us
    ppermute x3, starting transfers between devices, per_device_small(): lax.ppermute(near, 'gy', [(i, i ^ n) for i in range(cy)])  5.08 us
    ppermute x3, waiting for transfers between devices, per_device_small(): lax.ppermute(near, 'gy', [(i, i ^ n) for i in range(cy)])  4.47 us
    ppermute x2, waiting for transfers between devices, doubled_over(): lax.ppermute(block, (axis, 'gz'), route)  4.14 us
    ppermute x4, waiting for transfers between devices, traded(): taken.append(lax.ppermute(block, (axis, 'gz'), route))  4.13 us
    pallas_call x1, Pallas kernels, per_device_small(): pl.pallas_call(whole_kernel, out_shape=f32(nx, ny, nz), scratch_shapes=[p...  3.79 us
    ppermute x4, waiting for transfers between devices, per_device_small(): there = [lax.ppermute(block, 'gz', [(0, 1), (1, 0)]) for block in here]  1.05 us
  transfers between devices with their start and end apart: 15, of which 9 were waited for; matrix products, arithmetic and copies ran while one was open for 0% of the time, Pallas kernels for 2%

profile of v8, /device:TPU:0, one launch (start us, length us, event | category | flops | bytes accessed | tf_op | source)
XLA Modules:
  0.0 38.8 jit_solution(4969554686202581544)
XLA Ops:
  0.0 1.0 %pad_maximum_fusion.own = f32[4,8,16,128]{3,2,1,0:T(8,128)S(1)} fusion(f32[1,8,16,128]{3,2,1,0:T(8,128)} %bitcast.8, f32[1,8,16,128]{3,2,1,0:T(8,128)} %bitcast.9, f32[1,8,16,128]{3,2,1,0:T(8,128)} %bitcast.10, f32[1,8,16,128]{3,2,1,0:T(8,128)} %bitcast.11), kind=kLoop, calls=%fused_computation | loop fusion | flops 196608 | bytes 524288 | tf_op jit(solution)/shard_map/stack | solution.py:549
  1.0 3.1 %collective-permute-start = (f32[9,16,128]{2,1,0:T(8,128)S(1)}, f32[9,16,128]{2,1,0:T(8,128)S(1)}, u32[]{:S(2)}, u32[]{:S(2)}) collective-permute-start(f32[9,16,128]{2,1,0:T(8,128)S(1)} %get-tuple-element.22), channel_id=1, source_target_pairs={{0,8},{1,9},{8,0},{9,1},{16,24},{17,25},{24,16},{25,17},{2,10},{3,... | collective-permute-start | bytes 221192 | tf_op jit(solution)/shard_map/ppermute | solution.py:528
  4.1 0.0 collective-permute-start.1
  4.1 2.3 %collective-permute-done.s0 = f32[9,16,128]{2,1,0:T(8,128)S(1)} collective-permute-done((f32[9,16,128]{2,1,0:T(8,128)S(1)}, f32[9,16,128]{2,1,0:T(8,128)S(1)}, u32[]{:S(2)}, u32[]{:S(2)}) %collective-permute-start) | collective-permute-done | bytes 73760 | tf_op jit(solution)/shard_map/ppermute | solution.py:528
  6.4 0.0 collective-permute-done.1.s1
  6.4 0.1 slabs_y.1
  6.5 2.0 %collective-permute-start.2 = (f32[112,128]{1,0:T(8,128)S(1)}, f32[112,128]{1,0:T(8,128)S(1)}, u32[]{:S(2)}, u32[]{:S(2)}) collective-permute-start(f32[112,128]{1,0:T(8,128)S(1)} %get-tuple-element.24), channel_id=1, source_target_pairs={{0,2},{1,3},{2,0},{3,1},{4,6},{5,7},{6,4},{7,5},{8,10},{9,11},{10,... | collective-permute-start | bytes 172040 | tf_op jit(solution)/shard_map/ppermute | solution.py:528
  8.5 0.1 edges_x.1
  8.7 0.6 %collective-permute-start.4 = (f32[12,24,128]{2,1,0:T(8,128)S(1)}, f32[12,24,128]{2,1,0:T(8,128)S(1)}, u32[]{:S(2)}, u32[]{:S(2)}) collective-permute-start(f32[12,24,128]{2,1,0:T(8,128)S(1)} %edges_x.1), channel_id=1, source_target_pairs={{0,1},{1,0},{2,3},{3,2},{4,5},{5,4},{6,7},{7,6},{8,9},{9,8},{10,11... | collective-permute-start | bytes 442376 | tf_op jit(solution)/shard_map/ppermute | solution.py:583
  9.3 1.8 %collective-permute-done.2.o0 = f32[112,128]{1,0:T(8,128)S(1)} collective-permute-done((f32[112,128]{1,0:T(8,128)S(1)}, f32[112,128]{1,0:T(8,128)S(1)}, u32[]{:S(2)}, u32[]{:S(2)}) %collective-permute-start.2) | collective-permute-done | bytes 57376 | tf_op jit(solution)/shard_map/ppermute | solution.py:528
  11.1 0.1 edges_y.1
  11.2 0.1 collective-permute-start.5
  11.2 0.2 faces.1
  11.4 0.1 extend.1.local
  11.6 1.0 %collective-permute-done.5.edges_y = f32[12,16,128]{2,1,0:T(8,128)S(1)} collective-permute-done((f32[12,16,128]{2,1,0:T(8,128)S(1)}, f32[12,16,128]{2,1,0:T(8,128)S(1)}, u32[]{:S(2)}, u32[]{:S(2)}) %collective-permute-start.5) | collective-permute-done | bytes 98336 | tf_op jit(solution)/shard_map/ppermute | solution.py:590
  12.5 0.7 %fine.1 = (f32[8,16,128]{2,1,0:T(8,128)S(1)}, f32[8,16,128]{2,1,0:T(8,128)S(1)}, f32[8,16,128]{2,1,0:T(8,128)S(1)}, f32[2,4,8,128]{3,2,1,0:T(8,128)S(1)}) custom-call(f32[4,14,24,128]{3,2,1,0:T(8,128)S(1)} %extend.1.local, f32[12,24,128]{2,1,0:T(8,128)S(1)} %collective-permute-done.4.edges_x, f32[12,16,128]{2,1,0:T(8,128)S(1)} %collective-permute-done.5.edges_y, ...), custom_call_target="tpu_custom_call" | custom-call | tf_op jit(solution)/shard_map/fine/pallas_call | solution.py:601
  13.2 3.4 %collective-permute-start.6 = (f32[1,2,4,8,128]{4,3,2,1,0:T(8,128)S(1)}, f32[1,2,4,8,128]{4,3,2,1,0:T(8,128)S(1)}, u32[]{:S(2)}, u32[]{:S(2)}) collective-permute-start(f32[1,2,4,8,128]{4,3,2,1,0:T(8,128)S(1)} %bitcast.5), channel_id=1, source_target_pairs={{0,8},{1,17},{8,0},{9,25},{16,24},{17,1},{24,16},{25,9},{2,10},{3,... | collective-permute-start | bytes 98312 | tf_op jit(solution)/shard_map/ppermute | solution.py:537
  16.6 1.9 %collective-permute-done.6 = f32[1,2,4,8,128]{4,3,2,1,0:T(8,128)S(1)} collective-permute-done((f32[1,2,4,8,128]{4,3,2,1,0:T(8,128)S(1)}, f32[1,2,4,8,128]{4,3,2,1,0:T(8,128)S(1)}, u32[]{:S(2)}, u32[]{:S(2)}) %collective-permute-start.6) | collective-permute-done | bytes 32800 | tf_op jit(solution)/shard_map/ppermute | solution.py:537
  18.5 3.4 %collective-permute-start.7 = (f32[2,2,4,8,128]{4,3,2,1,0:T(8,128)S(1)}, f32[2,2,4,8,128]{4,3,2,1,0:T(8,128)S(1)}, u32[]{:S(2)}, u32[]{:S(2)}) collective-permute-start(f32[2,2,4,8,128]{4,3,2,1,0:T(8,128)S(1)} %pad_maximum_fusion.2), channel_id=1, source_target_pairs={{0,16},{1,9},{8,24},{9,1},{16,0},{17,25},{24,8},{25,17},{2,18},{3,... | collective-permute-start | bytes 196616 | tf_op jit(solution)/shard_map/ppermute | solution.py:537
  21.9 2.2 %collective-permute-done.7 = f32[2,2,4,8,128]{4,3,2,1,0:T(8,128)S(1)} collective-permute-done((f32[2,2,4,8,128]{4,3,2,1,0:T(8,128)S(1)}, f32[2,2,4,8,128]{4,3,2,1,0:T(8,128)S(1)}, u32[]{:S(2)}, u32[]{:S(2)}) %collective-permute-start.7) | collective-permute-done | bytes 65568 | tf_op jit(solution)/shard_map/ppermute | solution.py:537
  24.1 2.8 %collective-permute-start.8 = (f32[4,2,4,8,128]{4,3,2,1,0:T(8,128)S(1)}, f32[4,2,4,8,128]{4,3,2,1,0:T(8,128)S(1)}, u32[]{:S(2)}, u32[]{:S(2)}) collective-permute-start(f32[4,2,4,8,128]{4,3,2,1,0:T(8,128)S(1)} %pad_maximum_fusion.1.refs_0_), channel_id=1, source_target_pairs={{0,2},{2,0},{4,6},{6,4},{1,3},{3,1},{5,7},{7,5},{8,10},{10,8},{12,... | collective-permute-start | bytes 393224 | tf_op jit(solution)/shard_map/ppermute | solution.py:627
  26.9 0.9 %collective-permute-start.9 = (f32[4,2,4,8,128]{4,3,2,1,0:T(8,128)S(1)}, f32[4,2,4,8,128]{4,3,2,1,0:T(8,128)S(1)}, u32[]{:S(2)}, u32[]{:S(2)}) collective-permute-start(f32[4,2,4,8,128]{4,3,2,1,0:T(8,128)S(1)} %pad_maximum_fusion.1.refs_0_), channel_id=1, source_target_pairs={{0,4},{2,6},{4,0},{6,2},{1,5},{3,7},{5,1},{7,3},{8,12},{10,14},{12... | collective-permute-start | bytes 393224 | tf_op jit(solution)/shard_map/ppermute | solution.py:627
  27.8 1.4 %collective-permute-start.10 = (f32[4,2,4,8,128]{4,3,2,1,0:T(8,128)S(1)}, f32[4,2,4,8,128]{4,3,2,1,0:T(8,128)S(1)}, u32[]{:S(2)}, u32[]{:S(2)}) collective-permute-start(f32[4,2,4,8,128]{4,3,2,1,0:T(8,128)S(1)} %pad_maximum_fusion.1.refs_0_), channel_id=1, source_target_pairs={{0,6},{2,4},{4,2},{6,0},{1,7},{3,5},{5,3},{7,1},{8,14},{10,12},{12... | collective-permute-start | bytes 393224 | tf_op jit(solution)/shard_map/ppermute | solution.py:627
  29.2 1.9 %collective-permute-done.8.refs_1_ = f32[4,2,4,8,128]{4,3,2,1,0:T(8,128)S(1)} collective-permute-done((f32[4,2,4,8,128]{4,3,2,1,0:T(8,128)S(1)}, f32[4,2,4,8,128]{4,3,2,1,0:T(8,128)S(1)}, u32[]{:S(2)}, u32[]{:S(2)}) %collective-permute-start.8) | collective-permute-done | bytes 131104 | tf_op jit(solution)/shard_map/ppermute | solution.py:627
  31.2 0.0 collective-permute-start.12
  31.2 1.0 %collective-permute-done.9.refs_2_ = f32[4,2,4,8,128]{4,3,2,1,0:T(8,128)S(1)} collective-permute-done((f32[4,2,4,8,128]{4,3,2,1,0:T(8,128)S(1)}, f32[4,2,4,8,128]{4,3,2,1,0:T(8,128)S(1)}, u32[]{:S(2)}, u32[]{:S(2)}) %collective-permute-start.9) | collective-permute-done | bytes 131104 | tf_op jit(solution)/shard_map/ppermute | solution.py:627
  32.1 1.6 %collective-permute-done.10.refs_3_ = f32[4,2,4,8,128]{4,3,2,1,0:T(8,128)S(1)} collective-permute-done((f32[4,2,4,8,128]{4,3,2,1,0:T(8,128)S(1)}, f32[4,2,4,8,128]{4,3,2,1,0:T(8,128)S(1)}, u32[]{:S(2)}, u32[]{:S(2)}) %collective-permute-start.10) | collective-permute-done | bytes 131104 | tf_op jit(solution)/shard_map/ppermute | solution.py:627
  33.7 0.3 sweep.1
  34.0 0.0 collective-permute-done.12.refs_5_
  34.0 0.0 collective-permute-done.13.refs_6_
  34.0 1.0 %collective-permute-done.14.refs_7_ = f32[4,2,4,8,128]{4,3,2,1,0:T(8,128)S(1)} collective-permute-done((f32[4,2,4,8,128]{4,3,2,1,0:T(8,128)S(1)}, f32[4,2,4,8,128]{4,3,2,1,0:T(8,128)S(1)}, u32[]{:S(2)}, u32[]{:S(2)}) %collective-permute-start.14) | collective-permute-done | bytes 131104 | tf_op jit(solution)/shard_map/ppermute | solution.py:629
  35.1 3.8 %whole.1 = f32[8,16,128]{2,1,0:T(8,128)} custom-call(f32[4,2,4,8,128]{4,3,2,1,0:T(8,128)S(1)} %pad_maximum_fusion.1.refs_0_, f32[4,2,4,8,128]{4,3,2,1,0:T(8,128)S(1)} %collective-permute-done.8.refs_1_, f32[4,2,4,8,128]{4,3,2,1,0:T(8,128)S(1)} %collective-permute-done.9.refs_2_, f32[4,2,4,8,128]{4,3,2,1,0:T(8,128)S(1)} %collective-permute-done.10.refs_3_, ...), custom_call_target="tpu_custom_call" | custom-call | tf_op jit(solution)/shard_map/whole/pallas_call | solution.py:633
  (10 shorter events, 0.1 us)
Async XLA Ops:
  1.0 5.5 %collective-permute-start = (f32[9,16,128]{2,1,0:T(8,128)S(1)}, f32[9,16,128]{2,1,0:T(8,128)S(1)}, u32[]{:S(2)}, u32[]{:S(2)}) collective-permute-start(f32[9,16,128]{2,1,0:T(8,128)S(1)} %get-tuple-element.22), channel_id=1, source_target_pairs={{0,8},{1,9},{8,0},{9,1},{16,24},{17,25},{24,16},{25,17},{2,10},{3,... | collective-permute-start | bytes 221192 | tf_op jit(solution)/shard_map/ppermute | solution.py:528
  4.1 2.3 %collective-permute-start.1 = (f32[9,16,128]{2,1,0:T(8,128)S(1)}, f32[9,16,128]{2,1,0:T(8,128)S(1)}, u32[]{:S(2)}, u32[]{:S(2)}) collective-permute-start(f32[9,16,128]{2,1,0:T(8,128)S(1)} %get-tuple-element.23), channel_id=1, source_target_pairs={{0,1},{1,0},{8,16},{9,17},{16,8},{17,9},{24,25},{25,24},{2,3},{3,2... | collective-permute-start | bytes 221192 | tf_op jit(solution)/shard_map/ppermute | solution.py:528
  6.5 4.5 %collective-permute-start.2 = (f32[112,128]{1,0:T(8,128)S(1)}, f32[112,128]{1,0:T(8,128)S(1)}, u32[]{:S(2)}, u32[]{:S(2)}) collective-permute-start(f32[112,128]{1,0:T(8,128)S(1)} %get-tuple-element.24), channel_id=1, source_target_pairs={{0,2},{1,3},{2,0},{3,1},{4,6},{5,7},{6,4},{7,5},{8,10},{9,11},{10,... | collective-permute-start | bytes 172040 | tf_op jit(solution)/shard_map/ppermute | solution.py:528
  8.5 2.5 %collective-permute-start.3 = (f32[112,128]{1,0:T(8,128)S(1)}, f32[112,128]{1,0:T(8,128)S(1)}, u32[]{:S(2)}, u32[]{:S(2)}) collective-permute-start(f32[112,128]{1,0:T(8,128)S(1)} %get-tuple-element.25), channel_id=1, source_target_pairs={{0,1},{1,0},{2,4},{3,5},{4,2},{5,3},{6,7},{7,6},{8,9},{9,8},{10,12... | collective-permute-start | bytes 172040 | tf_op jit(solution)/shard_map/ppermute | solution.py:528
  8.7 2.9 %collective-permute-start.4 = (f32[12,24,128]{2,1,0:T(8,128)S(1)}, f32[12,24,128]{2,1,0:T(8,128)S(1)}, u32[]{:S(2)}, u32[]{:S(2)}) collective-permute-start(f32[12,24,128]{2,1,0:T(8,128)S(1)} %edges_x.1), channel_id=1, source_target_pairs={{0,1},{1,0},{2,3},{3,2},{4,5},{5,4},{6,7},{7,6},{8,9},{9,8},{10,11... | collective-permute-start | bytes 442376 | tf_op jit(solution)/shard_map/ppermute | solution.py:583
  11.2 1.4 %collective-permute-start.5 = (f32[12,16,128]{2,1,0:T(8,128)S(1)}, f32[12,16,128]{2,1,0:T(8,128)S(1)}, u32[]{:S(2)}, u32[]{:S(2)}) collective-permute-start(f32[12,16,128]{2,1,0:T(8,128)S(1)} %edges_y.1), channel_id=1, source_target_pairs={{0,1},{1,0},{2,3},{3,2},{4,5},{5,4},{6,7},{7,6},{8,9},{9,8},{10,11... | collective-permute-start | bytes 294920 | tf_op jit(solution)/shard_map/ppermute | solution.py:590
  13.2 5.3 %collective-permute-start.6 = (f32[1,2,4,8,128]{4,3,2,1,0:T(8,128)S(1)}, f32[1,2,4,8,128]{4,3,2,1,0:T(8,128)S(1)}, u32[]{:S(2)}, u32[]{:S(2)}) collective-permute-start(f32[1,2,4,8,128]{4,3,2,1,0:T(8,128)S(1)} %bitcast.5), channel_id=1, source_target_pairs={{0,8},{1,17},{8,0},{9,25},{16,24},{17,1},{24,16},{25,9},{2,10},{3,... | collective-permute-start | bytes 98312 | tf_op jit(solution)/shard_map/ppermute | solution.py:537
  18.5 5.6 %collective-permute-start.7 = (f32[2,2,4,8,128]{4,3,2,1,0:T(8,128)S(1)}, f32[2,2,4,8,128]{4,3,2,1,0:T(8,128)S(1)}, u32[]{:S(2)}, u32[]{:S(2)}) collective-permute-start(f32[2,2,4,8,128]{4,3,2,1,0:T(8,128)S(1)} %pad_maximum_fusion.2), channel_id=1, source_target_pairs={{0,16},{1,9},{8,24},{9,1},{16,0},{17,25},{24,8},{25,17},{2,18},{3,... | collective-permute-start | bytes 196616 | tf_op jit(solution)/shard_map/ppermute | solution.py:537
  24.1 7.0 %collective-permute-start.8 = (f32[4,2,4,8,128]{4,3,2,1,0:T(8,128)S(1)}, f32[4,2,4,8,128]{4,3,2,1,0:T(8,128)S(1)}, u32[]{:S(2)}, u32[]{:S(2)}) collective-permute-start(f32[4,2,4,8,128]{4,3,2,1,0:T(8,128)S(1)} %pad_maximum_fusion.1.refs_0_), channel_id=1, source_target_pairs={{0,2},{2,0},{4,6},{6,4},{1,3},{3,1},{5,7},{7,5},{8,10},{10,8},{12,... | collective-permute-start | bytes 393224 | tf_op jit(solution)/shard_map/ppermute | solution.py:627
  26.9 5.2 %collective-permute-start.9 = (f32[4,2,4,8,128]{4,3,2,1,0:T(8,128)S(1)}, f32[4,2,4,8,128]{4,3,2,1,0:T(8,128)S(1)}, u32[]{:S(2)}, u32[]{:S(2)}) collective-permute-start(f32[4,2,4,8,128]{4,3,2,1,0:T(8,128)S(1)} %pad_maximum_fusion.1.refs_0_), channel_id=1, source_target_pairs={{0,4},{2,6},{4,0},{6,2},{1,5},{3,7},{5,1},{7,3},{8,12},{10,14},{12... | collective-permute-start | bytes 393224 | tf_op jit(solution)/shard_map/ppermute | solution.py:627
  27.8 5.9 %collective-permute-start.10 = (f32[4,2,4,8,128]{4,3,2,1,0:T(8,128)S(1)}, f32[4,2,4,8,128]{4,3,2,1,0:T(8,128)S(1)}, u32[]{:S(2)}, u32[]{:S(2)}) collective-permute-start(f32[4,2,4,8,128]{4,3,2,1,0:T(8,128)S(1)} %pad_maximum_fusion.1.refs_0_), channel_id=1, source_target_pairs={{0,6},{2,4},{4,2},{6,0},{1,7},{3,5},{5,3},{7,1},{8,14},{10,12},{12... | collective-permute-start | bytes 393224 | tf_op jit(solution)/shard_map/ppermute | solution.py:627
  29.2 4.8 %collective-permute-start.11 = (f32[4,2,4,8,128]{4,3,2,1,0:T(8,128)S(1)}, f32[4,2,4,8,128]{4,3,2,1,0:T(8,128)S(1)}, u32[]{:S(2)}, u32[]{:S(2)}) collective-permute-start(f32[4,2,4,8,128]{4,3,2,1,0:T(8,128)S(1)} %pad_maximum_fusion.1.refs_0_), channel_id=1, source_target_pairs={{0,1},{1,0},{2,3},{3,2},{4,5},{5,4},{6,7},{7,6},{8,9},{9,8},{10,11... | collective-permute-start | bytes 393224 | tf_op jit(solution)/shard_map/ppermute | solution.py:629
  31.2 2.8 %collective-permute-start.12 = (f32[4,2,4,8,128]{4,3,2,1,0:T(8,128)S(1)}, f32[4,2,4,8,128]{4,3,2,1,0:T(8,128)S(1)}, u32[]{:S(2)}, u32[]{:S(2)}) collective-permute-start(f32[4,2,4,8,128]{4,3,2,1,0:T(8,128)S(1)} %collective-permute-done.8.refs_1_), channel_id=1, source_target_pairs={{0,1},{1,0},{2,3},{3,2},{4,5},{5,4},{6,7},{7,6},{8,9},{9,8},{10,11... | collective-permute-start | bytes 393224 | tf_op jit(solution)/shard_map/ppermute | solution.py:629
  32.1 1.9 %collective-permute-start.13 = (f32[4,2,4,8,128]{4,3,2,1,0:T(8,128)S(1)}, f32[4,2,4,8,128]{4,3,2,1,0:T(8,128)S(1)}, u32[]{:S(2)}, u32[]{:S(2)}) collective-permute-start(f32[4,2,4,8,128]{4,3,2,1,0:T(8,128)S(1)} %collective-permute-done.9.refs_2_), channel_id=1, source_target_pairs={{0,1},{1,0},{2,3},{3,2},{4,5},{5,4},{6,7},{7,6},{8,9},{9,8},{10,11... | collective-permute-start | bytes 393224 | tf_op jit(solution)/shard_map/ppermute | solution.py:629
  33.7 1.3 %collective-permute-start.14 = (f32[4,2,4,8,128]{4,3,2,1,0:T(8,128)S(1)}, f32[4,2,4,8,128]{4,3,2,1,0:T(8,128)S(1)}, u32[]{:S(2)}, u32[]{:S(2)}) collective-permute-start(f32[4,2,4,8,128]{4,3,2,1,0:T(8,128)S(1)} %collective-permute-done.10.refs_3_), channel_id=1, source_target_pairs={{0,1},{1,0},{2,3},{3,2},{4,5},{5,4},{6,7},{7,6},{8,9},{9,8},{10,11... | collective-permute-start | bytes 393224 | tf_op jit(solution)/shard_map/ppermute | solution.py:629
